TPU v7x, 768 devices: a whole 4x8x12 slice. The times are simulated.
768 devices in a mesh: lat: 16 (over z_lo, x), lon: 6 (over z_hi, core), opt: 8 (over y).
Axes of the slice: x: 4, y: 8, z: 12 (z_hi: 3, z_lo: 4; z = z_hi * 4 + z_lo), core: 2. Of those that a mesh axis runs over, the one named last changes fastest.
Arguments:
- queries: bfloat16 [8, 16, 6, 128, 512], P('opt', 'lat', 'lon'), may hold values from -8 to 8
- keys: bfloat16 [8, 16, 6, 128, 512], P('opt', 'lat', 'lon'), may hold values from -8 to 8
- values: bfloat16 [8, 16, 6, 128, 512], P('opt', 'lat', 'lon'), may hold values from -6 to 6
- grad_out: bfloat16 [8, 16, 6, 128, 1024], P('opt', 'lat', 'lon'), may hold values from -6 to 6
- w_out: bfloat16 [512, 1024], replicated, may hold values from -0.25 to 0.25
- pattern: int32 [16, 6, 9], replicated, may hold values from 0 to 1, as said below
Outputs:
- grad_queries: bfloat16 [8, 16, 6, 128, 512], P('opt', 'lat', 'lon')
- grad_keys: bfloat16 [8, 16, 6, 128, 512], P('opt', 'lat', 'lon')
- grad_values: bfloat16 [8, 16, 6, 128, 512], P('opt', 'lat', 'lon')
- grad_w_out: float32 [512, 1024], P('opt')
Inputs may be any that keep to these rules, and one draw needn't show every extreme that they name: `pattern`: entry 4 of each block's nine (the block itself) is 1.
All inputs are finite; a program needn't handle non-finite values.
Results may differ from a plain program's by a relative error of at most 0.034.
Values may be sent and summed in bfloat16 or wider, within the bound.
No kernel may reach another device: no remote copies, remote signals or barrier semaphores. Data moves between devices by JAX's collectives and lax.ppermute only.
A program may use at most 32 MiB of HBM per device.

v0:
```python
from functools import partial

import jax
import jax.numpy as jnp
from jax import lax
from jax.sharding import PartitionSpec as P

HDIM = 64


def passed_along(block, axis, distance):
    devices = range(lax.axis_size(axis))
    route = [(i - distance, i) for i in devices if i - distance in devices]
    return lax.ppermute(block, axis, route)


def shifted(array, axis, by):
    length = lax.axis_size(axis)
    return lax.ppermute(array, axis, [(i, (i + by) % length) for i in range(length)])


def with_halo(cells, sides, width):
    for axis, dim in sides:
        count = lax.axis_size(axis)
        head = lax.slice_in_dim(cells, 0, width, axis=dim)
        tail = lax.slice_in_dim(cells, cells.shape[dim] - width, cells.shape[dim], axis=dim)
        cells = jnp.concatenate(
            [
                lax.ppermute(tail, axis, [(i, (i + 1) % count) for i in range(count)]),
                cells,
                lax.ppermute(head, axis, [((i + 1) % count, i) for i in range(count)]),
            ],
            axis=dim,
        )
    return cells


def head_view(block_array):
    return block_array.reshape(block_array.shape[:-1] + (block_array.shape[-1] // HDIM, HDIM))


def query_scan(keys_ext, pattern_near, key_valid, lon_blocks, keep, carried, inputs):
    query_blk, dout_blk, position = inputs
    row_pos = position // lon_blocks
    col_pos = position % lon_blocks
    block_len, att_width = query_blk.shape
    score_scale = HDIM ** (-0.5)
    nearby = keys_ext
    nearby = head_view(nearby.reshape(2, 9, block_len, att_width))
    pattern_flags = lax.dynamic_slice(
        pattern_near, (row_pos + 1, col_pos + 1, 0), (1, 1, 9)
    ).reshape(9)
    lat_flags = key_valid.reshape(9)
    live = ((pattern_flags > 0) & lat_flags)[None, None, :, None]
    query_heads = head_view(query_blk)
    dout_heads = head_view(dout_blk)
    scores = (
        jnp.einsum("qhe,dkhe->hqdk", query_heads, nearby[0], preferred_element_type=jnp.float32)
        * score_scale
    )
    row_max = jnp.max(jnp.where(live, scores, -jnp.inf), axis=(2, 3))
    shifted_exp = jnp.where(live, jnp.exp(scores - row_max[:, :, None, None]), 0.0)
    log_norm = row_max + jnp.log(jnp.sum(shifted_exp, axis=(2, 3)))
    softmax_w = jnp.where(live, jnp.exp(scores - log_norm[:, :, None, None]), 0.0)
    softmax_low = softmax_w.astype(jnp.bfloat16)
    attended = jnp.einsum(
        "hqdk,dkhe->qhe", softmax_low, nearby[1], preferred_element_type=jnp.float32
    ).astype(jnp.bfloat16)
    row_delta = jnp.sum(dout_heads.astype(jnp.float32) * attended.astype(jnp.float32), axis=2).T
    grad_prob = jnp.einsum(
        "qhe,dkhe->hqdk", dout_heads, nearby[1], preferred_element_type=jnp.float32
    )
    grad_score = (softmax_w * (grad_prob - row_delta[:, :, None, None])).astype(jnp.bfloat16)
    grad_query = (
        jnp.einsum("hqdk,dkhe->qhe", grad_score, nearby[0], preferred_element_type=jnp.float32)
        * score_scale
    )
    key_part = (
        jnp.einsum("hqdk,qhe->dkhe", grad_score, query_heads, preferred_element_type=jnp.float32)
        * score_scale
    )
    value_part = jnp.einsum(
        "hqdk,qhe->dkhe", softmax_low, dout_heads, preferred_element_type=jnp.float32
    )
    grads_pair = jnp.stack((key_part, value_part)).reshape(2, 3, 3, block_len, att_width)
    outputs = (
        attended.reshape(block_len, att_width),
        grad_query.astype(jnp.bfloat16).reshape(block_len, att_width),
        log_norm,
        row_delta,
        grads_pair,
    )
    return (carried, outputs)


def pass_lat(rim_part, offset):
    return passed_along(rim_part.astype(jnp.bfloat16), "lat", offset).astype(rim_part.dtype)


def pass_lon(rim_part, offset):
    return shifted(rim_part.astype(jnp.bfloat16), "lon", offset).astype(rim_part.dtype)


def shards(queries, keys, values, grad_out, w_out, pattern):
    query_tile = queries[0]
    key_tile = keys[0]
    value_tile = values[0]
    grad_tile = grad_out[0]
    lat_blocks, lon_blocks, block_len, att_width = query_tile.shape
    block_count = lat_blocks * lon_blocks
    lat_total = lat_blocks * lax.axis_size("lat")
    base_lat = lax.axis_index("lat") * lat_blocks
    base_lon = lax.axis_index("lon") * lon_blocks
    grad_flat = grad_tile.reshape(block_count * block_len, grad_tile.shape[-1])
    dout_flat = lax.dot_general(
        grad_flat, w_out, (((1,), (1,)), ((), ())), preferred_element_type=jnp.float32
    ).astype(jnp.bfloat16)
    dout_tile = dout_flat.reshape(lat_blocks, lon_blocks, block_len, att_width)
    keys_ext = with_halo(jnp.stack((key_tile, value_tile)), (("lat", 1), ("lon", 2)), 1)
    wrapped = jnp.concatenate((pattern[:, -1:], pattern, pattern[:, :1]), axis=1)
    padded = jnp.pad(wrapped, ((1, 1), (0, 0), (0, 0)))
    pattern_near = lax.dynamic_slice(
        padded, (base_lat, base_lon, 0), (lat_blocks + 2, lon_blocks + 2, 9)
    )
    key_rows = (
        base_lat
        + lax.broadcasted_iota(jnp.int32, (lat_blocks, 9), 0)
        + lax.broadcasted_iota(jnp.int32, (lat_blocks, 9), 1) // 3
        - 1
    )
    key_valid = (key_rows >= 0) & (key_rows < lat_total)
    positions = jnp.arange(block_count, dtype=jnp.int32)
    inputs = (
        query_tile.reshape(block_count, block_len, att_width),
        dout_tile.reshape(block_count, block_len, att_width),
        positions,
    )
    scanner = partial(query_scan, keys_ext, pattern_near, key_valid, lon_blocks, True)
    unused, (attended, grad_query, log_norm, row_delta, block_parts) = lax.scan(
        scanner, jnp.zeros((), jnp.float32), inputs
    )
    attended_flat = attended.reshape(block_count * block_len, att_width)
    w_share = lax.psum_scatter(
        lax.dot_general(
            attended_flat, grad_flat, (((0,), (0,)), ((), ())), preferred_element_type=jnp.float32
        ).astype(jnp.bfloat16),
        "opt",
        scatter_dimension=0,
        tiled=True,
    ).astype(jnp.float32)
    grad_weight = lax.psum(w_share, ("lat", "lon"))
    tile_shape = (1, lat_blocks, lon_blocks, block_len, att_width)
    totals = jnp.zeros((2, lat_blocks + 2, lon_blocks + 2, block_len, att_width), jnp.float32)
    row_pos = 0 // lon_blocks
    col_pos = 0 % lon_blocks
    totals = totals.at[:, row_pos : row_pos + 3, col_pos : col_pos + 3].add(block_parts[0])
    from_below = pass_lat(totals[:, 0], -1)
    from_above = pass_lat(totals[:, lat_blocks + 1], 1)
    inner = totals[:, 1 : lat_blocks + 1]
    inner = inner.at[:, 0].add(from_above)
    inner = inner.at[:, lat_blocks - 1].add(from_below)
    from_right = pass_lon(inner[:, :, 0], -1)
    from_left = pass_lon(inner[:, :, lon_blocks + 1], 1)
    owned = inner[:, :, 1 : lon_blocks + 1]
    owned = owned.at[:, :, 0].add(from_left)
    owned = owned.at[:, :, lon_blocks - 1].add(from_right)
    grad_key = owned[0].astype(jnp.bfloat16)
    grad_value = owned[1].astype(jnp.bfloat16)
    return (
        grad_query.reshape(tile_shape),
        grad_key.reshape(tile_shape),
        grad_value.reshape(tile_shape),
        grad_weight,
    )


def solution(mesh):
    in_specs = (
        P("opt", "lat", "lon", None, None),
        P("opt", "lat", "lon", None, None),
        P("opt", "lat", "lon", None, None),
        P("opt", "lat", "lon", None, None),
        P(),
        P(),
    )
    out_specs = (
        P("opt", "lat", "lon", None, None),
        P("opt", "lat", "lon", None, None),
        P("opt", "lat", "lon", None, None),
        P("opt", None),
    )
    return jax.shard_map(shards, mesh=mesh, in_specs=in_specs, out_specs=out_specs, check_vma=False)
```

profile of v0, /device:TPU:64, one launch (start us, length us, event | category | flops | bytes accessed | tf_op | source)
XLA Modules:
  0.0 693.1 jit_solution(17698550311207441713)
XLA Ops:
  7.2 1.1 copy.22
  9.4 3.8 collective-permute-start.1
  13.2 2.1 collective-permute-start
  16.3 3.0 collective-permute-done.1
  19.4 5.6 collective-permute-done
  25.9 12.8 %collective-permute-start.3 = (bf16[2,3,1,128,512]{3,4,2,1,0:T(8,128)(2,1)}, bf16[2,3,1,128,512]{3,4,2,1,0:T(8,128)(2,1)S(1)}, u32[]{:S(2)}, u32[]{:S(2)}) collective-permute-start(bf16[2,3,1,128,512]{3,4,2,1,0:T(8,128)(2,1)} %pad_maximum_fusion.1), channel_id=1, source_target_pairs={{8,0},{16,8},{24,16},{32,24},{40,32},{0,40},{9,1},{17,9},{25,17},{... | collective-permute-start | bytes 2359304 | tf_op jit(solution)/shard_map/ppermute | solution.py:31
  38.7 1.9 collective-permute-start.2
  41.7 32.1 %collective-permute-done.3 = bf16[2,3,1,128,512]{3,4,2,1,0:T(8,128)(2,1)S(1)} collective-permute-done((bf16[2,3,1,128,512]{3,4,2,1,0:T(8,128)(2,1)}, bf16[2,3,1,128,512]{3,4,2,1,0:T(8,128)(2,1)S(1)}, u32[]{:S(2)}, u32[]{:S(2)}) %collective-permute-start.3) | collective-permute-done | bytes 786464 | tf_op jit(solution)/shard_map/ppermute | solution.py:31
  73.8 1.3 pad_maximum_fusion
  80.9 1.6 fusion
  85.5 1.3 slice_bitcast_fusion.2
  86.8 8.2 %collective-permute-start.4 = (bf16[2,3,128,512]{2,3,1,0:T(8,128)(2,1)}, bf16[2,3,128,512]{2,3,1,0:T(8,128)(2,1)}, u32[]{:S(2)}, u32[]{:S(2)}) collective-permute-start(bf16[2,3,128,512]{2,3,1,0:T(8,128)(2,1)} %get-tuple-element.109), channel_id=1, source_target_pairs={{0,48},{48,96},{96,144},{144,192},{192,240},{240,288},{288,336},{3... | collective-permute-start | bytes 2359304 | tf_op jit(solution)/shard_map/ppermute | solution.py:14
  95.0 1.9 collective-permute-start.5
  96.9 1.4 convolution_convert_fusion
  98.3 2.0 maximum_bitcast_fusion
  100.4 4.4 collective-permute-done.4
  104.8 4.4 collective-permute-done.5
  109.2 1.6 fusion.33
  111.6 1.9 collective-permute-start.6
  113.5 7.5 %collective-permute-start.7 = (bf16[2,1,128,512]{2,3,0,1:T(8,128)(2,1)S(1)}, bf16[2,1,128,512]{2,3,0,1:T(8,128)(2,1)S(1)}, u32[]{:S(2)}, u32[]{:S(2)}) collective-permute-start(bf16[2,1,128,512]{2,3,0,1:T(8,128)(2,1)S(1)} %get-tuple-element.114), channel_id=1, source_target_pairs={{0,40},{8,0},{16,8},{24,16},{32,24},{40,32},{1,41},{9,1},{17,9},{2... | collective-permute-start | bytes 786440 | tf_op jit(solution)/shard_map/ppermute | solution.py:19
  122.4 1.1 collective-permute-done.6
  123.5 4.2 collective-permute-done.7
  129.4 11.7 %reduce-scatter.2.cloned.1.call-done = bf16[64,1024]{1,0:T(8,128)(2,1)} async-done(((bf16[512,1024]{1,0:T(8,128)(2,1)}), bf16[64,1024]{1,0:T(8,128)(2,1)}) %reduce-scatter.2.cloned.1.call-update) | async-done | bytes 131088 | tf_op jit(solution)/shard_map/reduce_scatter | solution.py:143
  141.1 545.1 %all-reduce.2 = f32[64,1024]{1,0:T(8,128)} all-reduce(bf16[64,1024]{1,0:T(8,128)(2,1)} %reduce-scatter.2.cloned.1.call-done), channel_id=1, replica_groups=mesh['lat'=16,'lon'=6,'opt'=8] {'lat','lon'}, use_global_device_ids=true, to_apply=%region_4.5 | all-reduce | flops 65536 | bytes 393216 | tf_op jit(solution)/shard_map/psum | solution.py:151
  (53 shorter events, 16.5 us)
Async XLA Ops:
  7.2 33.5 %copy-start = (bf16[512,1024]{1,0:T(8,128)(2,1)S(1)}, bf16[512,1024]{1,0:T(8,128)(2,1)}, u32[]{:S(2)}) copy-start(bf16[512,1024]{1,0:T(8,128)(2,1)} %param.22) | copy-start | bytes 3145732
  7.2 33.5 %copy-start.6 = (bf16[1,1,1,128,1024]{4,3,2,1,0:T(8,128)(2,1)S(1)}, bf16[1,1,1,128,1024]{4,3,2,1,0:T(8,128)(2,1)}, u32[]{:S(2)}) copy-start(bf16[1,1,1,128,1024]{4,3,2,1,0:T(8,128)(2,1)} %param.21) | copy-start | bytes 786436
  7.2 34.1 %copy-start.10 = (s32[16,6,9]{0,1,2:T(8,128)S(1)}, s32[16,6,9]{0,1,2:T(8,128)}, u32[]{:S(2)}) copy-start(s32[16,6,9]{0,1,2:T(8,128)} %param.23) | copy-start | bytes 10372
  7.2 133.9 %reduce-scatter.2.cloned.1.call-start = ((), (), s32[]{:S(2)}) async-start(), calls=%async_computation.1 | async-start | bytes 1179648 | tf_op jit(solution)/shard_map/reduce_scatter | solution.py:143
  9.4 9.9 %collective-permute-start.1 = (bf16[2,1,1,128,512]{3,4,2,1,0:T(8,128)(2,1)S(1)}, bf16[2,1,1,128,512]{3,4,2,1,0:T(8,128)(2,1)S(1)}, u32[]{:S(2)}, u32[]{:S(2)}) collective-permute-start(bf16[2,1,1,128,512]{3,4,2,1,0:T(8,128)(2,1)S(1)} %pad_maximum_fusion.2), channel_id=1, source_target_pairs={{48,0},{96,48},{144,96},{192,144},{240,192},{288,240},{336,288},{3... | collective-permute-start | bytes 786440 | tf_op jit(solution)/shard_map/ppermute | solution.py:31
  13.2 11.8 %collective-permute-start = (bf16[2,1,1,128,512]{3,4,2,1,0:T(8,128)(2,1)S(1)}, bf16[2,1,1,128,512]{3,4,2,1,0:T(8,128)(2,1)S(1)}, u32[]{:S(2)}, u32[]{:S(2)}) collective-permute-start(bf16[2,1,1,128,512]{3,4,2,1,0:T(8,128)(2,1)S(1)} %pad_maximum_fusion.2), channel_id=1, source_target_pairs={{0,48},{48,96},{96,144},{144,192},{192,240},{240,288},{288,336},{3... | collective-permute-start | bytes 786440 | tf_op jit(solution)/shard_map/ppermute | solution.py:29
  25.9 47.9 %collective-permute-start.3 = (bf16[2,3,1,128,512]{3,4,2,1,0:T(8,128)(2,1)}, bf16[2,3,1,128,512]{3,4,2,1,0:T(8,128)(2,1)S(1)}, u32[]{:S(2)}, u32[]{:S(2)}) collective-permute-start(bf16[2,3,1,128,512]{3,4,2,1,0:T(8,128)(2,1)} %pad_maximum_fusion.1), channel_id=1, source_target_pairs={{8,0},{16,8},{24,16},{32,24},{40,32},{0,40},{9,1},{17,9},{25,17},{... | collective-permute-start | bytes 2359304 | tf_op jit(solution)/shard_map/ppermute | solution.py:31
  38.7 35.1 %collective-permute-start.2 = (bf16[2,3,1,128,512]{3,4,2,1,0:T(8,128)(2,1)}, bf16[2,3,1,128,512]{3,4,2,1,0:T(8,128)(2,1)}, u32[]{:S(2)}, u32[]{:S(2)}) collective-permute-start(bf16[2,3,1,128,512]{3,4,2,1,0:T(8,128)(2,1)} %pad_maximum_fusion.1), channel_id=1, source_target_pairs={{0,8},{8,16},{16,24},{24,32},{32,40},{40,0},{1,9},{9,17},{17,25},{... | collective-permute-start | bytes 2359304 | tf_op jit(solution)/shard_map/ppermute | solution.py:29
  41.3 37.6 %copy-start.8 = (bf16[128,512]{0,1:T(8,128)(2,1)}, bf16[128,512]{0,1:T(8,128)(2,1)S(1)}, u32[]{:S(2)}) copy-start(bf16[128,512]{0,1:T(8,128)(2,1)S(1)} %copy.26) | copy-start | bytes 393220
  75.3 1.1 copy-start.4
  80.0 0.9 copy-start.9
  82.5 1.4 copy-start.2
  84.1 1.4 copy-start.1
  85.5 11.4 %copy-start.7 = (bf16[1,1,1,128,1024]{4,3,2,1,0:T(8,128)(2,1)S(1)}, bf16[1,1,1,128,1024]{4,3,2,1,0:T(8,128)(2,1)}, u32[]{:S(2)}) copy-start(bf16[1,1,1,128,1024]{4,3,2,1,0:T(8,128)(2,1)} %param.21) | copy-start | bytes 786436
  86.8 18.0 %collective-permute-start.4 = (bf16[2,3,128,512]{2,3,1,0:T(8,128)(2,1)}, bf16[2,3,128,512]{2,3,1,0:T(8,128)(2,1)}, u32[]{:S(2)}, u32[]{:S(2)}) collective-permute-start(bf16[2,3,128,512]{2,3,1,0:T(8,128)(2,1)} %get-tuple-element.109), channel_id=1, source_target_pairs={{0,48},{48,96},{96,144},{144,192},{192,240},{240,288},{288,336},{3... | collective-permute-start | bytes 2359304 | tf_op jit(solution)/shard_map/ppermute | solution.py:14
  95.0 14.2 %collective-permute-start.5 = (bf16[2,3,128,512]{2,3,1,0:T(8,128)(2,1)}, bf16[2,3,128,512]{2,3,1,0:T(8,128)(2,1)}, u32[]{:S(2)}, u32[]{:S(2)}) collective-permute-start(bf16[2,3,128,512]{2,3,1,0:T(8,128)(2,1)} %get-tuple-element.110), channel_id=1, source_target_pairs={{48,0},{96,48},{144,96},{192,144},{240,192},{288,240},{336,288},{3... | collective-permute-start | bytes 2359304 | tf_op jit(solution)/shard_map/ppermute | solution.py:14
  100.3 20.7 %copy-start.3 = (bf16[8,128,9,128]{1,3,2,0:T(8,128)(2,1)S(1)}, bf16[8,128,9,128]{1,3,2,0:T(8,128)(2,1)}, u32[]{:S(2)}) copy-start(bf16[8,128,9,128]{1,3,2,0:T(8,128)(2,1)} %copy-done.2) | copy-start | bytes 7077892
  100.3 20.7 %copy-start.5 = (bf16[1,3,3,128,512]{3,4,2,1,0:T(8,128)(2,1)S(1)}, bf16[1,3,3,128,512]{3,4,2,1,0:T(8,128)(2,1)}, u32[]{:S(2)}) copy-start(bf16[1,3,3,128,512]{3,4,2,1,0:T(8,128)(2,1)} %copy-done.4) | copy-start | bytes 3538948
  111.6 12.0 %collective-permute-start.6 = (bf16[2,1,128,512]{2,3,0,1:T(8,128)(2,1)}, bf16[2,1,128,512]{2,3,0,1:T(8,128)(2,1)S(1)}, u32[]{:S(2)}, u32[]{:S(2)}) collective-permute-start(bf16[2,1,128,512]{2,3,0,1:T(8,128)(2,1)} %get-tuple-element.113), channel_id=1, source_target_pairs={{0,8},{8,16},{16,24},{24,32},{32,40},{40,0},{1,9},{9,17},{17,25},{... | collective-permute-start | bytes 786440 | tf_op jit(solution)/shard_map/ppermute | solution.py:19
  113.5 14.2 %collective-permute-start.7 = (bf16[2,1,128,512]{2,3,0,1:T(8,128)(2,1)S(1)}, bf16[2,1,128,512]{2,3,0,1:T(8,128)(2,1)S(1)}, u32[]{:S(2)}, u32[]{:S(2)}) collective-permute-start(bf16[2,1,128,512]{2,3,0,1:T(8,128)(2,1)S(1)} %get-tuple-element.114), channel_id=1, source_target_pairs={{0,40},{8,0},{16,8},{24,16},{32,24},{40,32},{1,41},{9,1},{17,9},{2... | collective-permute-start | bytes 786440 | tf_op jit(solution)/shard_map/ppermute | solution.py:19
Sparse Core Ops, SparseCore 0:
  98.5 42.5 reduce-scatter.1
where the time goes:
time: 694 us; the launch traced here: 693 us
  blocking collectives  545 us (79%)
  waiting for transfers between devices  66.5 us (10%)
  starting transfers between devices  40.1 us (6%)
  between operations  14.4 us (2%)
  local copies, waits for them, and re-layouts  10.3 us (1%)
  other arithmetic  8.75 us (1%)
  matrix products  7.8 us (1%)
    psum x1, blocking collectives, shards(): grad_weight = lax.psum(w_share, ('lat', 'lon'))  545 us
    ppermute x2, waiting for transfers between devices, with_halo(): lax.ppermute(head, axis, [((i + 1) % count, i) for i in range(count)])  35.1 us
    ppermute x2, starting transfers between devices, with_halo(): lax.ppermute(head, axis, [((i + 1) % count, i) for i in range(count)])  16.5 us
  transfers between devices with their start and end apart: 9, of which 8 were waited for; matrix products, arithmetic and copies ran while one was open for 2% of the time, Pallas kernels for 0%

commit v1 on v0

v1 whole, which is shorter than its diff:
```python
import jax
import jax.numpy as jnp
from jax import lax
from jax.sharding import PartitionSpec as P

HDIM = 64
SCALE = HDIM ** (-0.5)


def around(array, axis, by):
    count = lax.axis_size(axis)
    return lax.ppermute(array, axis, [(i, (i + by) % count) for i in range(count)])


def along(array, axis, by):
    count = lax.axis_size(axis)
    return lax.ppermute(array, axis, [(i, i + by) for i in range(count) if 0 <= i + by < count])


def to_all(array, axis):
    count = lax.axis_size(axis)
    return lax.all_to_all(jnp.broadcast_to(array[None], (count,) + array.shape), axis, 0, 0)


def heads_of(array):
    return array.reshape(array.shape[:-1] + (array.shape[-1] // HDIM, HDIM))


def attention(query, dout, near_keys, near_values, live):
    query_heads, dout_heads = heads_of(query), heads_of(dout)
    keys, values = heads_of(near_keys), heads_of(near_values)
    live = live[None, None, :, None]
    scores = (
        jnp.einsum("qhe,dkhe->hqdk", query_heads, keys, preferred_element_type=jnp.float32)
        * SCALE
    )
    row_max = jnp.max(jnp.where(live, scores, -jnp.inf), axis=(2, 3))
    weights = jnp.where(live, jnp.exp(scores - row_max[:, :, None, None]), 0.0)
    log_norm = row_max + jnp.log(jnp.sum(weights, axis=(2, 3)))
    prob = jnp.where(live, jnp.exp(scores - log_norm[:, :, None, None]), 0.0)
    prob_low = prob.astype(jnp.bfloat16)
    attended = jnp.einsum(
        "hqdk,dkhe->qhe", prob_low, values, preferred_element_type=jnp.float32
    ).astype(jnp.bfloat16)
    row_delta = jnp.sum(dout_heads.astype(jnp.float32) * attended.astype(jnp.float32), axis=2).T
    grad_prob = jnp.einsum("qhe,dkhe->hqdk", dout_heads, values, preferred_element_type=jnp.float32)
    grad_score = (prob * (grad_prob - row_delta[:, :, None, None])).astype(jnp.bfloat16)
    grad_query = (
        jnp.einsum("hqdk,dkhe->qhe", grad_score, keys, preferred_element_type=jnp.float32) * SCALE
    )
    key_part = (
        jnp.einsum("hqdk,qhe->dkhe", grad_score, query_heads, preferred_element_type=jnp.float32)
        * SCALE
    )
    value_part = jnp.einsum(
        "hqdk,qhe->dkhe", prob_low, dout_heads, preferred_element_type=jnp.float32
    )
    flat = query.shape
    pair = jnp.stack((key_part, value_part), axis=1).reshape((9, 2) + flat)
    return attended.reshape(flat), grad_query.astype(jnp.bfloat16).reshape(flat), pair


def shards(queries, keys, values, grad_out, w_out, pattern):
    low, wide = jnp.bfloat16, jnp.float32
    query, key, value, grad = queries[0, 0, 0], keys[0, 0, 0], values[0, 0, 0], grad_out[0, 0, 0]
    block_len, att_width = query.shape
    model_width = grad.shape[1]
    lat_count, opt_count = lax.axis_size("lat"), lax.axis_size("opt")
    at_lat, at_lon = lax.axis_index("lat"), lax.axis_index("lon")

    own = jnp.stack((key, value))
    left, right = around(own, "lon", 1), around(own, "lon", -1)
    row = jnp.stack((left, own, right))
    above, below = along(row, "lat", 1), along(row, "lat", -1)
    grads_of_samples = to_all(grad, "opt")

    dout = lax.dot_general(
        grad, w_out, (((1,), (1,)), ((), ())), preferred_element_type=wide
    ).astype(low)
    flags = lax.dynamic_slice(pattern, (at_lat, at_lon, 0), (1, 1, 9)).reshape(9)
    key_rows = at_lat + jnp.arange(9) // 3 - 1
    live = (flags > 0) & (key_rows >= 0) & (key_rows < lat_count)

    near = jnp.stack((above, row, below)).reshape(9, 2, block_len, att_width)
    near, grads_of_samples = lax.optimization_barrier((near, grads_of_samples))
    attended, grad_query, pair = attention(query, dout, near[:, 0], near[:, 1], live)

    attended_of_samples = lax.all_to_all(
        attended.T.reshape(opt_count, att_width // opt_count, block_len), "opt", 0, 0
    )
    w_part = jnp.einsum(
        "srt,stc->rc", attended_of_samples, grads_of_samples, preferred_element_type=wide
    ).astype(low)
    w_rows = w_part.shape[0] // lat_count
    w_part = lax.all_to_all(w_part.reshape(lat_count, w_rows, model_width), "lat", 0, 0)
    w_part = jnp.sum(w_part.astype(wide), axis=0).astype(low)
    w_part = jnp.sum(to_all(w_part, "lon").astype(wide), axis=0).astype(low)
    grad_weight = to_all(w_part, "lat").reshape(lat_count * w_rows, model_width).astype(wide)

    pair = pair.reshape(3, 3, 2, block_len, att_width)
    up, down = along(pair[0].astype(low), "lat", -1), along(pair[2].astype(low), "lat", 1)
    sums = pair[1] + up.astype(wide) + down.astype(wide)
    from_right, from_left = around(sums[0].astype(low), "lon", -1), around(sums[2].astype(low), "lon", 1)
    owned = (sums[1] + from_right.astype(wide) + from_left.astype(wide)).astype(low)
    return (
        grad_query[None, None, None],
        owned[0][None, None, None],
        owned[1][None, None, None],
        grad_weight,
    )


def solution(mesh):
    blocks = P("opt", "lat", "lon", None, None)
    return jax.shard_map(
        shards,
        mesh=mesh,
        in_specs=(blocks, blocks, blocks, blocks, P(), P()),
        out_specs=(blocks, blocks, blocks, P("opt", None)),
        check_vma=False,
    )
```

time: 694 us -> 164 us (0.24)
  the two profiles are of different devices: /device:TPU:64 before, /device:TPU:72 now
where the time goes in v1:
time: 164 us; the launch traced here: 163 us
  starting transfers between devices  80 us (49%)
  waiting for transfers between devices  40.6 us (25%)
  other arithmetic  15.3 us (9%)
  local copies, waits for them, and re-layouts  15 us (9%)
  matrix products  11.2 us (7%)
    ppermute x4, starting transfers between devices, around(): lax.ppermute(array, axis, [(i, (i + by) % count) for i in range(count)])  24.1 us
    all_to_all x3, starting transfers between devices, to_all(): lax.all_to_all(jnp.broadcast_to(array[None], (count,) + array.shape), axi...  24.1 us
    ppermute x4, waiting for transfers between devices, around(): lax.ppermute(array, axis, [(i, (i + by) % count) for i in range(count)])  23.9 us
    ppermute x4, starting transfers between devices, along(): lax.ppermute(array, axis, [(i, i + by) for i in range(count) if 0 <= i +...  20.6 us
    ppermute x4, waiting for transfers between devices, along(): lax.ppermute(array, axis, [(i, i + by) for i in range(count) if 0 <= i +...  11.8 us
    all_to_all x1, starting transfers between devices, shards(): lax.all_to_all(attended.T.reshape(opt_count, att_width // opt_count, bloc...  7.21 us
    another operation x2, other arithmetic  5.02 us
    all_to_all x1, waiting for transfers between devices, shards(): lax.all_to_all(w_part.reshape(lat_count, w_rows, model_width), 'lat', 0, 0)  4.88 us
  transfers between devices with their start and end apart: 13, of which 6 were waited for; matrix products, arithmetic and copies ran while one was open for 18% of the time, Pallas kernels for 0%

profile of v1, /device:TPU:72, one launch (start us, length us, event | category | flops | bytes accessed | tf_op | source)
XLA Modules:
  0.0 163.1 jit_solution(902405707555381053)
XLA Ops:
  0.6 2.6 %broadcast_in_dim.46 = bf16[8,128,1024]{2,1,0:T(8,128)(2,1)} broadcast(bf16[128,1024]{1,0:T(8,128)(2,1)} %bitcast.105), dimensions={1,2} | broadcast | bytes 2359296 | tf_op jit(solution)/shard_map/broadcast_in_dim | solution.py:22
  3.3 7.7 %all-to-all-start = ((bf16[8,128,1024]{2,1,0:T(8,128)(2,1)}), bf16[8,128,1024]{2,1,0:T(8,128)(2,1)}, u32[]{:S(2)}, u32[]{:S(2)}) async-start(bf16[8,128,1024]{2,1,0:T(8,128)(2,1)} %broadcast_in_dim.46), calls=%async_computation | async-start | bytes 4194304 | tf_op jit(solution)/shard_map/all_to_all | solution.py:22
  11.0 12.7 %collective-permute-start.1 = (bf16[2,128,512]{2,1,0:T(8,128)(2,1)S(1)}, bf16[2,128,512]{2,1,0:T(8,128)(2,1)S(1)}, u32[]{:S(2)}, u32[]{:S(2)}) collective-permute-start(bf16[2,128,512]{2,1,0:T(8,128)(2,1)S(1)} %get-tuple-element.33), channel_id=1, source_target_pairs={{0,40},{8,0},{16,8},{24,16},{32,24},{40,32},{1,41},{9,1},{17,9},{2... | collective-permute-start | bytes 786440 | tf_op jit(solution)/shard_map/ppermute | solution.py:12
  23.7 1.9 %collective-permute-start = (bf16[2,128,512]{2,1,0:T(8,128)(2,1)S(1)}, bf16[2,128,512]{2,1,0:T(8,128)(2,1)S(1)}, u32[]{:S(2)}, u32[]{:S(2)}) collective-permute-start(bf16[2,128,512]{2,1,0:T(8,128)(2,1)S(1)} %get-tuple-element.33), channel_id=1, source_target_pairs={{0,8},{8,16},{16,24},{24,32},{32,40},{40,0},{1,9},{9,17},{17,25},{... | collective-permute-start | bytes 786440 | tf_op jit(solution)/shard_map/ppermute | solution.py:12
  25.6 8.7 %collective-permute-done.1 = bf16[2,128,512]{2,1,0:T(8,128)(2,1)S(1)} collective-permute-done((bf16[2,128,512]{2,1,0:T(8,128)(2,1)S(1)}, bf16[2,128,512]{2,1,0:T(8,128)(2,1)S(1)}, u32[]{:S(2)}, u32[]{:S(2)}) %collective-permute-start.1) | collective-permute-done | bytes 262176 | tf_op jit(solution)/shard_map/ppermute | solution.py:12
  34.3 3.4 %collective-permute-done = bf16[2,128,512]{2,1,0:T(8,128)(2,1)S(1)} collective-permute-done((bf16[2,128,512]{2,1,0:T(8,128)(2,1)S(1)}, bf16[2,128,512]{2,1,0:T(8,128)(2,1)S(1)}, u32[]{:S(2)}, u32[]{:S(2)}) %collective-permute-start) | collective-permute-done | bytes 262176 | tf_op jit(solution)/shard_map/ppermute | solution.py:12
  38.7 10.7 %collective-permute-start.3 = (bf16[3,2,128,512]{3,2,1,0:T(8,128)(2,1)}, bf16[3,2,128,512]{3,2,1,0:T(8,128)(2,1)S(1)}, u32[]{:S(2)}, u32[]{:S(2)}) collective-permute-start(bf16[3,2,128,512]{3,2,1,0:T(8,128)(2,1)} %get-tuple-element.29), channel_id=1, source_target_pairs={{48,0},{96,48},{144,96},{192,144},{240,192},{288,240},{336,288},{3... | collective-permute-start | bytes 2359304 | tf_op jit(solution)/shard_map/ppermute | solution.py:17
  49.4 1.9 %collective-permute-start.2 = (bf16[3,2,128,512]{3,2,1,0:T(8,128)(2,1)}, bf16[3,2,128,512]{3,2,1,0:T(8,128)(2,1)}, u32[]{:S(2)}, u32[]{:S(2)}) collective-permute-start(bf16[3,2,128,512]{3,2,1,0:T(8,128)(2,1)} %get-tuple-element.29), channel_id=1, source_target_pairs={{0,48},{48,96},{96,144},{144,192},{192,240},{240,288},{288,336},{3... | collective-permute-start | bytes 2359304 | tf_op jit(solution)/shard_map/ppermute | solution.py:17
  53.9 5.3 %collective-permute-done.3 = bf16[3,2,128,512]{3,2,1,0:T(8,128)(2,1)S(1)} collective-permute-done((bf16[3,2,128,512]{3,2,1,0:T(8,128)(2,1)}, bf16[3,2,128,512]{3,2,1,0:T(8,128)(2,1)S(1)}, u32[]{:S(2)}, u32[]{:S(2)}) %collective-permute-start.3) | collective-permute-done | bytes 786464 | tf_op jit(solution)/shard_map/ppermute | solution.py:17
  59.2 6.5 %collective-permute-done.2 = bf16[3,2,128,512]{3,2,1,0:T(8,128)(2,1)} collective-permute-done((bf16[3,2,128,512]{3,2,1,0:T(8,128)(2,1)}, bf16[3,2,128,512]{3,2,1,0:T(8,128)(2,1)}, u32[]{:S(2)}, u32[]{:S(2)}) %collective-permute-start.2) | collective-permute-done | bytes 786464 | tf_op jit(solution)/shard_map/ppermute | solution.py:17
  65.7 2.8 %pad_maximum_fusion.1 = bf16[3,3,2,128,512]{4,3,2,1,0:T(8,128)(2,1)} fusion(bf16[1,3,2,128,512]{4,3,2,1,0:T(8,128)(2,1)S(1)} %bitcast.106, bf16[1,3,2,128,512]{4,3,2,1,0:T(8,128)(2,1)S(1)} %get-tuple-element.28, bf16[1,3,2,128,512]{4,3,2,1,0:T(8,128)(2,1)} %bitcast.5), kind=kLoop, calls=%fused_computation.10 | loop fusion | flops 2359296 | bytes 4718592 | tf_op jit(solution)/shard_map/stack | solution.py:84
  68.5 3.0 %copy.39 = bf16[3,3,2,128,512]{3,4,1,0,2:T(8,128)(2,1)S(1)} copy(bf16[3,3,2,128,512]{4,3,2,1,0:T(8,128)(2,1)} %pad_maximum_fusion.1) | data formatting | bytes 4718592 | tf_op jit(solution)/shard_map/stack | solution.py:84
  78.7 2.4 %multiply_bitcast_fusion = f32[9,1,128,8,64]{2,4,0,3,1:T(8,128)} fusion(bf16[8,128,9,128]{1,3,2,0:T(8,128)(2,1)S(1)} %fusion.1, bf16[128,8,64,1]{0,2,3,1:T(8,128)(2,1)S(1)} %bitcast.108), kind=kOutput, calls=%fused_computation.15 | convolution fusion | flops 151584768 | bytes 4849664 | tf_op jit(solution)/shard_map/hqdk,qhe->dkhe/dot_general | solution.py:52
  81.1 7.2 %all-to-all-start.1 = ((bf16[8,64,128]{2,1,0:T(8,128)(2,1)}), bf16[8,64,128]{2,1,0:T(8,128)(2,1)S(1)}, u32[]{:S(2)}, u32[]{:S(2)}) async-start(bf16[8,64,128]{2,1,0:T(8,128)(2,1)} %get-tuple-element.37), calls=%async_computation.1 | async-start | bytes 262144 | tf_op jit(solution)/shard_map/all_to_all | solution.py:88
  88.4 2.1 %fusion = bf16[9,2,128,8,64]{2,4,0,3,1:T(8,128)(2,1)S(1)} fusion(f32[9,1,128,8,64]{2,4,0,3,1:T(8,128)S(1)} %convolution_bitcast_fusion, f32[9,1,128,8,64]{2,4,0,3,1:T(8,128)} %multiply_bitcast_fusion), kind=kLoop, calls=%fused_computation.3 | loop fusion | flops 1179648 | bytes 7077888 | tf_op jit(solution)/shard_map/convert.6
  94.5 6.0 %collective-permute-start.4 = (bf16[3,2,128,512]{2,3,1,0:T(8,128)(2,1)}, bf16[3,2,128,512]{2,3,1,0:T(8,128)(2,1)}, u32[]{:S(2)}, u32[]{:S(2)}) collective-permute-start(bf16[3,2,128,512]{2,3,1,0:T(8,128)(2,1)} %bitcast.34), channel_id=1, source_target_pairs={{48,0},{96,48},{144,96},{192,144},{240,192},{288,240},{336,288},{3... | collective-permute-start | bytes 2359304 | tf_op jit(solution)/shard_map/ppermute | solution.py:17
  100.5 2.7 %fusion.20 = bf16[64,1024]{1,0:T(8,128)(2,1)} fusion(bf16[8,64,128]{2,1,0:T(8,128)(2,1)S(1)} %all-to-all-done.1, bf16[8,128,1024]{2,1,0:T(8,128)(2,1)} %all-to-all-done), kind=kOutput, calls=%fused_computation.27 | convolution fusion | flops 134283264 | bytes 2359296 | tf_op jit(solution)/shard_map/srt,stc->rc/dot_general | solution.py:91
  104.8 4.1 %all-to-all-start.2 = ((bf16[16,4,1024]{2,1,0:T(4,128)(2,1)}), bf16[16,4,1024]{2,1,0:T(4,128)(2,1)}, u32[]{:S(2)}, u32[]{:S(2)}) async-start(bf16[16,4,1024]{2,1,0:T(4,128)(2,1)} %reshape.78), calls=%async_computation.2 | async-start | bytes 262144 | tf_op jit(solution)/shard_map/all_to_all | solution.py:95
  110.3 4.9 %all-to-all-done.2 = bf16[16,4,1024]{2,1,0:T(4,128)(2,1)} async-done(((bf16[16,4,1024]{2,1,0:T(4,128)(2,1)}), bf16[16,4,1024]{2,1,0:T(4,128)(2,1)}, u32[]{:S(2)}, u32[]{:S(2)}) %all-to-all-start.2) | async-done | bytes 131104 | tf_op jit(solution)/shard_map/all_to_all | solution.py:95
  116.8 10.5 %all-to-all-start.3 = ((bf16[6,4,1024]{2,1,0:T(4,128)(2,1)}), bf16[6,4,1024]{2,1,0:T(4,128)(2,1)S(1)}, u32[]{:S(2)}, u32[]{:S(2)}) async-start(bf16[6,4,1024]{2,1,0:T(4,128)(2,1)} %broadcast_in_dim.50), calls=%async_computation.3 | async-start | bytes 98304 | tf_op jit(solution)/shard_map/all_to_all | solution.py:22
  127.4 3.0 %fusion.35 = (bf16[3,2,128,512]{2,3,1,0:T(8,128)(2,1)S(1)}, f32[3,2,128,512]{2,3,1,0:T(8,128)}) fusion(bf16[3,2,128,512]{2,3,1,0:T(8,128)(2,1)} %collective-permute-done.5, bf16[3,2,128,512]{2,3,1,0:T(8,128)(2,1)} %collective-permute-done.4, f32[3,2,128,8,64]{2,4,3,1,0:T(8,128)S(1)} %copy.49), kind=kLoop, calls=%fused_computation.54 | loop fusion | flops 1966080 | bytes 5505024 | tf_op jit(solution)/shard_map/convert.4
  130.4 7.6 %collective-permute-start.6 = (bf16[2,128,512]{1,2,0:T(8,128)(2,1)S(1)}, bf16[2,128,512]{1,2,0:T(8,128)(2,1)S(1)}, u32[]{:S(2)}, u32[]{:S(2)}) collective-permute-start(bf16[2,128,512]{1,2,0:T(8,128)(2,1)S(1)} %get-tuple-element.26), channel_id=1, source_target_pairs={{0,40},{8,0},{16,8},{24,16},{32,24},{40,32},{1,41},{9,1},{17,9},{2... | collective-permute-start | bytes 786440 | tf_op jit(solution)/shard_map/ppermute | solution.py:12
  142.0 5.9 %all-to-all-start.4 = ((bf16[16,4,1024]{2,1,0:T(4,128)(2,1)}), bf16[16,4,1024]{2,1,0:T(4,128)(2,1)S(1)}, u32[]{:S(2)}, u32[]{:S(2)}) async-start(bf16[16,4,1024]{2,1,0:T(4,128)(2,1)} %broadcast_in_dim.51), calls=%async_computation.4 | async-start | bytes 262144 | tf_op jit(solution)/shard_map/all_to_all | solution.py:22
  147.9 11.8 %collective-permute-done.7 = bf16[2,128,512]{1,2,0:T(8,128)(2,1)S(1)} collective-permute-done((bf16[2,128,512]{1,2,0:T(8,128)(2,1)S(1)}, bf16[2,128,512]{1,2,0:T(8,128)(2,1)S(1)}, u32[]{:S(2)}, u32[]{:S(2)}) %collective-permute-start.7) | collective-permute-done | bytes 262176 | tf_op jit(solution)/shard_map/ppermute | solution.py:12
  (62 shorter events, 26.7 us)
Async XLA Ops:
  0.6 50.8 %copy-start = (bf16[512,1024]{1,0:T(8,128)(2,1)S(1)}, bf16[512,1024]{1,0:T(8,128)(2,1)}, u32[]{:S(2)}) copy-start(bf16[512,1024]{1,0:T(8,128)(2,1)} %param.10) | copy-start | bytes 3145732
  3.3 7.7 %copy-start.8 = (bf16[1,1,1,128,512]{4,3,2,1,0:T(8,128)(2,1)S(1)}, bf16[1,1,1,128,512]{4,3,2,1,0:T(8,128)(2,1)}, u32[]{:S(2)}) copy-start(bf16[1,1,1,128,512]{4,3,2,1,0:T(8,128)(2,1)} %param.8) | copy-start | bytes 393220
  3.3 7.7 %copy-start.9 = (bf16[1,1,1,128,512]{4,3,2,1,0:T(8,128)(2,1)S(1)}, bf16[1,1,1,128,512]{4,3,2,1,0:T(8,128)(2,1)}, u32[]{:S(2)}) copy-start(bf16[1,1,1,128,512]{4,3,2,1,0:T(8,128)(2,1)} %param.7) | copy-start | bytes 393220
  3.3 68.3 %all-to-all-start = ((bf16[8,128,1024]{2,1,0:T(8,128)(2,1)}), bf16[8,128,1024]{2,1,0:T(8,128)(2,1)}, u32[]{:S(2)}, u32[]{:S(2)}) async-start(bf16[8,128,1024]{2,1,0:T(8,128)(2,1)} %broadcast_in_dim.46), calls=%async_computation | async-start | bytes 4194304 | tf_op jit(solution)/shard_map/all_to_all | solution.py:22
  11.0 40.4 %copy-start.7 = (bf16[1,1,1,128,512]{4,3,2,1,0:T(8,128)(2,1)S(1)}, bf16[1,1,1,128,512]{4,3,2,1,0:T(8,128)(2,1)}, u32[]{:S(2)}) copy-start(bf16[1,1,1,128,512]{4,3,2,1,0:T(8,128)(2,1)} %param.6) | copy-start | bytes 393220
  11.0 40.5 %copy-start.5 = (bf16[1,1,1,128,1024]{4,3,2,1,0:T(8,128)(2,1)S(1)}, bf16[1,1,1,128,1024]{4,3,2,1,0:T(8,128)(2,1)}, u32[]{:S(2)}) copy-start(bf16[1,1,1,128,1024]{4,3,2,1,0:T(8,128)(2,1)} %param.9) | copy-start | bytes 786436
  11.0 23.3 %collective-permute-start.1 = (bf16[2,128,512]{2,1,0:T(8,128)(2,1)S(1)}, bf16[2,128,512]{2,1,0:T(8,128)(2,1)S(1)}, u32[]{:S(2)}, u32[]{:S(2)}) collective-permute-start(bf16[2,128,512]{2,1,0:T(8,128)(2,1)S(1)} %get-tuple-element.33), channel_id=1, source_target_pairs={{0,40},{8,0},{16,8},{24,16},{32,24},{40,32},{1,41},{9,1},{17,9},{2... | collective-permute-start | bytes 786440 | tf_op jit(solution)/shard_map/ppermute | solution.py:12
  23.7 14.0 %collective-permute-start = (bf16[2,128,512]{2,1,0:T(8,128)(2,1)S(1)}, bf16[2,128,512]{2,1,0:T(8,128)(2,1)S(1)}, u32[]{:S(2)}, u32[]{:S(2)}) collective-permute-start(bf16[2,128,512]{2,1,0:T(8,128)(2,1)S(1)} %get-tuple-element.33), channel_id=1, source_target_pairs={{0,8},{8,16},{16,24},{24,32},{32,40},{40,0},{1,9},{9,17},{17,25},{... | collective-permute-start | bytes 786440 | tf_op jit(solution)/shard_map/ppermute | solution.py:12
  38.7 20.5 %collective-permute-start.3 = (bf16[3,2,128,512]{3,2,1,0:T(8,128)(2,1)}, bf16[3,2,128,512]{3,2,1,0:T(8,128)(2,1)S(1)}, u32[]{:S(2)}, u32[]{:S(2)}) collective-permute-start(bf16[3,2,128,512]{3,2,1,0:T(8,128)(2,1)} %get-tuple-element.29), channel_id=1, source_target_pairs={{48,0},{96,48},{144,96},{192,144},{240,192},{288,240},{336,288},{3... | collective-permute-start | bytes 2359304 | tf_op jit(solution)/shard_map/ppermute | solution.py:17
  49.4 16.3 %collective-permute-start.2 = (bf16[3,2,128,512]{3,2,1,0:T(8,128)(2,1)}, bf16[3,2,128,512]{3,2,1,0:T(8,128)(2,1)}, u32[]{:S(2)}, u32[]{:S(2)}) collective-permute-start(bf16[3,2,128,512]{3,2,1,0:T(8,128)(2,1)} %get-tuple-element.29), channel_id=1, source_target_pairs={{0,48},{48,96},{96,144},{144,192},{192,240},{240,288},{288,336},{3... | collective-permute-start | bytes 2359304 | tf_op jit(solution)/shard_map/ppermute | solution.py:17
  71.7 1.1 copy-start.3
  73.8 1.0 copy-start.6
  78.7 2.4 %copy-start.1 = (bf16[8,128,9,128]{1,3,2,0:T(8,128)(2,1)}, bf16[8,128,9,128]{1,3,2,0:T(8,128)(2,1)S(1)}, u32[]{:S(2)}) copy-start(bf16[8,128,9,128]{1,3,2,0:T(8,128)(2,1)S(1)} %fusion.1) | copy-start | bytes 7077892
  81.1 19.3 %all-to-all-start.1 = ((bf16[8,64,128]{2,1,0:T(8,128)(2,1)}), bf16[8,64,128]{2,1,0:T(8,128)(2,1)S(1)}, u32[]{:S(2)}, u32[]{:S(2)}) async-start(bf16[8,64,128]{2,1,0:T(8,128)(2,1)} %get-tuple-element.37), calls=%async_computation.1 | async-start | bytes 262144 | tf_op jit(solution)/shard_map/all_to_all | solution.py:88
  92.5 34.8 %collective-permute-start.5 = (bf16[3,2,128,512]{2,3,1,0:T(8,128)(2,1)}, bf16[3,2,128,512]{2,3,1,0:T(8,128)(2,1)}, u32[]{:S(2)}, u32[]{:S(2)}) collective-permute-start(bf16[3,2,128,512]{2,3,1,0:T(8,128)(2,1)} %bitcast.35), channel_id=1, source_target_pairs={{0,48},{48,96},{96,144},{144,192},{192,240},{240,288},{288,336},{3... | collective-permute-start | bytes 2359304 | tf_op jit(solution)/shard_map/ppermute | solution.py:17
  94.5 32.9 %collective-permute-start.4 = (bf16[3,2,128,512]{2,3,1,0:T(8,128)(2,1)}, bf16[3,2,128,512]{2,3,1,0:T(8,128)(2,1)}, u32[]{:S(2)}, u32[]{:S(2)}) collective-permute-start(bf16[3,2,128,512]{2,3,1,0:T(8,128)(2,1)} %bitcast.34), channel_id=1, source_target_pairs={{48,0},{96,48},{144,96},{192,144},{240,192},{288,240},{336,288},{3... | collective-permute-start | bytes 2359304 | tf_op jit(solution)/shard_map/ppermute | solution.py:17
  104.8 10.3 %all-to-all-start.2 = ((bf16[16,4,1024]{2,1,0:T(4,128)(2,1)}), bf16[16,4,1024]{2,1,0:T(4,128)(2,1)}, u32[]{:S(2)}, u32[]{:S(2)}) async-start(bf16[16,4,1024]{2,1,0:T(4,128)(2,1)} %reshape.78), calls=%async_computation.2 | async-start | bytes 262144 | tf_op jit(solution)/shard_map/all_to_all | solution.py:95
  116.8 24.5 %all-to-all-start.3 = ((bf16[6,4,1024]{2,1,0:T(4,128)(2,1)}), bf16[6,4,1024]{2,1,0:T(4,128)(2,1)S(1)}, u32[]{:S(2)}, u32[]{:S(2)}) async-start(bf16[6,4,1024]{2,1,0:T(4,128)(2,1)} %broadcast_in_dim.50), calls=%async_computation.3 | async-start | bytes 98304 | tf_op jit(solution)/shard_map/all_to_all | solution.py:22
  127.3 12.5 %copy-start.2 = (bf16[8,128,9,128]{1,3,2,0:T(8,128)(2,1)S(1)}, bf16[8,128,9,128]{1,3,2,0:T(8,128)(2,1)}, u32[]{:S(2)}) copy-start(bf16[8,128,9,128]{1,3,2,0:T(8,128)(2,1)} %copy-done.1) | copy-start | bytes 7077892
  127.3 12.5 %copy-start.4 = (bf16[9,1,128,512]{2,3,0,1:T(8,128)(2,1)S(1)}, bf16[9,1,128,512]{2,3,0,1:T(8,128)(2,1)}, u32[]{:S(2)}) copy-start(bf16[9,1,128,512]{2,3,0,1:T(8,128)(2,1)} %copy-done.3) | copy-start | bytes 3538948
  130.4 17.5 %collective-permute-start.6 = (bf16[2,128,512]{1,2,0:T(8,128)(2,1)S(1)}, bf16[2,128,512]{1,2,0:T(8,128)(2,1)S(1)}, u32[]{:S(2)}, u32[]{:S(2)}) collective-permute-start(bf16[2,128,512]{1,2,0:T(8,128)(2,1)S(1)} %get-tuple-element.26), channel_id=1, source_target_pairs={{0,40},{8,0},{16,8},{24,16},{32,24},{40,32},{1,41},{9,1},{17,9},{2... | collective-permute-start | bytes 786440 | tf_op jit(solution)/shard_map/ppermute | solution.py:12
  138.0 21.7 %collective-permute-start.7 = (bf16[2,128,512]{1,2,0:T(8,128)(2,1)S(1)}, bf16[2,128,512]{1,2,0:T(8,128)(2,1)S(1)}, u32[]{:S(2)}, u32[]{:S(2)}) collective-permute-start(bf16[2,128,512]{1,2,0:T(8,128)(2,1)S(1)} %get-tuple-element.27), channel_id=1, source_target_pairs={{0,8},{8,16},{16,24},{24,32},{32,40},{40,0},{1,9},{9,17},{17,25},{... | collective-permute-start | bytes 786440 | tf_op jit(solution)/shard_map/ppermute | solution.py:12
  142.0 20.4 %all-to-all-start.4 = ((bf16[16,4,1024]{2,1,0:T(4,128)(2,1)}), bf16[16,4,1024]{2,1,0:T(4,128)(2,1)S(1)}, u32[]{:S(2)}, u32[]{:S(2)}) async-start(bf16[16,4,1024]{2,1,0:T(4,128)(2,1)} %broadcast_in_dim.51), calls=%async_computation.4 | async-start | bytes 262144 | tf_op jit(solution)/shard_map/all_to_all | solution.py:22

commit v2 on v1

v2 whole, which is shorter than its diff:
```python
import jax
import jax.numpy as jnp
from jax import lax
from jax.experimental import pallas as pl
from jax.experimental.pallas import tpu as pltpu
from jax.sharding import PartitionSpec as P

HDIM = 64
SCALE = HDIM ** (-0.5)
DEAD = -1e30
LANES = 2 * HDIM


def exchange(array, axis, mate):
    pairs = [(i, mate(i)) for i in range(lax.axis_size(axis))]
    return lax.ppermute(array, axis, [(i, j) for i, j in pairs if 0 <= j < lax.axis_size(axis)])


def next_door(i):
    return i ^ 1


def other_door(i):
    return i - 1 if i % 2 == 0 else i + 1


def partner_of(array):
    return exchange(array, "lon", next_door)


def far_of(array):
    count = lax.axis_size("lon")
    return exchange(array, "lon", lambda i: other_door(i) % count)


def lat_mates_of(array):
    return exchange(array, "lat", next_door), exchange(array, "lat", other_door)


def to_all(array, axis):
    count = lax.axis_size(axis)
    return lax.all_to_all(jnp.broadcast_to(array[None], (count,) + array.shape), axis, 0, 0)


def sum_over_lon(part):
    count = lax.axis_size("lon")
    chips = count // 2
    part = part + partner_of(part)
    at = lax.axis_index("lon") // 2
    terms = [part] + [
        lax.ppermute(part, "lon", [(i, (i + 2 * by) % count) for i in range(count)])
        for by in range(1, chips)
    ]
    total = None
    for chip in range(chips):
        term = terms[0]
        for by in range(1, chips):
            term = jnp.where((at - by) % chips == chip, terms[by], term)
        total = term if total is None else total + term
    return total


def attention_kernel(
    live,
    query,
    dout,
    key,
    value,
    partner,
    far,
    pair_p,
    far_p,
    pair_q,
    far_q,
    attended_t,
    grad_query,
    up,
    middle,
    down,
    prob,
):
    wide, low = jnp.float32, jnp.bfloat16
    block_len = query.shape[0]
    first_head = lax.broadcasted_iota(jnp.int32, query.shape, 1) < HDIM

    def apart(array):
        zero = jnp.zeros_like(array)
        return jnp.concatenate(
            [jnp.where(first_head, array, zero), jnp.where(first_head, zero, array)], axis=0
        )

    def joined(array):
        return jnp.concatenate([array[:HDIM, :block_len], array[HDIM:, block_len:]], axis=0)

    def nine(own, at):
        return jnp.concatenate(
            [
                pair_p[0, at], pair_p[1, at], far_p[at],
                partner[at], own[...], far[at],
                pair_q[0, at], pair_q[1, at], far_q[at],
            ],
            axis=0,
        )

    def block(array, at):
        return array[at * block_len : (at + 1) * block_len]

    def dot(left, right, dims):
        return lax.dot_general(left, right, (dims, ((), ())), preferred_element_type=wide)

    query_cat = apart(query[...] * jnp.asarray(SCALE, low))
    dout_cat = apart(dout[...])
    keys, values = nine(key, 0), nine(value, 1)

    scores = dot(keys, query_cat, ((1,), (1,)))
    row_max = None
    for at in range(9):
        part = block(scores, at) + jnp.where(live[at] > 0, 0.0, DEAD)
        prob[at * block_len : (at + 1) * block_len, :] = part
        row_max = part if row_max is None else jnp.maximum(row_max, part)
    row_max = jnp.max(row_max, axis=0, keepdims=True)
    total = None
    for at in range(9):
        part = jnp.exp(prob[at * block_len : (at + 1) * block_len, :] - row_max)
        prob[at * block_len : (at + 1) * block_len, :] = part
        total = part if total is None else total + part
    norm = 1.0 / jnp.sum(total, axis=0, keepdims=True)
    low_parts = []
    for at in range(9):
        part = prob[at * block_len : (at + 1) * block_len, :] * norm
        prob[at * block_len : (at + 1) * block_len, :] = part
        low_parts.append(part.astype(low))
    prob_low = jnp.concatenate(low_parts, axis=0)
    attended = joined(dot(values.T, prob_low, ((1,), (0,)))).astype(low)
    attended_t[...] = attended

    product = dout[...].T.astype(wide) * attended.astype(wide)
    row_delta = jnp.concatenate(
        [
            jnp.sum(product[:HDIM], axis=0, keepdims=True),
            jnp.sum(product[HDIM:], axis=0, keepdims=True),
        ],
        axis=1,
    )
    grad_prob = dot(values, dout_cat, ((1,), (1,)))
    grad_score = jnp.concatenate(
        [
            (
                prob[at * block_len : (at + 1) * block_len, :] * (block(grad_prob, at) - row_delta)
            ).astype(low)
            for at in range(9)
        ],
        axis=0,
    )
    grad_query[...] = (joined(dot(keys.T, grad_score, ((1,), (0,)))) * SCALE).T.astype(low)
    grad_keys = dot(grad_score, query_cat, ((1,), (0,)))
    grad_values = dot(prob_low, dout_cat, ((1,), (0,)))
    for row, out in enumerate((up, middle, down)):
        for column in range(3):
            out[column, 0] = block(grad_keys, row * 3 + column).astype(out.dtype)
            out[column, 1] = block(grad_values, row * 3 + column).astype(out.dtype)


def attention(live, query, dout, near):
    block_len, width = query.shape
    low, wide = query.dtype, jnp.float32
    one = pl.BlockSpec((block_len, LANES), lambda p: (0, p))
    two = pl.BlockSpec((2, block_len, LANES), lambda p: (0, 0, p))
    four = pl.BlockSpec((2, 2, block_len, LANES), lambda p: (0, 0, 0, p))
    pairs = pl.BlockSpec((3, 2, block_len, LANES), lambda p: (0, 0, 0, p))
    shape = jax.ShapeDtypeStruct
    return pl.pallas_call(
        attention_kernel,
        grid=(width // LANES,),
        in_specs=[pl.BlockSpec(memory_space=pltpu.SMEM), one, one, one, one, two, two, four, two, four, two],
        out_specs=[pl.BlockSpec((LANES, block_len), lambda p: (p, 0)), one, pairs, pairs, pairs],
        out_shape=[
            shape((width, block_len), low),
            shape((block_len, width), low),
            shape((3, 2, block_len, width), low),
            shape((3, 2, block_len, width), wide),
            shape((3, 2, block_len, width), low),
        ],
        scratch_shapes=[pltpu.VMEM((9 * block_len, 2 * block_len), wide)],
        compiler_params=pltpu.CompilerParams(
            dimension_semantics=("arbitrary",), vmem_limit_bytes=40 << 20
        ),
        cost_estimate=pl.CostEstimate(
            flops=12 * 9 * block_len * block_len * width * 2,
            bytes_accessed=8 << 20,
            transcendentals=9 * block_len * block_len * (width // HDIM),
        ),
    )(live, query, dout, *near)


def shards(queries, keys, values, grad_out, w_out, pattern):
    low, wide = jnp.bfloat16, jnp.float32
    query, key, value, grad = queries[0, 0, 0], keys[0, 0, 0], values[0, 0, 0], grad_out[0, 0, 0]
    block_len, att_width = query.shape
    model_width = grad.shape[1]
    lat_count, opt_count = lax.axis_size("lat"), lax.axis_size("opt")
    at_lat, at_lon = lax.axis_index("lat"), lax.axis_index("lon")

    dout = lax.dot_general(
        grad, w_out, (((1,), (1,)), ((), ())), preferred_element_type=wide
    ).astype(low)
    flags = lax.dynamic_slice(pattern, (at_lat, at_lon, 0), (1, 1, 9)).reshape(9)
    at = jnp.arange(9)
    lat_step = (1 - 2 * (at_lat % 2)) * (1 - at // 3)
    lon_step = (1 - 2 * (at_lon % 2)) * (1 - at % 3)
    direction = (lat_step + 1) * 3 + lon_step + 1
    flags = jnp.sum(jnp.where(direction[:, None] == at[None, :], flags[None, :], 0), axis=1)
    key_rows = at_lat + lat_step
    live = ((flags > 0) & (key_rows >= 0) & (key_rows < lat_count)).astype(jnp.int32)

    own = jnp.stack((key, value))
    far, partner = far_of(own), partner_of(own)
    pair_p, pair_q = lat_mates_of(jnp.stack((partner, own)))
    far_p, far_q = lat_mates_of(far)
    grads_of_samples = to_all(grad, "opt")
    attended_t, grad_query, to_p, middle, to_q = attention(
        live, query, dout, (key, value, partner, far, pair_p, far_p, pair_q, far_q)
    )
    attended_t, grads_of_samples = lax.optimization_barrier((attended_t, grads_of_samples))

    attended_of_samples = lax.all_to_all(
        attended_t.reshape(opt_count, att_width // opt_count, block_len), "opt", 0, 0
    )
    w_part = jnp.einsum(
        "srt,stc->rc", attended_of_samples, grads_of_samples, preferred_element_type=wide
    ).astype(low)
    from_p, from_q = exchange(to_p, "lat", next_door), exchange(to_q, "lat", other_door)
    from_p, from_q, w_part = lax.optimization_barrier((from_p, from_q, w_part))
    sums = middle + from_p.astype(wide) + from_q.astype(wide)
    from_far = far_of(sums[2].astype(low))
    from_partner = partner_of(sums[0].astype(low))

    w_rows = w_part.shape[0] // lat_count
    w_part = lax.all_to_all(w_part.reshape(lat_count, w_rows, model_width), "lat", 0, 0)
    w_part = sum_over_lon(jnp.sum(w_part.astype(wide), axis=0)).astype(low)
    grad_weight = to_all(w_part, "lat").reshape(lat_count * w_rows, model_width).astype(wide)

    owned = (sums[1] + from_partner.astype(wide) + from_far.astype(wide)).astype(low)
    return (
        grad_query[None, None, None],
        owned[0][None, None, None],
        owned[1][None, None, None],
        grad_weight,
    )


def solution(mesh):
    blocks = P("opt", "lat", "lon", None, None)
    return jax.shard_map(
        shards,
        mesh=mesh,
        in_specs=(blocks, blocks, blocks, blocks, P(), P()),
        out_specs=(blocks, blocks, blocks, P("opt", None)),
        check_vma=False,
    )
```

time: 164 us -> 146 us (0.89)
  the two profiles are of different devices: /device:TPU:72 before, /device:TPU:1 now
where the time goes in v2:
time: 146 us; the launch traced here: 144 us
  starting transfers between devices  80 us (55%)
  waiting for transfers between devices  24.9 us (17%)
  blocking collectives  14.8 us (10%)
  Pallas kernels  8.82 us (6%)
  local copies, waits for them, and re-layouts  7.52 us (5%)
  other arithmetic  4.25 us (3%)
  matrix products  2.55 us (2%)
    ppermute x11, starting transfers between devices, exchange(): lax.ppermute(array, axis, [(i, j) for i, j in pairs if 0 <= j < lax.axis_...  37.8 us
    all_to_all x1, starting transfers between devices, shards(): lax.all_to_all(w_part.reshape(lat_count, w_rows, model_width), 'lat', 0, 0)  18.2 us
    all_to_all x2, starting transfers between devices, to_all(): lax.all_to_all(jnp.broadcast_to(array[None], (count,) + array.shape), axi...  14.8 us
    all_to_all x1, blocking collectives, shards(): lax.all_to_all(attended_t.reshape(opt_count, att_width // opt_count, bloc...  14.8 us
    ppermute x11, waiting for transfers between devices, exchange(): lax.ppermute(array, axis, [(i, j) for i, j in pairs if 0 <= j < lax.axis_...  13.8 us
    ppermute x2, starting transfers between devices, sum_over_lon(): lax.ppermute(part, 'lon', [(i, (i + 2 * by) % count) for i in range(count)])  9.18 us
    pallas_call x1, Pallas kernels, attention(): pl.pallas_call(attention_kernel, grid=(width // LANES,), in_specs=[pl.Blo...  8.82 us
    all_to_all x2, waiting for transfers between devices, to_all(): lax.all_to_all(jnp.broadcast_to(array[None], (count,) + array.shape), axi...  5.9 us
  transfers between devices with their start and end apart: 16, of which 6 were waited for; matrix products, arithmetic and copies ran while one was open for 7% of the time, Pallas kernels for 6%

profile of v2, /device:TPU:1, one launch (start us, length us, event | category | flops | bytes accessed | tf_op | source)
XLA Modules:
  0.0 143.8 jit_solution(5267892388098830951)
XLA Ops:
  0.6 2.6 %broadcast_in_dim.34 = bf16[8,128,1024]{2,1,0:T(8,128)(2,1)} broadcast(bf16[128,1024]{1,0:T(8,128)(2,1)} %bitcast.43), dimensions={1,2} | broadcast | bytes 2359296 | tf_op jit(solution)/shard_map/broadcast_in_dim | solution.py:42
  3.3 7.8 %all-to-all-start = ((bf16[8,128,1024]{2,1,0:T(8,128)(2,1)}), bf16[8,128,1024]{2,1,0:T(8,128)(2,1)}, u32[]{:S(2)}, u32[]{:S(2)}) async-start(bf16[8,128,1024]{2,1,0:T(8,128)(2,1)} %broadcast_in_dim.34), calls=%async_computation | async-start | bytes 4194304 | tf_op jit(solution)/shard_map/all_to_all | solution.py:42
  11.1 9.1 %collective-permute-start = (bf16[2,128,512]{2,1,0:T(8,128)(2,1)S(1)}, bf16[2,128,512]{2,1,0:T(8,128)(2,1)S(1)}, u32[]{:S(2)}, u32[]{:S(2)}) collective-permute-start(bf16[2,128,512]{2,1,0:T(8,128)(2,1)S(1)} %get-tuple-element.31), channel_id=1, source_target_pairs={{0,8},{8,0},{16,24},{24,16},{32,40},{40,32},{1,9},{9,1},{17,25},{2... | collective-permute-start | bytes 786440 | tf_op jit(solution)/shard_map/ppermute | solution.py:16
  20.3 4.3 %collective-permute-start.1 = (bf16[2,128,512]{2,1,0:T(8,128)(2,1)S(1)}, bf16[2,128,512]{2,1,0:T(8,128)(2,1)S(1)}, u32[]{:S(2)}, u32[]{:S(2)}) collective-permute-start(bf16[2,128,512]{2,1,0:T(8,128)(2,1)S(1)} %get-tuple-element.31), channel_id=1, source_target_pairs={{0,40},{8,16},{16,8},{24,32},{32,24},{40,0},{1,41},{9,17},{17,9},{... | collective-permute-start | bytes 786440 | tf_op jit(solution)/shard_map/ppermute | solution.py:16
  25.8 3.1 %collective-permute-start.2 = (bf16[2,2,128,512]{3,2,1,0:T(8,128)(2,1)S(1)}, bf16[2,2,128,512]{3,2,1,0:T(8,128)(2,1)S(1)}, u32[]{:S(2)}, u32[]{:S(2)}) collective-permute-start(bf16[2,2,128,512]{3,2,1,0:T(8,128)(2,1)S(1)} %pad_maximum_fusion), channel_id=1, source_target_pairs={{0,48},{48,0},{96,144},{144,96},{192,240},{240,192},{288,336},{336... | collective-permute-start | bytes 1572872 | tf_op jit(solution)/shard_map/ppermute | solution.py:16
  29.8 8.6 %collective-permute-done.1.far = bf16[2,128,512]{2,1,0:T(8,128)(2,1)S(1)} collective-permute-done((bf16[2,128,512]{2,1,0:T(8,128)(2,1)S(1)}, bf16[2,128,512]{2,1,0:T(8,128)(2,1)S(1)}, u32[]{:S(2)}, u32[]{:S(2)}) %collective-permute-start.1) | collective-permute-done | bytes 262176 | tf_op jit(solution)/shard_map/ppermute | solution.py:16
  38.3 1.9 %collective-permute-start.3 = (bf16[2,128,512]{2,1,0:T(8,128)(2,1)S(1)}, bf16[2,128,512]{2,1,0:T(8,128)(2,1)S(1)}, u32[]{:S(2)}, u32[]{:S(2)}) collective-permute-start(bf16[2,128,512]{2,1,0:T(8,128)(2,1)S(1)} %collective-permute-done.1.far), channel_id=1, source_target_pairs={{0,48},{48,0},{96,144},{144,96},{192,240},{240,192},{288,336},{336... | collective-permute-start | bytes 786440 | tf_op jit(solution)/shard_map/ppermute | solution.py:16
  41.5 4.4 %collective-permute-done.3.far_p = bf16[2,128,512]{2,1,0:T(8,128)(2,1)S(1)} collective-permute-done((bf16[2,128,512]{2,1,0:T(8,128)(2,1)S(1)}, bf16[2,128,512]{2,1,0:T(8,128)(2,1)S(1)}, u32[]{:S(2)}, u32[]{:S(2)}) %collective-permute-start.3) | collective-permute-done | bytes 262176 | tf_op jit(solution)/shard_map/ppermute | solution.py:16
  46.7 8.8 %shard_map.93 = (bf16[512,128]{1,0:T(8,128)(2,1)S(1)}, bf16[128,512]{1,0:T(8,128)(2,1)}, bf16[3,2,128,512]{3,2,1,0:T(8,128)(2,1)}, f32[3,2,128,512]{3,2,1,0:T(8,128)S(1)}, bf16[3,2,128,512]{3,2,1,0:T(8,128)(2,1)}) custom-call(s32[9]{0:T(128)S(1)} %and_convert_fusion.live, bf16[128,512]{1,0:T(8,128)(2,1)S(1)} %bitcast.42, ...), custom_call_target="tpu_custom_call" | custom-call | flops 1811939328 | bytes 8388608 | tf_op jit(solution)/shard_map/pallas_call | solution.py:172
  55.6 5.3 %collective-permute-start.6 = (bf16[3,2,128,512]{3,2,1,0:T(8,128)(2,1)}, bf16[3,2,128,512]{3,2,1,0:T(8,128)(2,1)S(1)}, u32[]{:S(2)}, u32[]{:S(2)}) collective-permute-start(bf16[3,2,128,512]{3,2,1,0:T(8,128)(2,1)} %get-tuple-element.16), channel_id=1, source_target_pairs={{0,48},{48,0},{96,144},{144,96},{192,240},{240,192},{288,336},{336... | collective-permute-start | bytes 2359304 | tf_op jit(solution)/shard_map/ppermute | solution.py:16
  60.8 1.6 %collective-permute-start.7 = (bf16[3,2,128,512]{3,2,1,0:T(8,128)(2,1)}, bf16[3,2,128,512]{3,2,1,0:T(8,128)(2,1)}, u32[]{:S(2)}, u32[]{:S(2)}) collective-permute-start(bf16[3,2,128,512]{3,2,1,0:T(8,128)(2,1)} %get-tuple-element.17), channel_id=1, source_target_pairs={{48,96},{96,48},{144,192},{192,144},{240,288},{288,240},{336,384},... | collective-permute-start | bytes 2359304 | tf_op jit(solution)/shard_map/ppermute | solution.py:16
  62.4 14.8 %all_to_all.20 = bf16[8,64,128]{2,1,0:T(8,128)(2,1)S(1)} all-to-all(bf16[8,64,128]{2,1,0:T(8,128)(2,1)S(1)} %bitcast.37), channel_id=1, replica_groups=mesh['lat'=16,'lon'=6,'opt'=8] {'opt'}, dimensions={0} | all-to-all | bytes 262144 | tf_op jit(solution)/shard_map/all_to_all | solution.py:226
  77.2 2.1 %fusion = bf16[64,1024]{1,0:T(8,128)(2,1)S(1)} fusion(bf16[8,64,128]{2,1,0:T(8,128)(2,1)S(1)} %all_to_all.20, bf16[8,128,1024]{2,1,0:T(8,128)(2,1)} %all-to-all-done), kind=kOutput, calls=%fused_computation.2 | convolution fusion | flops 134283264 | bytes 2359296 | tf_op jit(solution)/shard_map/srt,stc->rc/dot_general | solution.py:229
  80.0 18.2 %all-to-all-start.2 = ((bf16[16,4,1024]{2,1,0:T(4,128)(2,1)}), bf16[16,4,1024]{2,1,0:T(4,128)(2,1)S(1)}, u32[]{:S(2)}, u32[]{:S(2)}) async-start(bf16[16,4,1024]{2,1,0:T(4,128)(2,1)} %reshape.48), calls=%async_computation.2 | async-start | bytes 262144 | tf_op jit(solution)/shard_map/all_to_all | solution.py:239
  98.2 2.7 %fusion.12 = (bf16[3,2,128,512]{3,2,1,0:T(8,128)(2,1)S(1)}, f32[3,2,128,512]{3,2,1,0:T(8,128)}) fusion(bf16[3,2,128,512]{3,2,1,0:T(8,128)(2,1)} %collective-permute-done.7, f32[3,2,128,512]{3,2,1,0:T(8,128)S(1)} %get-tuple-element.15, bf16[3,2,128,512]{3,2,1,0:T(8,128)(2,1)S(1)} %collective-permute-done.6), kind=kLoop, calls=%fused_computation.33 | loop fusion | flops 1966080 | bytes 5505024 | tf_op jit(solution)/shard_map/convert.2
  100.9 3.7 %collective-permute-start.8 = (bf16[2,128,512]{2,1,0:T(8,128)(2,1)S(1)}, bf16[2,128,512]{2,1,0:T(8,128)(2,1)S(1)}, u32[]{:S(2)}, u32[]{:S(2)}) collective-permute-start(bf16[2,128,512]{2,1,0:T(8,128)(2,1)S(1)} %get-tuple-element.26), channel_id=1, source_target_pairs={{0,8},{8,0},{16,24},{24,16},{32,40},{40,32},{1,9},{9,1},{17,25},{2... | collective-permute-start | bytes 786440 | tf_op jit(solution)/shard_map/ppermute | solution.py:16
  104.6 4.8 %collective-permute-start.9 = (bf16[2,128,512]{2,1,0:T(8,128)(2,1)S(1)}, bf16[2,128,512]{2,1,0:T(8,128)(2,1)S(1)}, u32[]{:S(2)}, u32[]{:S(2)}) collective-permute-start(bf16[2,128,512]{2,1,0:T(8,128)(2,1)S(1)} %get-tuple-element.27), channel_id=1, source_target_pairs={{0,40},{8,16},{16,8},{24,32},{32,24},{40,0},{1,41},{9,17},{17,9},{... | collective-permute-start | bytes 786440 | tf_op jit(solution)/shard_map/ppermute | solution.py:16
  109.5 2.7 %collective-permute-start.10 = (f32[4,1024]{1,0:T(4,128)S(1)}, f32[4,1024]{1,0:T(4,128)S(1)}, u32[]{:S(2)}, u32[]{:S(2)}) collective-permute-start(f32[4,1024]{1,0:T(4,128)S(1)} %convert_reduce_fusion), channel_id=1, source_target_pairs={{0,8},{8,0},{16,24},{24,16},{32,40},{40,32},{1,9},{9,1},{17,25},{2... | collective-permute-start | bytes 49160 | tf_op jit(solution)/shard_map/ppermute | solution.py:16
  113.0 4.3 %collective-permute-start.11 = (f32[4,1024]{1,0:T(4,128)S(1)}, f32[4,1024]{1,0:T(4,128)S(1)}, u32[]{:S(2)}, u32[]{:S(2)}) collective-permute-start(f32[4,1024]{1,0:T(4,128)S(1)} %add.104), channel_id=1, source_target_pairs={{0,32},{8,40},{16,0},{24,8},{32,16},{40,24},{1,33},{9,41},{17,1},{... | collective-permute-start | bytes 49160 | tf_op jit(solution)/shard_map/ppermute | solution.py:51
  117.3 4.9 %collective-permute-start.12 = (f32[4,1024]{1,0:T(4,128)S(1)}, f32[4,1024]{1,0:T(4,128)S(1)}, u32[]{:S(2)}, u32[]{:S(2)}) collective-permute-start(f32[4,1024]{1,0:T(4,128)S(1)} %add.104), channel_id=1, source_target_pairs={{0,16},{8,24},{16,32},{24,40},{32,0},{40,8},{1,17},{9,25},{17,33},... | collective-permute-start | bytes 49160 | tf_op jit(solution)/shard_map/ppermute | solution.py:51
  122.3 3.8 %collective-permute-done.11 = f32[4,1024]{1,0:T(4,128)S(1)} collective-permute-done((f32[4,1024]{1,0:T(4,128)S(1)}, f32[4,1024]{1,0:T(4,128)S(1)}, u32[]{:S(2)}, u32[]{:S(2)}) %collective-permute-start.11) | collective-permute-done | bytes 16416 | tf_op jit(solution)/shard_map/ppermute | solution.py:51
  126.1 1.4 collective-permute-done.12
  128.2 7.0 %all-to-all-start.3 = ((bf16[16,4,1024]{2,1,0:T(4,128)(2,1)}), bf16[16,4,1024]{2,1,0:T(4,128)(2,1)S(1)}, u32[]{:S(2)}, u32[]{:S(2)}) async-start(bf16[16,4,1024]{2,1,0:T(4,128)(2,1)} %broadcast_in_dim.35), calls=%async_computation.3 | async-start | bytes 262144 | tf_op jit(solution)/shard_map/all_to_all | solution.py:42
  137.1 5.9 %all-to-all-done.3 = bf16[16,4,1024]{2,1,0:T(4,128)(2,1)S(1)} async-done(((bf16[16,4,1024]{2,1,0:T(4,128)(2,1)}), bf16[16,4,1024]{2,1,0:T(4,128)(2,1)S(1)}, u32[]{:S(2)}, u32[]{:S(2)}) %all-to-all-start.3) | async-done | bytes 131104 | tf_op jit(solution)/shard_map/all_to_all | solution.py:42
  (39 shorter events, 9.1 us)
Async XLA Ops:
  0.6 40.3 %copy-start = (bf16[512,1024]{1,0:T(8,128)(2,1)S(1)}, bf16[512,1024]{1,0:T(8,128)(2,1)}, u32[]{:S(2)}) copy-start(bf16[512,1024]{1,0:T(8,128)(2,1)} %param.10) | copy-start | bytes 3145732
  3.3 7.8 %copy-start.1 = (bf16[1,1,1,128,512]{4,3,2,1,0:T(8,128)(2,1)S(1)}, bf16[1,1,1,128,512]{4,3,2,1,0:T(8,128)(2,1)}, u32[]{:S(2)}) copy-start(bf16[1,1,1,128,512]{4,3,2,1,0:T(8,128)(2,1)} %param.7) | copy-start | bytes 393220
  3.3 7.8 %copy-start.2 = (bf16[1,1,1,128,512]{4,3,2,1,0:T(8,128)(2,1)S(1)}, bf16[1,1,1,128,512]{4,3,2,1,0:T(8,128)(2,1)}, u32[]{:S(2)}) copy-start(bf16[1,1,1,128,512]{4,3,2,1,0:T(8,128)(2,1)} %param.8) | copy-start | bytes 393220
  3.3 59.1 %all-to-all-start = ((bf16[8,128,1024]{2,1,0:T(8,128)(2,1)}), bf16[8,128,1024]{2,1,0:T(8,128)(2,1)}, u32[]{:S(2)}, u32[]{:S(2)}) async-start(bf16[8,128,1024]{2,1,0:T(8,128)(2,1)} %broadcast_in_dim.34), calls=%async_computation | async-start | bytes 4194304 | tf_op jit(solution)/shard_map/all_to_all | solution.py:42
  11.0 29.9 %copy-start.4 = (bf16[1,1,1,128,1024]{4,3,2,1,0:T(8,128)(2,1)S(1)}, bf16[1,1,1,128,1024]{4,3,2,1,0:T(8,128)(2,1)}, u32[]{:S(2)}) copy-start(bf16[1,1,1,128,1024]{4,3,2,1,0:T(8,128)(2,1)} %param.9) | copy-start | bytes 786436
  11.1 14.6 %collective-permute-start = (bf16[2,128,512]{2,1,0:T(8,128)(2,1)S(1)}, bf16[2,128,512]{2,1,0:T(8,128)(2,1)S(1)}, u32[]{:S(2)}, u32[]{:S(2)}) collective-permute-start(bf16[2,128,512]{2,1,0:T(8,128)(2,1)S(1)} %get-tuple-element.31), channel_id=1, source_target_pairs={{0,8},{8,0},{16,24},{24,16},{32,40},{40,32},{1,9},{9,1},{17,25},{2... | collective-permute-start | bytes 786440 | tf_op jit(solution)/shard_map/ppermute | solution.py:16
  20.3 18.1 %collective-permute-start.1 = (bf16[2,128,512]{2,1,0:T(8,128)(2,1)S(1)}, bf16[2,128,512]{2,1,0:T(8,128)(2,1)S(1)}, u32[]{:S(2)}, u32[]{:S(2)}) collective-permute-start(bf16[2,128,512]{2,1,0:T(8,128)(2,1)S(1)} %get-tuple-element.31), channel_id=1, source_target_pairs={{0,40},{8,16},{16,8},{24,32},{32,24},{40,0},{1,41},{9,17},{17,9},{... | collective-permute-start | bytes 786440 | tf_op jit(solution)/shard_map/ppermute | solution.py:16
  25.8 20.1 %collective-permute-start.2 = (bf16[2,2,128,512]{3,2,1,0:T(8,128)(2,1)S(1)}, bf16[2,2,128,512]{3,2,1,0:T(8,128)(2,1)S(1)}, u32[]{:S(2)}, u32[]{:S(2)}) collective-permute-start(bf16[2,2,128,512]{3,2,1,0:T(8,128)(2,1)S(1)} %pad_maximum_fusion), channel_id=1, source_target_pairs={{0,48},{48,0},{96,144},{144,96},{192,240},{240,192},{288,336},{336... | collective-permute-start | bytes 1572872 | tf_op jit(solution)/shard_map/ppermute | solution.py:16
  28.9 17.0 %collective-permute-start.4 = (bf16[2,2,128,512]{3,2,1,0:T(8,128)(2,1)S(1)}, bf16[2,2,128,512]{3,2,1,0:T(8,128)(2,1)S(1)}, u32[]{:S(2)}, u32[]{:S(2)}) collective-permute-start(bf16[2,2,128,512]{3,2,1,0:T(8,128)(2,1)S(1)} %pad_maximum_fusion), channel_id=1, source_target_pairs={{48,96},{96,48},{144,192},{192,144},{240,288},{288,240},{336,384},... | collective-permute-start | bytes 1572872 | tf_op jit(solution)/shard_map/ppermute | solution.py:16
  38.3 7.5 %collective-permute-start.3 = (bf16[2,128,512]{2,1,0:T(8,128)(2,1)S(1)}, bf16[2,128,512]{2,1,0:T(8,128)(2,1)S(1)}, u32[]{:S(2)}, u32[]{:S(2)}) collective-permute-start(bf16[2,128,512]{2,1,0:T(8,128)(2,1)S(1)} %collective-permute-done.1.far), channel_id=1, source_target_pairs={{0,48},{48,0},{96,144},{144,96},{192,240},{240,192},{288,336},{336... | collective-permute-start | bytes 786440 | tf_op jit(solution)/shard_map/ppermute | solution.py:16
  40.2 5.6 %collective-permute-start.5 = (bf16[2,128,512]{2,1,0:T(8,128)(2,1)S(1)}, bf16[2,128,512]{2,1,0:T(8,128)(2,1)S(1)}, u32[]{:S(2)}, u32[]{:S(2)}) collective-permute-start(bf16[2,128,512]{2,1,0:T(8,128)(2,1)S(1)} %collective-permute-done.1.far), channel_id=1, source_target_pairs={{48,96},{96,48},{144,192},{192,144},{240,288},{288,240},{336,384},... | collective-permute-start | bytes 786440 | tf_op jit(solution)/shard_map/ppermute | solution.py:16
  45.8 0.9 copy-start.3
  55.6 23.7 %collective-permute-start.6 = (bf16[3,2,128,512]{3,2,1,0:T(8,128)(2,1)}, bf16[3,2,128,512]{3,2,1,0:T(8,128)(2,1)S(1)}, u32[]{:S(2)}, u32[]{:S(2)}) collective-permute-start(bf16[3,2,128,512]{3,2,1,0:T(8,128)(2,1)} %get-tuple-element.16), channel_id=1, source_target_pairs={{0,48},{48,0},{96,144},{144,96},{192,240},{240,192},{288,336},{336... | collective-permute-start | bytes 2359304 | tf_op jit(solution)/shard_map/ppermute | solution.py:16
  60.8 18.4 %collective-permute-start.7 = (bf16[3,2,128,512]{3,2,1,0:T(8,128)(2,1)}, bf16[3,2,128,512]{3,2,1,0:T(8,128)(2,1)}, u32[]{:S(2)}, u32[]{:S(2)}) collective-permute-start(bf16[3,2,128,512]{3,2,1,0:T(8,128)(2,1)} %get-tuple-element.17), channel_id=1, source_target_pairs={{48,96},{96,48},{144,192},{192,144},{240,288},{288,240},{336,384},... | collective-permute-start | bytes 2359304 | tf_op jit(solution)/shard_map/ppermute | solution.py:16
  80.0 29.4 %all-to-all-start.2 = ((bf16[16,4,1024]{2,1,0:T(4,128)(2,1)}), bf16[16,4,1024]{2,1,0:T(4,128)(2,1)S(1)}, u32[]{:S(2)}, u32[]{:S(2)}) async-start(bf16[16,4,1024]{2,1,0:T(4,128)(2,1)} %reshape.48), calls=%async_computation.2 | async-start | bytes 262144 | tf_op jit(solution)/shard_map/all_to_all | solution.py:239
  100.9 34.4 %collective-permute-start.8 = (bf16[2,128,512]{2,1,0:T(8,128)(2,1)S(1)}, bf16[2,128,512]{2,1,0:T(8,128)(2,1)S(1)}, u32[]{:S(2)}, u32[]{:S(2)}) collective-permute-start(bf16[2,128,512]{2,1,0:T(8,128)(2,1)S(1)} %get-tuple-element.26), channel_id=1, source_target_pairs={{0,8},{8,0},{16,24},{24,16},{32,40},{40,32},{1,9},{9,1},{17,25},{2... | collective-permute-start | bytes 786440 | tf_op jit(solution)/shard_map/ppermute | solution.py:16
  104.6 30.7 %collective-permute-start.9 = (bf16[2,128,512]{2,1,0:T(8,128)(2,1)S(1)}, bf16[2,128,512]{2,1,0:T(8,128)(2,1)S(1)}, u32[]{:S(2)}, u32[]{:S(2)}) collective-permute-start(bf16[2,128,512]{2,1,0:T(8,128)(2,1)S(1)} %get-tuple-element.27), channel_id=1, source_target_pairs={{0,40},{8,16},{16,8},{24,32},{32,24},{40,0},{1,41},{9,17},{17,9},{... | collective-permute-start | bytes 786440 | tf_op jit(solution)/shard_map/ppermute | solution.py:16
  109.5 3.5 %collective-permute-start.10 = (f32[4,1024]{1,0:T(4,128)S(1)}, f32[4,1024]{1,0:T(4,128)S(1)}, u32[]{:S(2)}, u32[]{:S(2)}) collective-permute-start(f32[4,1024]{1,0:T(4,128)S(1)} %convert_reduce_fusion), channel_id=1, source_target_pairs={{0,8},{8,0},{16,24},{24,16},{32,40},{40,32},{1,9},{9,1},{17,25},{2... | collective-permute-start | bytes 49160 | tf_op jit(solution)/shard_map/ppermute | solution.py:16
  113.0 13.1 %collective-permute-start.11 = (f32[4,1024]{1,0:T(4,128)S(1)}, f32[4,1024]{1,0:T(4,128)S(1)}, u32[]{:S(2)}, u32[]{:S(2)}) collective-permute-start(f32[4,1024]{1,0:T(4,128)S(1)} %add.104), channel_id=1, source_target_pairs={{0,32},{8,40},{16,0},{24,8},{32,16},{40,24},{1,33},{9,41},{17,1},{... | collective-permute-start | bytes 49160 | tf_op jit(solution)/shard_map/ppermute | solution.py:51
  117.3 10.2 %collective-permute-start.12 = (f32[4,1024]{1,0:T(4,128)S(1)}, f32[4,1024]{1,0:T(4,128)S(1)}, u32[]{:S(2)}, u32[]{:S(2)}) collective-permute-start(f32[4,1024]{1,0:T(4,128)S(1)} %add.104), channel_id=1, source_target_pairs={{0,16},{8,24},{16,32},{24,40},{32,0},{40,8},{1,17},{9,25},{17,33},... | collective-permute-start | bytes 49160 | tf_op jit(solution)/shard_map/ppermute | solution.py:51
  128.2 14.8 %all-to-all-start.3 = ((bf16[16,4,1024]{2,1,0:T(4,128)(2,1)}), bf16[16,4,1024]{2,1,0:T(4,128)(2,1)S(1)}, u32[]{:S(2)}, u32[]{:S(2)}) async-start(bf16[16,4,1024]{2,1,0:T(4,128)(2,1)} %broadcast_in_dim.35), calls=%async_computation.3 | async-start | bytes 262144 | tf_op jit(solution)/shard_map/all_to_all | solution.py:42

commit v3 on v2

--- a/solution.py
+++ b/solution.py
@@ -9,6 +9,7 @@
 SCALE = HDIM ** (-0.5)
 DEAD = -1e30
 LANES = 2 * HDIM
+PART_ROWS = 8
 
 
 def exchange(array, axis, mate):
@@ -40,30 +41,13 @@
 def to_all(array, axis):
     count = lax.axis_size(axis)
     return lax.all_to_all(jnp.broadcast_to(array[None], (count,) + array.shape), axis, 0, 0)
-
-
-def sum_over_lon(part):
-    count = lax.axis_size("lon")
-    chips = count // 2
-    part = part + partner_of(part)
-    at = lax.axis_index("lon") // 2
-    terms = [part] + [
-        lax.ppermute(part, "lon", [(i, (i + 2 * by) % count) for i in range(count)])
-        for by in range(1, chips)
-    ]
-    total = None
-    for chip in range(chips):
-        term = terms[0]
-        for by in range(1, chips):
-            term = jnp.where((at - by) % chips == chip, terms[by], term)
-        total = term if total is None else total + term
-    return total
 
 
 def attention_kernel(
     live,
     query,
     dout,
+    grad,
     key,
     value,
     partner,
@@ -72,7 +56,7 @@
     far_p,
     pair_q,
     far_q,
-    attended_t,
+    w_parts,
     grad_query,
     up,
     middle,
@@ -132,7 +116,12 @@
         low_parts.append(part.astype(low))
     prob_low = jnp.concatenate(low_parts, axis=0)
     attended = joined(dot(values.T, prob_low, ((1,), (0,)))).astype(low)
-    attended_t[...] = attended
+    w_rows = dot(attended, grad[...], ((1,), (0,)))
+    width = w_parts.shape[2]
+    across = w_rows.shape[1] // width
+    for at in range(w_parts.shape[0]):
+        row, column = at // across * PART_ROWS, at % across * width
+        w_parts[at] = w_rows[row : row + PART_ROWS, column : column + width].astype(low)
 
     product = dout[...].T.astype(wide) * attended.astype(wide)
     row_delta = jnp.concatenate(
@@ -161,9 +150,12 @@
             out[column, 1] = block(grad_values, row * 3 + column).astype(out.dtype)
 
 
-def attention(live, query, dout, near):
+def attention(live, query, dout, grad, near, parts):
     block_len, width = query.shape
     low, wide = query.dtype, jnp.float32
+    model_width = grad.shape[1]
+    steps = width // LANES
+    part_width = width * model_width // parts // PART_ROWS
     one = pl.BlockSpec((block_len, LANES), lambda p: (0, p))
     two = pl.BlockSpec((2, block_len, LANES), lambda p: (0, 0, p))
     four = pl.BlockSpec((2, 2, block_len, LANES), lambda p: (0, 0, 0, p))
@@ -171,11 +163,19 @@
     shape = jax.ShapeDtypeStruct
     return pl.pallas_call(
         attention_kernel,
-        grid=(width // LANES,),
-        in_specs=[pl.BlockSpec(memory_space=pltpu.SMEM), one, one, one, one, two, two, four, two, four, two],
-        out_specs=[pl.BlockSpec((LANES, block_len), lambda p: (p, 0)), one, pairs, pairs, pairs],
+        grid=(steps,),
+        in_specs=[pl.BlockSpec(memory_space=pltpu.SMEM), one, one]
+        + [pl.BlockSpec((block_len, model_width), lambda p: (0, 0))]
+        + [one, one, two, two, four, two, four, two],
+        out_specs=[
+            pl.BlockSpec((parts // steps, PART_ROWS, part_width), lambda p: (p, 0, 0)),
+            one,
+            pairs,
+            pairs,
+            pairs,
+        ],
         out_shape=[
-            shape((width, block_len), low),
+            shape((parts, PART_ROWS, part_width), low),
             shape((block_len, width), low),
             shape((3, 2, block_len, width), low),
             shape((3, 2, block_len, width), wide),
@@ -190,7 +190,7 @@
             bytes_accessed=8 << 20,
             transcendentals=9 * block_len * block_len * (width // HDIM),
         ),
-    )(live, query, dout, *near)
+    )(live, query, dout, grad, *near)
 
 
 def shards(queries, keys, values, grad_out, w_out, pattern):
@@ -217,29 +217,21 @@
     far, partner = far_of(own), partner_of(own)
     pair_p, pair_q = lat_mates_of(jnp.stack((partner, own)))
     far_p, far_q = lat_mates_of(far)
-    grads_of_samples = to_all(grad, "opt")
-    attended_t, grad_query, to_p, middle, to_q = attention(
-        live, query, dout, (key, value, partner, far, pair_p, far_p, pair_q, far_q)
-    )
-    attended_t, grads_of_samples = lax.optimization_barrier((attended_t, grads_of_samples))
-
-    attended_of_samples = lax.all_to_all(
-        attended_t.reshape(opt_count, att_width // opt_count, block_len), "opt", 0, 0
-    )
-    w_part = jnp.einsum(
-        "srt,stc->rc", attended_of_samples, grads_of_samples, preferred_element_type=wide
-    ).astype(low)
+    parts = opt_count * lat_count
+    w_parts, grad_query, to_p, middle, to_q = attention(
+        live, query, dout, grad, (key, value, partner, far, pair_p, far_p, pair_q, far_q), parts
+    )
+
+    w_part = jnp.sum(lax.all_to_all(w_parts, ("opt", "lat"), 0, 0).astype(wide), axis=0)
+    w_part = jnp.sum(to_all(w_part, "lon"), axis=0).astype(low)
+    across = model_width // w_part.shape[1]
+    grad_weight = to_all(w_part, "lat").reshape(lat_count // across, across, PART_ROWS, -1)
+    grad_weight = grad_weight.swapaxes(1, 2).reshape(att_width // opt_count, model_width).astype(wide)
+
     from_p, from_q = exchange(to_p, "lat", next_door), exchange(to_q, "lat", other_door)
-    from_p, from_q, w_part = lax.optimization_barrier((from_p, from_q, w_part))
     sums = middle + from_p.astype(wide) + from_q.astype(wide)
     from_far = far_of(sums[2].astype(low))
     from_partner = partner_of(sums[0].astype(low))
-
-    w_rows = w_part.shape[0] // lat_count
-    w_part = lax.all_to_all(w_part.reshape(lat_count, w_rows, model_width), "lat", 0, 0)
-    w_part = sum_over_lon(jnp.sum(w_part.astype(wide), axis=0)).astype(low)
-    grad_weight = to_all(w_part, "lat").reshape(lat_count * w_rows, model_width).astype(wide)
-
     owned = (sums[1] + from_partner.astype(wide) + from_far.astype(wide)).astype(low)
     return (
         grad_query[None, None, None],

time: 146 us -> 152 us (1.041); the launches traced: 144 us -> 152 us
  waiting for transfers between devices: 24.9 us -> 44.4 us
  starting transfers between devices: 80 us -> 65.7 us
  blocking collectives: 14.8 us -> 18.2 us
  matrix products: 2.55 us -> 0.48 us
  other arithmetic: 4.25 us -> 6.28 us
    ppermute x11 -> x10, waiting for transfers between devices: 13.8 us -> 38.5 us  [exchange(): lax.ppermute(array, axis, [(i, j) for i, j in pairs if 0 <= j < lax.axis_...]
    ppermute x2 -> x0, starting transfers between devices: 9.18 us -> none  [sum_over_lon(): lax.ppermute(part, 'lon', [(i, (i + 2 * by) % count) for i in range(count)])]
    all_to_all x2 -> x1, starting transfers between devices: 14.8 us -> 7.91 us  [to_all(): lax.all_to_all(jnp.broadcast_to(array[None], (count,) + array.shape), axi...]
    ppermute x2 -> x0, waiting for transfers between devices: 5.24 us -> none  [sum_over_lon(): lax.ppermute(part, 'lon', [(i, (i + 2 * by) % count) for i in range(count)])]
    all_to_all x1, blocking collectives: 14.8 us -> 18.2 us  [to_all(): lax.all_to_all(jnp.broadcast_to(array[None], (count,) + array.shape), axi...]
    all_to_all x1, starting transfers between devices: 18.2 us -> 21.3 us  [shards(): lax.all_to_all(w_parts, ('opt', 'lat'), 0, 0).astype(wide)]
    unnamed x10 -> x22, local copies, waits for them, and re-layouts: 0.92 us -> 3.77 us
    broadcast_in_dim x2, local copies, waits for them, and re-layouts: 3.3 us -> 0.68 us  [to_all(): jnp.broadcast_to(array[None], (count,) + array.shape)]
  transfers between devices with their start and end apart: 16 -> 12, of which waited for: 6 -> 4; matrix products, arithmetic and copies ran while one was open for 7% -> 5% of each run, Pallas kernels for 6% -> 0%
where the time goes in v3:
time: 152 us
  starting transfers between devices  65.7 us (43%)
  waiting for transfers between devices  44.4 us (29%)
  blocking collectives  18.2 us (12%)
  Pallas kernels  9.15 us (6%)
  local copies, waits for them, and re-layouts  6.31 us (4%)
  other arithmetic  6.28 us (4%)
    ppermute x10, waiting for transfers between devices, exchange(): lax.ppermute(array, axis, [(i, j) for i, j in pairs if 0 <= j < lax.axis_...  38.5 us
    ppermute x10, starting transfers between devices, exchange(): lax.ppermute(array, axis, [(i, j) for i, j in pairs if 0 <= j < lax.axis_...  36.5 us
    all_to_all x1, starting transfers between devices, shards(): lax.all_to_all(w_parts, ('opt', 'lat'), 0, 0).astype(wide)  21.3 us
    all_to_all x1, blocking collectives, to_all(): lax.all_to_all(jnp.broadcast_to(array[None], (count,) + array.shape), axi...  18.2 us
    pallas_call x1, Pallas kernels, attention(): pl.pallas_call(attention_kernel, grid=(steps,), in_specs=[pl.BlockSpec(me...  9.15 us
    all_to_all x1, starting transfers between devices, to_all(): lax.all_to_all(jnp.broadcast_to(array[None], (count,) + array.shape), axi...  7.91 us
    all_to_all x1, waiting for transfers between devices, to_all(): lax.all_to_all(jnp.broadcast_to(array[None], (count,) + array.shape), axi...  5.89 us
    unnamed x22, local copies, waits for them, and re-layouts  3.77 us
  transfers between devices with their start and end apart: 12, of which 4 were waited for; matrix products, arithmetic and copies ran while one was open for 5% of the time, Pallas kernels for 0%

profile of v3, /device:TPU:1, one launch (start us, length us, event | category | flops | bytes accessed | tf_op | source)
XLA Modules:
  0.0 151.5 jit_solution(1872880016970226869)
XLA Ops:
  0.7 1.1 fusion.10
  1.8 12.4 %collective-permute-start = (bf16[2,128,512]{2,1,0:T(8,128)(2,1)S(1)}, bf16[2,128,512]{2,1,0:T(8,128)(2,1)S(1)}, u32[]{:S(2)}, u32[]{:S(2)}) collective-permute-start(bf16[2,128,512]{2,1,0:T(8,128)(2,1)S(1)} %get-tuple-element.21), channel_id=1, source_target_pairs={{0,8},{8,0},{16,24},{24,16},{32,40},{40,32},{1,9},{9,1},{17,25},{2... | collective-permute-start | bytes 786440 | tf_op jit(solution)/shard_map/ppermute | solution.py:17
  14.2 1.9 %collective-permute-start.1 = (bf16[2,128,512]{2,1,0:T(8,128)(2,1)S(1)}, bf16[2,128,512]{2,1,0:T(8,128)(2,1)S(1)}, u32[]{:S(2)}, u32[]{:S(2)}) collective-permute-start(bf16[2,128,512]{2,1,0:T(8,128)(2,1)S(1)} %get-tuple-element.21), channel_id=1, source_target_pairs={{0,40},{8,16},{16,8},{24,32},{32,24},{40,0},{1,41},{9,17},{17,9},{... | collective-permute-start | bytes 786440 | tf_op jit(solution)/shard_map/ppermute | solution.py:17
  16.2 1.1 dynamic-slice_reduce_fusion
  18.1 5.1 %collective-permute-start.2 = (bf16[2,2,128,512]{3,2,1,0:T(8,128)(2,1)S(1)}, bf16[2,2,128,512]{3,2,1,0:T(8,128)(2,1)S(1)}, u32[]{:S(2)}, u32[]{:S(2)}) collective-permute-start(bf16[2,2,128,512]{3,2,1,0:T(8,128)(2,1)S(1)} %pad_maximum_fusion), channel_id=1, source_target_pairs={{0,48},{48,0},{96,144},{144,96},{192,240},{240,192},{288,336},{336... | collective-permute-start | bytes 1572872 | tf_op jit(solution)/shard_map/ppermute | solution.py:17
  23.4 6.0 %collective-permute-done.1.far = bf16[2,128,512]{2,1,0:T(8,128)(2,1)S(1)} collective-permute-done((bf16[2,128,512]{2,1,0:T(8,128)(2,1)S(1)}, bf16[2,128,512]{2,1,0:T(8,128)(2,1)S(1)}, u32[]{:S(2)}, u32[]{:S(2)}) %collective-permute-start.1) | collective-permute-done | bytes 262176 | tf_op jit(solution)/shard_map/ppermute | solution.py:17
  30.1 1.9 %collective-permute-start.3 = (bf16[2,128,512]{2,1,0:T(8,128)(2,1)S(1)}, bf16[2,128,512]{2,1,0:T(8,128)(2,1)S(1)}, u32[]{:S(2)}, u32[]{:S(2)}) collective-permute-start(bf16[2,128,512]{2,1,0:T(8,128)(2,1)S(1)} %collective-permute-done.1.far), channel_id=1, source_target_pairs={{0,48},{48,0},{96,144},{144,96},{192,240},{240,192},{288,336},{336... | collective-permute-start | bytes 786440 | tf_op jit(solution)/shard_map/ppermute | solution.py:17
  32.5 5.7 %collective-permute-done.3.far_p = bf16[2,128,512]{2,1,0:T(8,128)(2,1)S(1)} collective-permute-done((bf16[2,128,512]{2,1,0:T(8,128)(2,1)S(1)}, bf16[2,128,512]{2,1,0:T(8,128)(2,1)S(1)}, u32[]{:S(2)}, u32[]{:S(2)}) %collective-permute-start.3) | collective-permute-done | bytes 262176 | tf_op jit(solution)/shard_map/ppermute | solution.py:17
  38.3 0.9 copy-done.9
  39.2 9.2 %shard_map.93 = (bf16[128,8,512]{2,1,0:T(8,128)(2,1)S(1)}, bf16[128,512]{1,0:T(8,128)(2,1)}, bf16[3,2,128,512]{3,2,1,0:T(8,128)(2,1)S(1)}, f32[3,2,128,512]{3,2,1,0:T(8,128)S(1)}, bf16[3,2,128,512]{3,2,1,0:T(8,128)(2,1)S(1)}) custom-call(s32[9]{0:T(128)S(1)} %and_convert_fusion.live, bf16[128,512]{1,0:T(8,128)(2,1)S(1)} %bitcast.40, ...), custom_call_target="tpu_custom_call" | custom-call | flops 1811939328 | bytes 8388608 | tf_op jit(solution)/shard_map/pallas_call | solution.py:164
  48.4 1.0 copy-done.1
  49.4 0.9 copy-done.5
  50.3 0.9 copy-done.7
  51.2 21.3 %all-to-all-start = ((bf16[128,8,512]{2,1,0:T(8,128)(2,1)}), bf16[128,8,512]{2,1,0:T(8,128)(2,1)}, u32[]{:S(2)}, u32[]{:S(2)}) async-start(bf16[128,8,512]{2,1,0:T(8,128)(2,1)} %copy-done.1), calls=%async_computation | async-start | bytes 2097152 | tf_op jit(solution)/shard_map/all_to_all | solution.py:225
  72.5 2.4 %collective-permute-start.6 = (bf16[3,2,128,512]{3,2,1,0:T(8,128)(2,1)}, bf16[3,2,128,512]{3,2,1,0:T(8,128)(2,1)S(1)}, u32[]{:S(2)}, u32[]{:S(2)}) collective-permute-start(bf16[3,2,128,512]{3,2,1,0:T(8,128)(2,1)} %copy-done.7), channel_id=1, source_target_pairs={{0,48},{48,0},{96,144},{144,96},{192,240},{240,192},{288,336},{336... | collective-permute-start | bytes 2359304 | tf_op jit(solution)/shard_map/ppermute | solution.py:17
  75.7 26.8 %collective-permute-done.6 = bf16[3,2,128,512]{3,2,1,0:T(8,128)(2,1)S(1)} collective-permute-done((bf16[3,2,128,512]{3,2,1,0:T(8,128)(2,1)}, bf16[3,2,128,512]{3,2,1,0:T(8,128)(2,1)S(1)}, u32[]{:S(2)}, u32[]{:S(2)}) %collective-permute-start.6) | collective-permute-done | bytes 786464 | tf_op jit(solution)/shard_map/ppermute | solution.py:17
  102.5 1.6 %fusion.11 = (bf16[3,2,128,512]{3,2,1,0:T(8,128)(2,1)S(1)}, f32[3,2,128,512]{3,2,1,0:T(8,128)}) fusion(bf16[3,2,128,512]{3,2,1,0:T(8,128)(2,1)S(1)} %collective-permute-done.7, f32[3,2,128,512]{3,2,1,0:T(8,128)S(1)} %get-tuple-element.10, bf16[3,2,128,512]{3,2,1,0:T(8,128)(2,1)S(1)} %collective-permute-done.6), kind=kLoop, calls=%fused_computation.30 | loop fusion | flops 1966080 | bytes 5505024 | tf_op jit(solution)/shard_map/convert.4
  104.1 3.6 %collective-permute-start.8 = (bf16[2,128,512]{2,1,0:T(8,128)(2,1)S(1)}, bf16[2,128,512]{2,1,0:T(8,128)(2,1)S(1)}, u32[]{:S(2)}, u32[]{:S(2)}) collective-permute-start(bf16[2,128,512]{2,1,0:T(8,128)(2,1)S(1)} %get-tuple-element.16), channel_id=1, source_target_pairs={{0,8},{8,0},{16,24},{24,16},{32,40},{40,32},{1,9},{9,1},{17,25},{2... | collective-permute-start | bytes 786440 | tf_op jit(solution)/shard_map/ppermute | solution.py:17
  107.8 7.0 %collective-permute-start.9 = (bf16[2,128,512]{2,1,0:T(8,128)(2,1)S(1)}, bf16[2,128,512]{2,1,0:T(8,128)(2,1)S(1)}, u32[]{:S(2)}, u32[]{:S(2)}) collective-permute-start(bf16[2,128,512]{2,1,0:T(8,128)(2,1)S(1)} %get-tuple-element.17), channel_id=1, source_target_pairs={{0,40},{8,16},{16,8},{24,32},{32,24},{40,0},{1,41},{9,17},{17,9},{... | collective-permute-start | bytes 786440 | tf_op jit(solution)/shard_map/ppermute | solution.py:17
  114.7 1.4 convert_reduce_fusion
  116.2 18.2 %all_to_all.15 = f32[6,8,512]{2,1,0:T(8,128)S(1)} all-to-all(f32[6,8,512]{2,1,0:T(8,128)S(1)} %broadcast_in_dim.35), channel_id=1, replica_groups=mesh['lat'=16,'lon'=6,'opt'=8] {'lon'}, dimensions={0} | all-to-all | bytes 196608 | tf_op jit(solution)/shard_map/all_to_all | solution.py:43
  135.1 7.9 %all-to-all-start.2 = ((bf16[16,8,512]{2,1,0:T(8,128)(2,1)}), bf16[16,8,512]{2,1,0:T(8,128)(2,1)S(1)}, u32[]{:S(2)}, u32[]{:S(2)}) async-start(bf16[16,8,512]{2,1,0:T(8,128)(2,1)} %broadcast_in_dim.36), calls=%async_computation.2 | async-start | bytes 262144 | tf_op jit(solution)/shard_map/all_to_all | solution.py:43
  143.0 1.1 fusion.2
  144.9 5.9 %all-to-all-done.2 = bf16[16,8,512]{2,1,0:T(8,128)(2,1)S(1)} async-done(((bf16[16,8,512]{2,1,0:T(8,128)(2,1)}), bf16[16,8,512]{2,1,0:T(8,128)(2,1)S(1)}, u32[]{:S(2)}, u32[]{:S(2)}) %all-to-all-start.2) | async-done | bytes 131104 | tf_op jit(solution)/shard_map/all_to_all | solution.py:43
  (40 shorter events, 5.1 us)
Async XLA Ops:
  0.6 31.4 %copy-start = (bf16[512,1024]{1,0:T(8,128)(2,1)S(1)}, bf16[512,1024]{1,0:T(8,128)(2,1)}, u32[]{:S(2)}) copy-start(bf16[512,1024]{1,0:T(8,128)(2,1)} %param.10) | copy-start | bytes 3145732
  0.6 31.4 %copy-start.2 = (bf16[1,1,1,128,1024]{4,3,2,1,0:T(8,128)(2,1)S(1)}, bf16[1,1,1,128,1024]{4,3,2,1,0:T(8,128)(2,1)}, u32[]{:S(2)}) copy-start(bf16[1,1,1,128,1024]{4,3,2,1,0:T(8,128)(2,1)} %param.9) | copy-start | bytes 786436
  0.7 37.6 %copy-start.3 = (bf16[1,1,1,128,512]{4,3,2,1,0:T(8,128)(2,1)S(1)}, bf16[1,1,1,128,512]{4,3,2,1,0:T(8,128)(2,1)}, u32[]{:S(2)}) copy-start(bf16[1,1,1,128,512]{4,3,2,1,0:T(8,128)(2,1)} %param.7) | copy-start | bytes 393220
  0.7 37.6 %copy-start.4 = (bf16[1,1,1,128,512]{4,3,2,1,0:T(8,128)(2,1)S(1)}, bf16[1,1,1,128,512]{4,3,2,1,0:T(8,128)(2,1)}, u32[]{:S(2)}) copy-start(bf16[1,1,1,128,512]{4,3,2,1,0:T(8,128)(2,1)} %param.8) | copy-start | bytes 393220
  0.7 37.6 %copy-start.10 = (bf16[1,1,1,128,512]{4,3,2,1,0:T(8,128)(2,1)S(1)}, bf16[1,1,1,128,512]{4,3,2,1,0:T(8,128)(2,1)}, u32[]{:S(2)}) copy-start(bf16[1,1,1,128,512]{4,3,2,1,0:T(8,128)(2,1)} %param.6) | copy-start | bytes 393220
  1.8 15.5 %collective-permute-start = (bf16[2,128,512]{2,1,0:T(8,128)(2,1)S(1)}, bf16[2,128,512]{2,1,0:T(8,128)(2,1)S(1)}, u32[]{:S(2)}, u32[]{:S(2)}) collective-permute-start(bf16[2,128,512]{2,1,0:T(8,128)(2,1)S(1)} %get-tuple-element.21), channel_id=1, source_target_pairs={{0,8},{8,0},{16,24},{24,16},{32,40},{40,32},{1,9},{9,1},{17,25},{2... | collective-permute-start | bytes 786440 | tf_op jit(solution)/shard_map/ppermute | solution.py:17
  14.2 15.2 %collective-permute-start.1 = (bf16[2,128,512]{2,1,0:T(8,128)(2,1)S(1)}, bf16[2,128,512]{2,1,0:T(8,128)(2,1)S(1)}, u32[]{:S(2)}, u32[]{:S(2)}) collective-permute-start(bf16[2,128,512]{2,1,0:T(8,128)(2,1)S(1)} %get-tuple-element.21), channel_id=1, source_target_pairs={{0,40},{8,16},{16,8},{24,32},{32,24},{40,0},{1,41},{9,17},{17,9},{... | collective-permute-start | bytes 786440 | tf_op jit(solution)/shard_map/ppermute | solution.py:17
  17.4 20.8 %collective-permute-start.4 = (bf16[2,2,128,512]{3,2,1,0:T(8,128)(2,1)S(1)}, bf16[2,2,128,512]{3,2,1,0:T(8,128)(2,1)S(1)}, u32[]{:S(2)}, u32[]{:S(2)}) collective-permute-start(bf16[2,2,128,512]{3,2,1,0:T(8,128)(2,1)S(1)} %pad_maximum_fusion), channel_id=1, source_target_pairs={{48,96},{96,48},{144,192},{192,144},{240,288},{288,240},{336,384},... | collective-permute-start | bytes 1572872 | tf_op jit(solution)/shard_map/ppermute | solution.py:17
  18.1 20.1 %collective-permute-start.2 = (bf16[2,2,128,512]{3,2,1,0:T(8,128)(2,1)S(1)}, bf16[2,2,128,512]{3,2,1,0:T(8,128)(2,1)S(1)}, u32[]{:S(2)}, u32[]{:S(2)}) collective-permute-start(bf16[2,2,128,512]{3,2,1,0:T(8,128)(2,1)S(1)} %pad_maximum_fusion), channel_id=1, source_target_pairs={{0,48},{48,0},{96,144},{144,96},{192,240},{240,192},{288,336},{336... | collective-permute-start | bytes 1572872 | tf_op jit(solution)/shard_map/ppermute | solution.py:17
  29.4 8.8 %copy-start.8 = (bf16[2,128,512]{2,1,0:T(8,128)(2,1)}, bf16[2,128,512]{2,1,0:T(8,128)(2,1)S(1)}, u32[]{:S(2)}) copy-start(bf16[2,128,512]{2,1,0:T(8,128)(2,1)S(1)} %collective-permute-done.1.far) | copy-start | bytes 786436
  29.4 3.1 %collective-permute-start.5 = (bf16[2,128,512]{2,1,0:T(8,128)(2,1)S(1)}, bf16[2,128,512]{2,1,0:T(8,128)(2,1)S(1)}, u32[]{:S(2)}, u32[]{:S(2)}) collective-permute-start(bf16[2,128,512]{2,1,0:T(8,128)(2,1)S(1)} %collective-permute-done.1.far), channel_id=1, source_target_pairs={{48,96},{96,48},{144,192},{192,144},{240,288},{288,240},{336,384},... | collective-permute-start | bytes 786440 | tf_op jit(solution)/shard_map/ppermute | solution.py:17
  30.1 8.2 %collective-permute-start.3 = (bf16[2,128,512]{2,1,0:T(8,128)(2,1)S(1)}, bf16[2,128,512]{2,1,0:T(8,128)(2,1)S(1)}, u32[]{:S(2)}, u32[]{:S(2)}) collective-permute-start(bf16[2,128,512]{2,1,0:T(8,128)(2,1)S(1)} %collective-permute-done.1.far), channel_id=1, source_target_pairs={{0,48},{48,0},{96,144},{144,96},{192,240},{240,192},{288,336},{336... | collective-permute-start | bytes 786440 | tf_op jit(solution)/shard_map/ppermute | solution.py:17
  38.3 1.0 copy-start.9
  48.4 1.0 copy-start.1
  49.4 0.9 copy-start.5
  50.3 0.9 copy-start.7
  51.2 23.8 %copy-start.6 = (bf16[3,2,128,512]{3,2,1,0:T(8,128)(2,1)S(1)}, bf16[3,2,128,512]{3,2,1,0:T(8,128)(2,1)}, u32[]{:S(2)}) copy-start(bf16[3,2,128,512]{3,2,1,0:T(8,128)(2,1)} %copy-done.5) | copy-start | bytes 2359300
  51.2 63.5 %all-to-all-start = ((bf16[128,8,512]{2,1,0:T(8,128)(2,1)}), bf16[128,8,512]{2,1,0:T(8,128)(2,1)}, u32[]{:S(2)}, u32[]{:S(2)}) async-start(bf16[128,8,512]{2,1,0:T(8,128)(2,1)} %copy-done.1), calls=%async_computation | async-start | bytes 2097152 | tf_op jit(solution)/shard_map/all_to_all | solution.py:225
  72.5 30.0 %collective-permute-start.6 = (bf16[3,2,128,512]{3,2,1,0:T(8,128)(2,1)}, bf16[3,2,128,512]{3,2,1,0:T(8,128)(2,1)S(1)}, u32[]{:S(2)}, u32[]{:S(2)}) collective-permute-start(bf16[3,2,128,512]{3,2,1,0:T(8,128)(2,1)} %copy-done.7), channel_id=1, source_target_pairs={{0,48},{48,0},{96,144},{144,96},{192,240},{240,192},{288,336},{336... | collective-permute-start | bytes 2359304 | tf_op jit(solution)/shard_map/ppermute | solution.py:17
  75.0 27.6 %collective-permute-start.7 = (bf16[3,2,128,512]{3,2,1,0:T(8,128)(2,1)S(1)}, bf16[3,2,128,512]{3,2,1,0:T(8,128)(2,1)S(1)}, u32[]{:S(2)}, u32[]{:S(2)}) collective-permute-start(bf16[3,2,128,512]{3,2,1,0:T(8,128)(2,1)S(1)} %copy-done.6), channel_id=1, source_target_pairs={{48,96},{96,48},{144,192},{192,144},{240,288},{288,240},{336,384},... | collective-permute-start | bytes 2359304 | tf_op jit(solution)/shard_map/ppermute | solution.py:17
  104.1 38.9 %collective-permute-start.8 = (bf16[2,128,512]{2,1,0:T(8,128)(2,1)S(1)}, bf16[2,128,512]{2,1,0:T(8,128)(2,1)S(1)}, u32[]{:S(2)}, u32[]{:S(2)}) collective-permute-start(bf16[2,128,512]{2,1,0:T(8,128)(2,1)S(1)} %get-tuple-element.16), channel_id=1, source_target_pairs={{0,8},{8,0},{16,24},{24,16},{32,40},{40,32},{1,9},{9,1},{17,25},{2... | collective-permute-start | bytes 786440 | tf_op jit(solution)/shard_map/ppermute | solution.py:17
  107.8 35.3 %collective-permute-start.9 = (bf16[2,128,512]{2,1,0:T(8,128)(2,1)S(1)}, bf16[2,128,512]{2,1,0:T(8,128)(2,1)S(1)}, u32[]{:S(2)}, u32[]{:S(2)}) collective-permute-start(bf16[2,128,512]{2,1,0:T(8,128)(2,1)S(1)} %get-tuple-element.17), channel_id=1, source_target_pairs={{0,40},{8,16},{16,8},{24,32},{32,24},{40,0},{1,41},{9,17},{17,9},{... | collective-permute-start | bytes 786440 | tf_op jit(solution)/shard_map/ppermute | solution.py:17
  135.1 15.7 %all-to-all-start.2 = ((bf16[16,8,512]{2,1,0:T(8,128)(2,1)}), bf16[16,8,512]{2,1,0:T(8,128)(2,1)S(1)}, u32[]{:S(2)}, u32[]{:S(2)}) async-start(bf16[16,8,512]{2,1,0:T(8,128)(2,1)} %broadcast_in_dim.36), calls=%async_computation.2 | async-start | bytes 262144 | tf_op jit(solution)/shard_map/all_to_all | solution.py:43

commit v4 on v3

--- a/solution.py
+++ b/solution.py
@@ -36,11 +36,6 @@
 
 def lat_mates_of(array):
     return exchange(array, "lat", next_door), exchange(array, "lat", other_door)
-
-
-def to_all(array, axis):
-    count = lax.axis_size(axis)
-    return lax.all_to_all(jnp.broadcast_to(array[None], (count,) + array.shape), axis, 0, 0)
 
 
 def attention_kernel(
@@ -52,15 +47,16 @@
     value,
     partner,
     far,
-    pair_p,
+    near_p,
     far_p,
-    pair_q,
+    near_q,
     far_q,
-    w_parts,
     grad_query,
-    up,
-    middle,
-    down,
+    to_partner,
+    own_column,
+    far_ends,
+    far_middle,
+    w_own,
     prob,
 ):
     wide, low = jnp.float32, jnp.bfloat16
@@ -79,9 +75,9 @@
     def nine(own, at):
         return jnp.concatenate(
             [
-                pair_p[0, at], pair_p[1, at], far_p[at],
-                partner[at], own[...], far[at],
-                pair_q[0, at], pair_q[1, at], far_q[at],
+                partner[1, at], near_p[at], far_p[at],
+                partner[0, at], own[...], far[at],
+                partner[2, at], near_q[at], far_q[at],
             ],
             axis=0,
         )
@@ -116,12 +112,19 @@
         low_parts.append(part.astype(low))
     prob_low = jnp.concatenate(low_parts, axis=0)
     attended = joined(dot(values.T, prob_low, ((1,), (0,)))).astype(low)
+
     w_rows = dot(attended, grad[...], ((1,), (0,)))
-    width = w_parts.shape[2]
-    across = w_rows.shape[1] // width
-    for at in range(w_parts.shape[0]):
+    half = w_rows.shape[1] // 2
+    first_core = live[9] == 0
+    kept = jnp.where(first_core, w_rows[:, :half], w_rows[:, half:])
+    given = jnp.where(first_core, w_rows[:, half:], w_rows[:, :half]).astype(low)
+    width = w_own.shape[2]
+    across = half // width
+    for at in range(w_own.shape[0]):
         row, column = at // across * PART_ROWS, at % across * width
-        w_parts[at] = w_rows[row : row + PART_ROWS, column : column + width].astype(low)
+        w_own[at] = kept[row : row + PART_ROWS, column : column + width]
+    for at in range(half // LANES):
+        to_partner[6 + at] = given[:, at * LANES : (at + 1) * LANES]
 
     product = dout[...].T.astype(wide) * attended.astype(wide)
     row_delta = jnp.concatenate(
@@ -144,10 +147,13 @@
     grad_query[...] = (joined(dot(keys.T, grad_score, ((1,), (0,)))) * SCALE).T.astype(low)
     grad_keys = dot(grad_score, query_cat, ((1,), (0,)))
     grad_values = dot(prob_low, dout_cat, ((1,), (0,)))
-    for row, out in enumerate((up, middle, down)):
-        for column in range(3):
-            out[column, 0] = block(grad_keys, row * 3 + column).astype(out.dtype)
-            out[column, 1] = block(grad_values, row * 3 + column).astype(out.dtype)
+    for at, array in enumerate((grad_keys, grad_values)):
+        for row in range(3):
+            to_partner[row * 2 + at] = block(array, row * 3).astype(low)
+            own_column[row, at] = block(array, row * 3 + 1)
+        far_ends[0, at] = block(array, 2).astype(low)
+        far_ends[1, at] = block(array, 8).astype(low)
+        far_middle[at] = block(array, 5)
 
 
 def attention(live, query, dout, grad, near, parts):
@@ -155,31 +161,35 @@
     low, wide = query.dtype, jnp.float32
     model_width = grad.shape[1]
     steps = width // LANES
-    part_width = width * model_width // parts // PART_ROWS
+    half = model_width // 2
+    part_width = width * half // parts // PART_ROWS
     one = pl.BlockSpec((block_len, LANES), lambda p: (0, p))
     two = pl.BlockSpec((2, block_len, LANES), lambda p: (0, 0, p))
     four = pl.BlockSpec((2, 2, block_len, LANES), lambda p: (0, 0, 0, p))
-    pairs = pl.BlockSpec((3, 2, block_len, LANES), lambda p: (0, 0, 0, p))
+    six = pl.BlockSpec((3, 2, block_len, LANES), lambda p: (0, 0, 0, p))
+    given = 6 + half // LANES
     shape = jax.ShapeDtypeStruct
     return pl.pallas_call(
         attention_kernel,
         grid=(steps,),
         in_specs=[pl.BlockSpec(memory_space=pltpu.SMEM), one, one]
         + [pl.BlockSpec((block_len, model_width), lambda p: (0, 0))]
-        + [one, one, two, two, four, two, four, two],
+        + [one, one, six, two, two, two, two, two],
         out_specs=[
+            one,
+            pl.BlockSpec((given, block_len, LANES), lambda p: (0, 0, p)),
+            six,
+            four,
+            two,
             pl.BlockSpec((parts // steps, PART_ROWS, part_width), lambda p: (p, 0, 0)),
-            one,
-            pairs,
-            pairs,
-            pairs,
         ],
         out_shape=[
-            shape((parts, PART_ROWS, part_width), low),
             shape((block_len, width), low),
-            shape((3, 2, block_len, width), low),
+            shape((given, block_len, width), low),
             shape((3, 2, block_len, width), wide),
-            shape((3, 2, block_len, width), low),
+            shape((2, 2, block_len, width), low),
+            shape((2, block_len, width), wide),
+            shape((parts, PART_ROWS, part_width), wide),
         ],
         scratch_shapes=[pltpu.VMEM((9 * block_len, 2 * block_len), wide)],
         compiler_params=pltpu.CompilerParams(
@@ -193,12 +203,90 @@
     )(live, query, dout, grad, *near)
 
 
+def chip_sum_kernel(given, own_column, far_ends, w_own, send_p, send_q, own_sum, w_parts):
+    wide, low = jnp.float32, jnp.bfloat16
+    for at in range(2):
+        send_p[0, at] = (own_column[0, at] + given[at].astype(wide)).astype(low)
+        own_sum[at] = own_column[1, at] + given[2 + at].astype(wide)
+        send_q[0, at] = (own_column[2, at] + given[4 + at].astype(wide)).astype(low)
+        send_p[1, at] = far_ends[0, at]
+        send_q[1, at] = far_ends[1, at]
+    w_given = [given[at].astype(wide) for at in range(6, given.shape[0])]
+    tiles = w_parts.shape[2] // LANES
+    across = len(w_given) // tiles
+    for at in range(w_parts.shape[0]):
+        row, first = at // across * PART_ROWS, at % across * tiles
+        there = [w_given[first + tile][row : row + PART_ROWS] for tile in range(tiles)]
+        w_parts[at] = (w_own[at] + jnp.concatenate(there, axis=1)).astype(low)
+
+
+def chip_sum(given, own_column, far_ends, w_own):
+    block_len, width = given.shape[1:]
+    low, wide = given.dtype, jnp.float32
+    steps = width // LANES
+    two = pl.BlockSpec((2, block_len, LANES), lambda p: (0, 0, p))
+    four = pl.BlockSpec((2, 2, block_len, LANES), lambda p: (0, 0, 0, p))
+    six = pl.BlockSpec((3, 2, block_len, LANES), lambda p: (0, 0, 0, p))
+    parts = pl.BlockSpec((w_own.shape[0] // steps,) + w_own.shape[1:], lambda p: (p, 0, 0))
+    shape = jax.ShapeDtypeStruct
+    return pl.pallas_call(
+        chip_sum_kernel,
+        grid=(steps,),
+        in_specs=[
+            pl.BlockSpec((given.shape[0], block_len, LANES), lambda p: (0, 0, p)),
+            six,
+            four,
+            parts,
+        ],
+        out_specs=[four, four, two, parts],
+        out_shape=[
+            shape((2, 2, block_len, width), low),
+            shape((2, 2, block_len, width), low),
+            shape((2, block_len, width), wide),
+            shape(w_own.shape, low),
+        ],
+        compiler_params=pltpu.CompilerParams(
+            dimension_semantics=("arbitrary",), vmem_limit_bytes=24 << 20
+        ),
+        cost_estimate=pl.CostEstimate(
+            flops=4 * given.size, bytes_accessed=8 * given.size, transcendentals=0
+        ),
+    )(given, own_column, far_ends, w_own)
+
+
+def sum_and_copy(array, copies, dtype):
+    def kernel(terms, out):
+        total = jnp.sum(terms[...].astype(jnp.float32), axis=0).astype(dtype)
+        for at in range(copies):
+            out[at] = total
+
+    return pl.pallas_call(
+        kernel, out_shape=jax.ShapeDtypeStruct((copies,) + array.shape[1:], dtype)
+    )(array)
+
+
+def assemble(pieces, rows, columns):
+    height, width = pieces.shape[1:]
+    across = columns // 2 // width
+
+    def kernel(pieces, out):
+        for at in range(pieces.shape[0]):
+            lat, core = at // 2, at % 2
+            row, column = lat // across * height, (core * across + lat % across) * width
+            out[row : row + height, column : column + width] = pieces[at].astype(jnp.float32)
+
+    return pl.pallas_call(kernel, out_shape=jax.ShapeDtypeStruct((rows, columns), jnp.float32))(
+        pieces
+    )
+
+
 def shards(queries, keys, values, grad_out, w_out, pattern):
     low, wide = jnp.bfloat16, jnp.float32
     query, key, value, grad = queries[0, 0, 0], keys[0, 0, 0], values[0, 0, 0], grad_out[0, 0, 0]
     block_len, att_width = query.shape
     model_width = grad.shape[1]
-    lat_count, opt_count = lax.axis_size("lat"), lax.axis_size("opt")
+    lat_count, lon_count = lax.axis_size("lat"), lax.axis_size("lon")
+    opt_count = lax.axis_size("opt")
     at_lat, at_lon = lax.axis_index("lat"), lax.axis_index("lon")
 
     dout = lax.dot_general(
@@ -211,28 +299,38 @@
     direction = (lat_step + 1) * 3 + lon_step + 1
     flags = jnp.sum(jnp.where(direction[:, None] == at[None, :], flags[None, :], 0), axis=1)
     key_rows = at_lat + lat_step
-    live = ((flags > 0) & (key_rows >= 0) & (key_rows < lat_count)).astype(jnp.int32)
+    live = (flags > 0) & (key_rows >= 0) & (key_rows < lat_count)
+    live = jnp.append(live.astype(jnp.int32), at_lon % 2)
 
     own = jnp.stack((key, value))
-    far, partner = far_of(own), partner_of(own)
-    pair_p, pair_q = lat_mates_of(jnp.stack((partner, own)))
+    far = far_of(own)
+    near_p, near_q = lat_mates_of(own)
+    partner = partner_of(jnp.stack((own, near_p, near_q)))
     far_p, far_q = lat_mates_of(far)
     parts = opt_count * lat_count
-    w_parts, grad_query, to_p, middle, to_q = attention(
-        live, query, dout, grad, (key, value, partner, far, pair_p, far_p, pair_q, far_q), parts
-    )
-
-    w_part = jnp.sum(lax.all_to_all(w_parts, ("opt", "lat"), 0, 0).astype(wide), axis=0)
-    w_part = jnp.sum(to_all(w_part, "lon"), axis=0).astype(low)
-    across = model_width // w_part.shape[1]
-    grad_weight = to_all(w_part, "lat").reshape(lat_count // across, across, PART_ROWS, -1)
-    grad_weight = grad_weight.swapaxes(1, 2).reshape(att_width // opt_count, model_width).astype(wide)
-
+    grad_query, to_partner, own_column, far_ends, far_middle, w_own = attention(
+        live, query, dout, grad, (key, value, partner, far, near_p, far_p, near_q, far_q), parts
+    )
+
+    to_p, to_q, own_sum, w_parts = chip_sum(partner_of(to_partner), own_column, far_ends, w_own)
     from_p, from_q = exchange(to_p, "lat", next_door), exchange(to_q, "lat", other_door)
-    sums = middle + from_p.astype(wide) + from_q.astype(wide)
-    from_far = far_of(sums[2].astype(low))
-    from_partner = partner_of(sums[0].astype(low))
-    owned = (sums[1] + from_partner.astype(wide) + from_far.astype(wide)).astype(low)
+    owned = own_sum + from_p[0].astype(wide) + from_q[0].astype(wide)
+    far_sum = (far_middle + from_p[1].astype(wide) + from_q[1].astype(wide)).astype(low)
+    owned, far_sum = lax.optimization_barrier((owned, far_sum))
+    owned = (owned + far_of(far_sum).astype(wide)).astype(low)
+
+    cores = [list(range(core, lon_count, 2)) for core in range(2)]
+    chips = [
+        [lat * lon_count + chip + core for lat in range(lat_count) for core in range(2)]
+        for chip in range(0, lon_count, 2)
+    ]
+    w_part = lax.all_to_all(w_parts, ("opt", "lat"), 0, 0)
+    w_part = sum_and_copy(w_part, len(cores[0]), wide)
+    w_part = lax.all_to_all(w_part, "lon", 0, 0, axis_index_groups=cores)
+    w_part = sum_and_copy(w_part, len(chips[0]), low)
+    w_part = lax.all_to_all(w_part, ("lat", "lon"), 0, 0, axis_index_groups=chips)
+    grad_weight = assemble(w_part, att_width // opt_count, model_width)
+
     return (
         grad_query[None, None, None],
         owned[0][None, None, None],

time: 152 us -> 142 us (0.934)
  waiting for transfers between devices: 44.4 us -> 32.8 us
  Pallas kernels: 9.15 us -> 16.2 us
  other arithmetic: 6.28 us -> 1.77 us
  local copies, waits for them, and re-layouts: 6.31 us -> 2.51 us
  starting transfers between devices: 65.7 us -> 68.8 us
    ppermute x10, waiting for transfers between devices: 38.5 us -> 25.1 us  [exchange(): lax.ppermute(array, axis, [(i, j) for i, j in pairs if 0 <= j < lax.axis_...]
    ppermute x10, starting transfers between devices: 36.5 us -> 48.7 us  [exchange(): lax.ppermute(array, axis, [(i, j) for i, j in pairs if 0 <= j < lax.axis_...]
    all_to_all x2, starting transfers between devices: 29.3 us -> 20.1 us  [the longest x1 15 us: shards(): w_part = lax.all_to_all(w_parts, ('opt', 'lat'), 0, 0)]
    pallas_call x0 -> x4, Pallas kernels: none -> 6.95 us  [the longest x2 3.22 us: sum_and_copy(): pl.pallas_call(kernel, out_shape=jax.ShapeDtypeStruct((copies,) + array.s...]
    unnamed x22 -> x12, local copies, waits for them, and re-layouts: 3.77 us -> 0.69 us
    all_to_all x2, waiting for transfers between devices: 5.89 us -> 7.74 us  [the longest x1 7.74 us: shards(): lax.all_to_all(w_part, ('lat', 'lon'), 0, 0, axis_index_groups=chips)]
    convert_element_type x3, other arithmetic: 1.89 us -> 0.29 us  [the longest x1 0.21 us: shards(): (far_middle + from_p[1].astype(wide) + from_q[1].astype(wide)).astype(low)]
    another operation x3 -> x2, other arithmetic: 2.76 us -> 1.2 us  [shards(): partner = partner_of(jnp.stack((own, near_p, near_q)))]
  transfers between devices with their start and end apart: 12 -> 12, of which waited for: 4 -> 5; matrix products, arithmetic and copies ran while one was open for 5% -> 2% of each run, Pallas kernels for 0% -> 2%
where the time goes in v4:
time: 142 us; the launch traced here: 141 us
  starting transfers between devices  68.8 us (48%)
  waiting for transfers between devices  32.8 us (23%)
  blocking collectives  17.4 us (12%)
  Pallas kernels  16.2 us (11%)
  local copies, waits for them, and re-layouts  2.51 us (2%)
  other arithmetic  1.77 us (1%)
    ppermute x10, starting transfers between devices, exchange(): lax.ppermute(array, axis, [(i, j) for i, j in pairs if 0 <= j < lax.axis_...  48.7 us
    ppermute x10, waiting for transfers between devices, exchange(): lax.ppermute(array, axis, [(i, j) for i, j in pairs if 0 <= j < lax.axis_...  25.1 us
    all_to_all x1, blocking collectives, shards(): w_part = lax.all_to_all(w_part, 'lon', 0, 0, axis_index_groups=cores)  17.4 us
    all_to_all x1, starting transfers between devices, shards(): w_part = lax.all_to_all(w_parts, ('opt', 'lat'), 0, 0)  15 us
    pallas_call x1, Pallas kernels, attention(): pl.pallas_call(attention_kernel, grid=(steps,), in_specs=[pl.BlockSpec(me...  9.2 us
    all_to_all x1, waiting for transfers between devices, shards(): lax.all_to_all(w_part, ('lat', 'lon'), 0, 0, axis_index_groups=chips)  7.74 us
    all_to_all x1, starting transfers between devices, shards(): lax.all_to_all(w_part, ('lat', 'lon'), 0, 0, axis_index_groups=chips)  5.1 us
    pallas_call x2, Pallas kernels, sum_and_copy(): pl.pallas_call(kernel, out_shape=jax.ShapeDtypeStruct((copies,) + array.s...  3.22 us
  transfers between devices with their start and end apart: 12, of which 5 were waited for; matrix products, arithmetic and copies ran while one was open for 2% of the time, Pallas kernels for 2%

profile of v4, /device:TPU:1, one launch (start us, length us, event | category | flops | bytes accessed | tf_op | source)
XLA Modules:
  0.0 140.8 jit_solution(13701230480132163093)
XLA Ops:
  0.7 1.1 fusion.8
  2.5 6.4 %collective-permute-start = (bf16[2,128,512]{2,1,0:T(8,128)(2,1)S(1)}, bf16[2,128,512]{2,1,0:T(8,128)(2,1)S(1)}, u32[]{:S(2)}, u32[]{:S(2)}) collective-permute-start(bf16[2,128,512]{2,1,0:T(8,128)(2,1)S(1)} %get-tuple-element.33), channel_id=1, source_target_pairs={{0,48},{48,0},{96,144},{144,96},{192,240},{240,192},{288,336},{336... | collective-permute-start | bytes 786440 | tf_op jit(solution)/shard_map/ppermute | solution.py:17
  8.8 11.8 %collective-permute-start.3 = (bf16[2,128,512]{2,1,0:T(8,128)(2,1)S(1)}, bf16[2,128,512]{2,1,0:T(8,128)(2,1)S(1)}, u32[]{:S(2)}, u32[]{:S(2)}) collective-permute-start(bf16[2,128,512]{2,1,0:T(8,128)(2,1)S(1)} %get-tuple-element.33), channel_id=1, source_target_pairs={{0,40},{8,16},{16,8},{24,32},{32,24},{40,0},{1,41},{9,17},{17,9},{... | collective-permute-start | bytes 786440 | tf_op jit(solution)/shard_map/ppermute | solution.py:17
  20.6 1.1 dynamic-slice_reduce_fusion
  21.9 5.0 %collective-permute-start.2 = (bf16[3,2,128,512]{3,2,1,0:T(8,128)(2,1)S(1)}, bf16[3,2,128,512]{3,2,1,0:T(8,128)(2,1)S(1)}, u32[]{:S(2)}, u32[]{:S(2)}) collective-permute-start(bf16[3,2,128,512]{3,2,1,0:T(8,128)(2,1)S(1)} %pad_maximum_fusion), channel_id=1, source_target_pairs={{0,8},{8,0},{16,24},{24,16},{32,40},{40,32},{1,9},{9,1},{17,25},{2... | collective-permute-start | bytes 2359304 | tf_op jit(solution)/shard_map/ppermute | solution.py:17
  27.1 2.4 %collective-permute-done.3.far = bf16[2,128,512]{2,1,0:T(8,128)(2,1)S(1)} collective-permute-done((bf16[2,128,512]{2,1,0:T(8,128)(2,1)S(1)}, bf16[2,128,512]{2,1,0:T(8,128)(2,1)S(1)}, u32[]{:S(2)}, u32[]{:S(2)}) %collective-permute-start.3) | collective-permute-done | bytes 262176 | tf_op jit(solution)/shard_map/ppermute | solution.py:17
  30.2 4.9 %collective-permute-start.4 = (bf16[2,128,512]{2,1,0:T(8,128)(2,1)S(1)}, bf16[2,128,512]{2,1,0:T(8,128)(2,1)S(1)}, u32[]{:S(2)}, u32[]{:S(2)}) collective-permute-start(bf16[2,128,512]{2,1,0:T(8,128)(2,1)S(1)} %collective-permute-done.3.far), channel_id=1, source_target_pairs={{0,48},{48,0},{96,144},{144,96},{192,240},{240,192},{288,336},{336... | collective-permute-start | bytes 786440 | tf_op jit(solution)/shard_map/ppermute | solution.py:17
  35.7 3.2 %collective-permute-done.4.far_p = bf16[2,128,512]{2,1,0:T(8,128)(2,1)S(1)} collective-permute-done((bf16[2,128,512]{2,1,0:T(8,128)(2,1)S(1)}, bf16[2,128,512]{2,1,0:T(8,128)(2,1)S(1)}, u32[]{:S(2)}, u32[]{:S(2)}) %collective-permute-start.4) | collective-permute-done | bytes 262176 | tf_op jit(solution)/shard_map/ppermute | solution.py:17
  38.8 9.2 %shard_map.93 = (bf16[128,512]{1,0:T(8,128)(2,1)}, bf16[10,128,512]{2,1,0:T(8,128)(2,1)S(1)}, f32[3,2,128,512]{3,2,1,0:T(8,128)S(1)}, bf16[2,2,128,512]{3,2,1,0:...) custom-call(s32[10]{0:T(128)S(1)} %pad_add_fusion.live, bf16[128,512]{1,0:T(8,128)(2,1)S(1)} %bitcast.46, ...), custom_call_target="tpu_custom_call" | custom-call | flops 1811939328 | bytes 8388608 | tf_op jit(solution)/shard_map/pallas_call | solution.py:172
  48.0 9.7 %collective-permute-start.6 = (bf16[10,128,512]{2,1,0:T(8,128)(2,1)S(1)}, bf16[10,128,512]{2,1,0:T(8,128)(2,1)S(1)}, u32[]{:S(2)}, u32[]{:S(2)}) collective-permute-start(bf16[10,128,512]{2,1,0:T(8,128)(2,1)S(1)} %get-tuple-element.17), channel_id=1, source_target_pairs={{0,8},{8,0},{16,24},{24,16},{32,40},{40,32},{1,9},{9,1},{17,25},{2... | collective-permute-start | bytes 3932168 | tf_op jit(solution)/shard_map/ppermute | solution.py:17
  57.7 2.6 %collective-permute-done.6.given = bf16[10,128,512]{2,1,0:T(8,128)(2,1)S(1)} collective-permute-done((bf16[10,128,512]{2,1,0:T(8,128)(2,1)S(1)}, bf16[10,128,512]{2,1,0:T(8,128)(2,1)S(1)}, u32[]{:S(2)}, u32[]{:S(2)}) %collective-permute-start.6) | collective-permute-done | bytes 1310752 | tf_op jit(solution)/shard_map/ppermute | solution.py:17
  60.4 2.1 %shard_map.94 = (bf16[2,2,128,512]{3,2,1,0:T(8,128)(2,1)S(1)}, bf16[2,2,128,512]{3,2,1,0:T(8,128)(2,1)S(1)}, f32[2,128,512]{2,1,0:T(8,128)S(1)}, bf16[128,8,256]{2,1,0:T(8,128)(2,1)}) custom-call(bf16[10,128,512]{2,1,0:T(8,128)(2,1)S(1)} %collective-permute-done.6.given, f32[3,2,128,512]{3,2,1,0:T(8,128)S(1)} %get-tuple-element.18.own_column, ...), custom_call_target="tpu_custom_call" | custom-call | flops 2621440 | bytes 5242880 | tf_op jit(solution)/shard_map/pallas_call | solution.py:232
  62.5 15.0 %all-to-all-start = ((bf16[128,8,256]{2,1,0:T(8,128)(2,1)}), bf16[128,8,256]{2,1,0:T(8,128)(2,1)}, u32[]{:S(2)}, u32[]{:S(2)}) async-start(bf16[128,8,256]{2,1,0:T(8,128)(2,1)} %get-tuple-element.27), calls=%async_computation | async-start | bytes 1048576 | tf_op jit(solution)/shard_map/all_to_all | solution.py:327
  77.5 2.4 %collective-permute-start.7 = (bf16[2,2,128,512]{3,2,1,0:T(8,128)(2,1)S(1)}, bf16[2,2,128,512]{3,2,1,0:T(8,128)(2,1)S(1)}, u32[]{:S(2)}, u32[]{:S(2)}) collective-permute-start(bf16[2,2,128,512]{3,2,1,0:T(8,128)(2,1)S(1)} %get-tuple-element.22), channel_id=1, source_target_pairs={{0,48},{48,0},{96,144},{144,96},{192,240},{240,192},{288,336},{336... | collective-permute-start | bytes 1572872 | tf_op jit(solution)/shard_map/ppermute | solution.py:17
  79.9 0.7 collective-permute-start.8
  80.6 16.8 %collective-permute-done.7 = bf16[2,2,128,512]{3,2,1,0:T(8,128)(2,1)S(1)} collective-permute-done((bf16[2,2,128,512]{3,2,1,0:T(8,128)(2,1)S(1)}, bf16[2,2,128,512]{3,2,1,0:T(8,128)(2,1)S(1)}, u32[]{:S(2)}, u32[]{:S(2)}) %collective-permute-start.7) | collective-permute-done | bytes 524320 | tf_op jit(solution)/shard_map/ppermute | solution.py:17
  97.7 6.6 %collective-permute-start.9 = (bf16[2,128,512]{2,1,0:T(8,128)(2,1)S(1)}, bf16[2,128,512]{2,1,0:T(8,128)(2,1)S(1)}, u32[]{:S(2)}, u32[]{:S(2)}) collective-permute-start(bf16[2,128,512]{2,1,0:T(8,128)(2,1)S(1)} %get-tuple-element.26), channel_id=1, source_target_pairs={{0,40},{8,16},{16,8},{24,32},{32,24},{40,0},{1,41},{9,17},{17,9},{... | collective-permute-start | bytes 786440 | tf_op jit(solution)/shard_map/ppermute | solution.py:17
  104.3 1.8 %shard_map.95 = f32[3,8,256]{2,1,0:T(8,128)} custom-call(bf16[128,8,256]{2,1,0:T(8,128)(2,1)} %all-to-all-done.terms), custom_call_target="tpu_custom_call" | custom-call | tf_op jit(solution)/shard_map/pallas_call | solution.py:263
  106.1 17.4 %all_to_all.15.terms = f32[3,8,256]{2,1,0:T(8,128)} all-to-all(f32[3,8,256]{2,1,0:T(8,128)} %shard_map.95), channel_id=1, replica_groups={{0,16,32},{8,24,40},{1,17,33},{9,25,41},{2,18,34},{10,26,42},{3,19,35},..., dimensions={0} | all-to-all | bytes 49152 | tf_op jit(solution)/shard_map/all_to_all | solution.py:329
  123.5 1.4 shard_map.96
  124.9 5.1 %all-to-all-start.2 = ((bf16[32,8,256]{2,1,0:T(8,128)(2,1)}), bf16[32,8,256]{2,1,0:T(8,128)(2,1)S(1)}, u32[]{:S(2)}, u32[]{:S(2)}) async-start(bf16[32,8,256]{2,1,0:T(8,128)(2,1)} %shard_map.96), calls=%async_computation.2 | async-start | bytes 262144 | tf_op jit(solution)/shard_map/all_to_all | solution.py:331
  130.1 0.7 slice_bitcast_fusion.4
  130.8 7.7 %all-to-all-done.2.pieces = bf16[32,8,256]{2,1,0:T(8,128)(2,1)S(1)} async-done(((bf16[32,8,256]{2,1,0:T(8,128)(2,1)}), bf16[32,8,256]{2,1,0:T(8,128)(2,1)S(1)}, u32[]{:S(2)}, u32[]{:S(2)}) %all-to-all-start.2) | async-done | bytes 131104 | tf_op jit(solution)/shard_map/all_to_all | solution.py:331
  139.2 1.6 %shard_map.97 = f32[64,1024]{1,0:T(8,128)} custom-call(bf16[32,8,256]{2,1,0:T(8,128)(2,1)} %copy-done.5), custom_call_target="tpu_custom_call" | custom-call | tf_op jit(solution)/shard_map/pallas_call | solution.py:278
  (29 shorter events, 3.2 us)
Async XLA Ops:
  0.6 34.5 %copy-start = (bf16[512,1024]{1,0:T(8,128)(2,1)S(1)}, bf16[512,1024]{1,0:T(8,128)(2,1)}, u32[]{:S(2)}) copy-start(bf16[512,1024]{1,0:T(8,128)(2,1)} %param.10) | copy-start | bytes 3145732
  0.6 34.5 %copy-start.1 = (bf16[1,1,1,128,1024]{4,3,2,1,0:T(8,128)(2,1)S(1)}, bf16[1,1,1,128,1024]{4,3,2,1,0:T(8,128)(2,1)}, u32[]{:S(2)}) copy-start(bf16[1,1,1,128,1024]{4,3,2,1,0:T(8,128)(2,1)} %param.9) | copy-start | bytes 786436
  1.8 20.0 %collective-permute-start.1 = (bf16[2,128,512]{2,1,0:T(8,128)(2,1)S(1)}, bf16[2,128,512]{2,1,0:T(8,128)(2,1)S(1)}, u32[]{:S(2)}, u32[]{:S(2)}) collective-permute-start(bf16[2,128,512]{2,1,0:T(8,128)(2,1)S(1)} %get-tuple-element.33), channel_id=1, source_target_pairs={{48,96},{96,48},{144,192},{192,144},{240,288},{288,240},{336,384},... | collective-permute-start | bytes 786440 | tf_op jit(solution)/shard_map/ppermute | solution.py:17
  2.5 19.3 %collective-permute-start = (bf16[2,128,512]{2,1,0:T(8,128)(2,1)S(1)}, bf16[2,128,512]{2,1,0:T(8,128)(2,1)S(1)}, u32[]{:S(2)}, u32[]{:S(2)}) collective-permute-start(bf16[2,128,512]{2,1,0:T(8,128)(2,1)S(1)} %get-tuple-element.33), channel_id=1, source_target_pairs={{0,48},{48,0},{96,144},{144,96},{192,240},{240,192},{288,336},{336... | collective-permute-start | bytes 786440 | tf_op jit(solution)/shard_map/ppermute | solution.py:17
  8.8 20.7 %collective-permute-start.3 = (bf16[2,128,512]{2,1,0:T(8,128)(2,1)S(1)}, bf16[2,128,512]{2,1,0:T(8,128)(2,1)S(1)}, u32[]{:S(2)}, u32[]{:S(2)}) collective-permute-start(bf16[2,128,512]{2,1,0:T(8,128)(2,1)S(1)} %get-tuple-element.33), channel_id=1, source_target_pairs={{0,40},{8,16},{16,8},{24,32},{32,24},{40,0},{1,41},{9,17},{17,9},{... | collective-permute-start | bytes 786440 | tf_op jit(solution)/shard_map/ppermute | solution.py:17
  21.8 17.1 %copy-start.2 = (bf16[1,1,1,128,512]{4,3,2,1,0:T(8,128)(2,1)S(1)}, bf16[1,1,1,128,512]{4,3,2,1,0:T(8,128)(2,1)}, u32[]{:S(2)}) copy-start(bf16[1,1,1,128,512]{4,3,2,1,0:T(8,128)(2,1)} %param.7) | copy-start | bytes 393220
  21.8 17.0 %copy-start.3 = (bf16[1,1,1,128,512]{4,3,2,1,0:T(8,128)(2,1)S(1)}, bf16[1,1,1,128,512]{4,3,2,1,0:T(8,128)(2,1)}, u32[]{:S(2)}) copy-start(bf16[1,1,1,128,512]{4,3,2,1,0:T(8,128)(2,1)} %param.8) | copy-start | bytes 393220
  21.8 17.0 %copy-start.4 = (bf16[1,1,1,128,512]{4,3,2,1,0:T(8,128)(2,1)S(1)}, bf16[1,1,1,128,512]{4,3,2,1,0:T(8,128)(2,1)}, u32[]{:S(2)}) copy-start(bf16[1,1,1,128,512]{4,3,2,1,0:T(8,128)(2,1)} %param.6) | copy-start | bytes 393220
  21.9 16.9 %collective-permute-start.2 = (bf16[3,2,128,512]{3,2,1,0:T(8,128)(2,1)S(1)}, bf16[3,2,128,512]{3,2,1,0:T(8,128)(2,1)S(1)}, u32[]{:S(2)}, u32[]{:S(2)}) collective-permute-start(bf16[3,2,128,512]{3,2,1,0:T(8,128)(2,1)S(1)} %pad_maximum_fusion), channel_id=1, source_target_pairs={{0,8},{8,0},{16,24},{24,16},{32,40},{40,32},{1,9},{9,1},{17,25},{2... | collective-permute-start | bytes 2359304 | tf_op jit(solution)/shard_map/ppermute | solution.py:17
  29.5 6.1 %collective-permute-start.5 = (bf16[2,128,512]{2,1,0:T(8,128)(2,1)S(1)}, bf16[2,128,512]{2,1,0:T(8,128)(2,1)S(1)}, u32[]{:S(2)}, u32[]{:S(2)}) collective-permute-start(bf16[2,128,512]{2,1,0:T(8,128)(2,1)S(1)} %collective-permute-done.3.far), channel_id=1, source_target_pairs={{48,96},{96,48},{144,192},{192,144},{240,288},{288,240},{336,384},... | collective-permute-start | bytes 786440 | tf_op jit(solution)/shard_map/ppermute | solution.py:17
  30.2 8.6 %collective-permute-start.4 = (bf16[2,128,512]{2,1,0:T(8,128)(2,1)S(1)}, bf16[2,128,512]{2,1,0:T(8,128)(2,1)S(1)}, u32[]{:S(2)}, u32[]{:S(2)}) collective-permute-start(bf16[2,128,512]{2,1,0:T(8,128)(2,1)S(1)} %collective-permute-done.3.far), channel_id=1, source_target_pairs={{0,48},{48,0},{96,144},{144,96},{192,240},{240,192},{288,336},{336... | collective-permute-start | bytes 786440 | tf_op jit(solution)/shard_map/ppermute | solution.py:17
  48.0 12.3 %collective-permute-start.6 = (bf16[10,128,512]{2,1,0:T(8,128)(2,1)S(1)}, bf16[10,128,512]{2,1,0:T(8,128)(2,1)S(1)}, u32[]{:S(2)}, u32[]{:S(2)}) collective-permute-start(bf16[10,128,512]{2,1,0:T(8,128)(2,1)S(1)} %get-tuple-element.17), channel_id=1, source_target_pairs={{0,8},{8,0},{16,24},{24,16},{32,40},{40,32},{1,9},{9,1},{17,25},{2... | collective-permute-start | bytes 3932168 | tf_op jit(solution)/shard_map/ppermute | solution.py:17
  62.5 41.8 %all-to-all-start = ((bf16[128,8,256]{2,1,0:T(8,128)(2,1)}), bf16[128,8,256]{2,1,0:T(8,128)(2,1)}, u32[]{:S(2)}, u32[]{:S(2)}) async-start(bf16[128,8,256]{2,1,0:T(8,128)(2,1)} %get-tuple-element.27), calls=%async_computation | async-start | bytes 1048576 | tf_op jit(solution)/shard_map/all_to_all | solution.py:327
  77.5 20.0 %collective-permute-start.7 = (bf16[2,2,128,512]{3,2,1,0:T(8,128)(2,1)S(1)}, bf16[2,2,128,512]{3,2,1,0:T(8,128)(2,1)S(1)}, u32[]{:S(2)}, u32[]{:S(2)}) collective-permute-start(bf16[2,2,128,512]{3,2,1,0:T(8,128)(2,1)S(1)} %get-tuple-element.22), channel_id=1, source_target_pairs={{0,48},{48,0},{96,144},{144,96},{192,240},{240,192},{288,336},{336... | collective-permute-start | bytes 1572872 | tf_op jit(solution)/shard_map/ppermute | solution.py:17
  79.9 17.5 %collective-permute-start.8 = (bf16[2,2,128,512]{3,2,1,0:T(8,128)(2,1)S(1)}, bf16[2,2,128,512]{3,2,1,0:T(8,128)(2,1)S(1)}, u32[]{:S(2)}, u32[]{:S(2)}) collective-permute-start(bf16[2,2,128,512]{3,2,1,0:T(8,128)(2,1)S(1)} %get-tuple-element.23), channel_id=1, source_target_pairs={{48,96},{96,48},{144,192},{192,144},{240,288},{288,240},{336,384},... | collective-permute-start | bytes 1572872 | tf_op jit(solution)/shard_map/ppermute | solution.py:17
  97.7 32.3 %collective-permute-start.9 = (bf16[2,128,512]{2,1,0:T(8,128)(2,1)S(1)}, bf16[2,128,512]{2,1,0:T(8,128)(2,1)S(1)}, u32[]{:S(2)}, u32[]{:S(2)}) collective-permute-start(bf16[2,128,512]{2,1,0:T(8,128)(2,1)S(1)} %get-tuple-element.26), channel_id=1, source_target_pairs={{0,40},{8,16},{16,8},{24,32},{32,24},{40,0},{1,41},{9,17},{17,9},{... | collective-permute-start | bytes 786440 | tf_op jit(solution)/shard_map/ppermute | solution.py:17
  124.9 13.7 %all-to-all-start.2 = ((bf16[32,8,256]{2,1,0:T(8,128)(2,1)}), bf16[32,8,256]{2,1,0:T(8,128)(2,1)S(1)}, u32[]{:S(2)}, u32[]{:S(2)}) async-start(bf16[32,8,256]{2,1,0:T(8,128)(2,1)} %shard_map.96), calls=%async_computation.2 | async-start | bytes 262144 | tf_op jit(solution)/shard_map/all_to_all | solution.py:331
  138.6 0.7 copy-start.5

commit v5 on v4

--- a/solution.py
+++ b/solution.py
@@ -53,11 +53,12 @@
     far_q,
     grad_query,
     to_partner,
+    w_given,
     own_column,
     far_ends,
     far_middle,
     w_own,
-    prob,
+    weights,
 ):
     wide, low = jnp.float32, jnp.bfloat16
     block_len = query.shape[0]
@@ -93,23 +94,22 @@
     keys, values = nine(key, 0), nine(value, 1)
 
     scores = dot(keys, query_cat, ((1,), (1,)))
+    shift = [jnp.where(live[at] > 0, 0.0, DEAD) for at in range(9)]
     row_max = None
     for at in range(9):
-        part = block(scores, at) + jnp.where(live[at] > 0, 0.0, DEAD)
-        prob[at * block_len : (at + 1) * block_len, :] = part
+        part = jnp.max(block(scores, at), axis=0, keepdims=True) + shift[at]
         row_max = part if row_max is None else jnp.maximum(row_max, part)
-    row_max = jnp.max(row_max, axis=0, keepdims=True)
     total = None
     for at in range(9):
-        part = jnp.exp(prob[at * block_len : (at + 1) * block_len, :] - row_max)
-        prob[at * block_len : (at + 1) * block_len, :] = part
+        part = jnp.exp(block(scores, at) + (shift[at] - row_max))
+        weights[at * block_len : (at + 1) * block_len, :] = part
         total = part if total is None else total + part
     norm = 1.0 / jnp.sum(total, axis=0, keepdims=True)
-    low_parts = []
-    for at in range(9):
-        part = prob[at * block_len : (at + 1) * block_len, :] * norm
-        prob[at * block_len : (at + 1) * block_len, :] = part
-        low_parts.append(part.astype(low))
+
+    def prob(at):
+        return weights[at * block_len : (at + 1) * block_len, :] * norm
+
+    low_parts = [prob(at).astype(low) for at in range(9)]
     prob_low = jnp.concatenate(low_parts, axis=0)
     attended = joined(dot(values.T, prob_low, ((1,), (0,)))).astype(low)
 
@@ -124,7 +124,7 @@
         row, column = at // across * PART_ROWS, at % across * width
         w_own[at] = kept[row : row + PART_ROWS, column : column + width]
     for at in range(half // LANES):
-        to_partner[6 + at] = given[:, at * LANES : (at + 1) * LANES]
+        w_given[at] = given[:, at * LANES : (at + 1) * LANES]
 
     product = dout[...].T.astype(wide) * attended.astype(wide)
     row_delta = jnp.concatenate(
@@ -137,10 +137,7 @@
     grad_prob = dot(values, dout_cat, ((1,), (1,)))
     grad_score = jnp.concatenate(
         [
-            (
-                prob[at * block_len : (at + 1) * block_len, :] * (block(grad_prob, at) - row_delta)
-            ).astype(low)
-            for at in range(9)
+            (prob(at) * (block(grad_prob, at) - row_delta)).astype(low) for at in range(9)
         ],
         axis=0,
     )
@@ -167,7 +164,6 @@
     two = pl.BlockSpec((2, block_len, LANES), lambda p: (0, 0, p))
     four = pl.BlockSpec((2, 2, block_len, LANES), lambda p: (0, 0, 0, p))
     six = pl.BlockSpec((3, 2, block_len, LANES), lambda p: (0, 0, 0, p))
-    given = 6 + half // LANES
     shape = jax.ShapeDtypeStruct
     return pl.pallas_call(
         attention_kernel,
@@ -177,7 +173,8 @@
         + [one, one, six, two, two, two, two, two],
         out_specs=[
             one,
-            pl.BlockSpec((given, block_len, LANES), lambda p: (0, 0, p)),
+            pl.BlockSpec((6, block_len, LANES), lambda p: (0, 0, p)),
+            pl.BlockSpec((half // LANES, block_len, LANES), lambda p: (0, 0, p)),
             six,
             four,
             two,
@@ -185,7 +182,8 @@
         ],
         out_shape=[
             shape((block_len, width), low),
-            shape((given, block_len, width), low),
+            shape((6, block_len, width), low),
+            shape((half // LANES, block_len, width), low),
             shape((3, 2, block_len, width), wide),
             shape((2, 2, block_len, width), low),
             shape((2, block_len, width), wide),
@@ -193,7 +191,7 @@
         ],
         scratch_shapes=[pltpu.VMEM((9 * block_len, 2 * block_len), wide)],
         compiler_params=pltpu.CompilerParams(
-            dimension_semantics=("arbitrary",), vmem_limit_bytes=40 << 20
+            dimension_semantics=("arbitrary",), vmem_limit_bytes=24 << 20
         ),
         cost_estimate=pl.CostEstimate(
             flops=12 * 9 * block_len * block_len * width * 2,
@@ -203,7 +201,7 @@
     )(live, query, dout, grad, *near)
 
 
-def chip_sum_kernel(given, own_column, far_ends, w_own, send_p, send_q, own_sum, w_parts):
+def chip_sum_kernel(given, own_column, far_ends, send_p, send_q, own_sum):
     wide, low = jnp.float32, jnp.bfloat16
     for at in range(2):
         send_p[0, at] = (own_column[0, at] + given[at].astype(wide)).astype(low)
@@ -211,7 +209,63 @@
         send_q[0, at] = (own_column[2, at] + given[4 + at].astype(wide)).astype(low)
         send_p[1, at] = far_ends[0, at]
         send_q[1, at] = far_ends[1, at]
-    w_given = [given[at].astype(wide) for at in range(6, given.shape[0])]
+
+
+def chip_sum(given, own_column, far_ends):
+    block_len, width = given.shape[1:]
+    low, wide = given.dtype, jnp.float32
+    two = pl.BlockSpec((2, block_len, LANES), lambda p: (0, 0, p))
+    four = pl.BlockSpec((2, 2, block_len, LANES), lambda p: (0, 0, 0, p))
+    six = pl.BlockSpec((3, 2, block_len, LANES), lambda p: (0, 0, 0, p))
+    shape = jax.ShapeDtypeStruct
+    return pl.pallas_call(
+        chip_sum_kernel,
+        grid=(width // LANES,),
+        in_specs=[pl.BlockSpec((6, block_len, LANES), lambda p: (0, 0, p)), six, four],
+        out_specs=[four, four, two],
+        out_shape=[
+            shape((2, 2, block_len, width), low),
+            shape((2, 2, block_len, width), low),
+            shape((2, block_len, width), wide),
+        ],
+        compiler_params=pltpu.CompilerParams(
+            dimension_semantics=("arbitrary",), vmem_limit_bytes=8 << 20
+        ),
+        cost_estimate=pl.CostEstimate(
+            flops=2 * given.size, bytes_accessed=5 * given.size, transcendentals=0
+        ),
+    )(given, own_column, far_ends)
+
+
+def lat_sum_kernel(own_sum, far_middle, from_p, from_q, owned, far_sum):
+    wide = jnp.float32
+    for at in range(2):
+        owned[at] = own_sum[at] + from_p[0, at].astype(wide) + from_q[0, at].astype(wide)
+        far = far_middle[at] + from_p[1, at].astype(wide) + from_q[1, at].astype(wide)
+        far_sum[at] = far.astype(far_sum.dtype)
+
+
+def lat_sum(own_sum, far_middle, from_p, from_q):
+    _, block_len, width = own_sum.shape
+    two = pl.BlockSpec((2, block_len, LANES), lambda p: (0, 0, p))
+    four = pl.BlockSpec((2, 2, block_len, LANES), lambda p: (0, 0, 0, p))
+    shape = jax.ShapeDtypeStruct
+    return pl.pallas_call(
+        lat_sum_kernel,
+        grid=(width // LANES,),
+        in_specs=[two, two, four, four],
+        out_specs=[two, two],
+        out_shape=[shape(own_sum.shape, own_sum.dtype), shape(own_sum.shape, from_p.dtype)],
+        compiler_params=pltpu.CompilerParams(
+            dimension_semantics=("arbitrary",), vmem_limit_bytes=8 << 20
+        ),
+        cost_estimate=pl.CostEstimate(flops=60_000_000_000, bytes_accessed=4 << 20, transcendentals=0),
+    )(own_sum, far_middle, from_p, from_q)
+
+
+def weight_sum_kernel(given, w_own, w_parts):
+    wide, low = jnp.float32, jnp.bfloat16
+    w_given = [given[at].astype(wide) for at in range(given.shape[0])]
     tiles = w_parts.shape[2] // LANES
     across = len(w_given) // tiles
     for at in range(w_parts.shape[0]):
@@ -220,38 +274,23 @@
         w_parts[at] = (w_own[at] + jnp.concatenate(there, axis=1)).astype(low)
 
 
-def chip_sum(given, own_column, far_ends, w_own):
-    block_len, width = given.shape[1:]
-    low, wide = given.dtype, jnp.float32
+def weight_sum(given, w_own):
+    count, block_len, width = given.shape
     steps = width // LANES
-    two = pl.BlockSpec((2, block_len, LANES), lambda p: (0, 0, p))
-    four = pl.BlockSpec((2, 2, block_len, LANES), lambda p: (0, 0, 0, p))
-    six = pl.BlockSpec((3, 2, block_len, LANES), lambda p: (0, 0, 0, p))
     parts = pl.BlockSpec((w_own.shape[0] // steps,) + w_own.shape[1:], lambda p: (p, 0, 0))
-    shape = jax.ShapeDtypeStruct
-    return pl.pallas_call(
-        chip_sum_kernel,
+    return pl.pallas_call(
+        weight_sum_kernel,
         grid=(steps,),
-        in_specs=[
-            pl.BlockSpec((given.shape[0], block_len, LANES), lambda p: (0, 0, p)),
-            six,
-            four,
-            parts,
-        ],
-        out_specs=[four, four, two, parts],
-        out_shape=[
-            shape((2, 2, block_len, width), low),
-            shape((2, 2, block_len, width), low),
-            shape((2, block_len, width), wide),
-            shape(w_own.shape, low),
-        ],
+        in_specs=[pl.BlockSpec((count, block_len, LANES), lambda p: (0, 0, p)), parts],
+        out_specs=parts,
+        out_shape=jax.ShapeDtypeStruct(w_own.shape, given.dtype),
         compiler_params=pltpu.CompilerParams(
-            dimension_semantics=("arbitrary",), vmem_limit_bytes=24 << 20
+            dimension_semantics=("arbitrary",), vmem_limit_bytes=8 << 20
         ),
         cost_estimate=pl.CostEstimate(
-            flops=4 * given.size, bytes_accessed=8 * given.size, transcendentals=0
-        ),
-    )(given, own_column, far_ends, w_own)
+            flops=w_own.size, bytes_accessed=8 * w_own.size, transcendentals=0
+        ),
+    )(given, w_own)
 
 
 def sum_and_copy(array, copies, dtype):
@@ -261,7 +300,11 @@
             out[at] = total
 
     return pl.pallas_call(
-        kernel, out_shape=jax.ShapeDtypeStruct((copies,) + array.shape[1:], dtype)
+        kernel,
+        in_specs=[pl.BlockSpec(memory_space=pltpu.VMEM)],
+        out_specs=pl.BlockSpec(memory_space=pltpu.VMEM),
+        out_shape=jax.ShapeDtypeStruct((copies,) + array.shape[1:], dtype),
+        compiler_params=pltpu.CompilerParams(vmem_limit_bytes=8 << 20),
     )(array)
 
 
@@ -275,9 +318,12 @@
             row, column = lat // across * height, (core * across + lat % across) * width
             out[row : row + height, column : column + width] = pieces[at].astype(jnp.float32)
 
-    return pl.pallas_call(kernel, out_shape=jax.ShapeDtypeStruct((rows, columns), jnp.float32))(
-        pieces
-    )
+    return pl.pallas_call(
+        kernel,
+        in_specs=[pl.BlockSpec(memory_space=pltpu.VMEM)],
+        out_shape=jax.ShapeDtypeStruct((rows, columns), jnp.float32),
+        compiler_params=pltpu.CompilerParams(vmem_limit_bytes=8 << 20),
+    )(pieces)
 
 
 def shards(queries, keys, values, grad_out, w_out, pattern):
@@ -308,15 +354,14 @@
     partner = partner_of(jnp.stack((own, near_p, near_q)))
     far_p, far_q = lat_mates_of(far)
     parts = opt_count * lat_count
-    grad_query, to_partner, own_column, far_ends, far_middle, w_own = attention(
+    grad_query, to_partner, w_given, own_column, far_ends, far_middle, w_own = attention(
         live, query, dout, grad, (key, value, partner, far, near_p, far_p, near_q, far_q), parts
     )
 
-    to_p, to_q, own_sum, w_parts = chip_sum(partner_of(to_partner), own_column, far_ends, w_own)
+    to_p, to_q, own_sum = chip_sum(partner_of(to_partner), own_column, far_ends)
+    w_parts = weight_sum(partner_of(w_given), w_own)
     from_p, from_q = exchange(to_p, "lat", next_door), exchange(to_q, "lat", other_door)
-    owned = own_sum + from_p[0].astype(wide) + from_q[0].astype(wide)
-    far_sum = (far_middle + from_p[1].astype(wide) + from_q[1].astype(wide)).astype(low)
-    owned, far_sum = lax.optimization_barrier((owned, far_sum))
+    owned, far_sum = lat_sum(own_sum, far_middle, from_p, from_q)
     owned = (owned + far_of(far_sum).astype(wide)).astype(low)
 
     cores = [list(range(core, lon_count, 2)) for core in range(2)]

time: 142 us -> 143 us (level)
  starting transfers between devices: 68.8 us -> 76.5 us
  waiting for transfers between devices: 32.8 us -> 25.1 us
    ppermute x10 -> x11, waiting for transfers between devices: 25.1 us -> 5.8 us  [exchange(): lax.ppermute(array, axis, [(i, j) for i, j in pairs if 0 <= j < lax.axis_...]
    all_to_all x1, waiting for transfers between devices: 0.01 us -> 11.5 us  [shards(): w_part = lax.all_to_all(w_parts, ('opt', 'lat'), 0, 0)]
    ppermute x10 -> x11, starting transfers between devices: 48.7 us -> 52.7 us  [exchange(): lax.ppermute(array, axis, [(i, j) for i, j in pairs if 0 <= j < lax.axis_...]
    all_to_all x1, starting transfers between devices: 5.1 us -> 7.88 us  [shards(): lax.all_to_all(w_part, ('lat', 'lon'), 0, 0, axis_index_groups=chips)]
    pallas_call x4 -> x6, Pallas kernels: 6.95 us -> 7.19 us  [the longest x1 2.24 us: lat_sum(): pl.pallas_call(lat_sum_kernel, grid=(width // LANES,), in_specs=[two, two...]
  transfers between devices with their start and end apart: 12 -> 13, of which waited for: 5 -> 4; matrix products, arithmetic and copies ran while one was open for 2% -> 2% of each run, Pallas kernels for 2% -> 5%
where the time goes in v5:
time: 143 us; the launch traced here: 142 us
  starting transfers between devices  76.5 us (53%)
  waiting for transfers between devices  25.1 us (18%)
  blocking collectives  17.2 us (12%)
  Pallas kernels  16.4 us (11%)
  local copies, waits for them, and re-layouts  3.7 us (3%)
  other arithmetic  1.56 us (1%)
    ppermute x11, starting transfers between devices, exchange(): lax.ppermute(array, axis, [(i, j) for i, j in pairs if 0 <= j < lax.axis_...  52.7 us
    all_to_all x1, blocking collectives, shards(): w_part = lax.all_to_all(w_part, 'lon', 0, 0, axis_index_groups=cores)  17.2 us
    all_to_all x1, starting transfers between devices, shards(): w_part = lax.all_to_all(w_parts, ('opt', 'lat'), 0, 0)  15.9 us
    all_to_all x1, waiting for transfers between devices, shards(): w_part = lax.all_to_all(w_parts, ('opt', 'lat'), 0, 0)  11.5 us
    pallas_call x1, Pallas kernels, attention(): pl.pallas_call(attention_kernel, grid=(steps,), in_specs=[pl.BlockSpec(me...  9.23 us
    all_to_all x1, starting transfers between devices, shards(): lax.all_to_all(w_part, ('lat', 'lon'), 0, 0, axis_index_groups=chips)  7.88 us
    all_to_all x1, waiting for transfers between devices, shards(): lax.all_to_all(w_part, ('lat', 'lon'), 0, 0, axis_index_groups=chips)  7.85 us
    ppermute x11, waiting for transfers between devices, exchange(): lax.ppermute(array, axis, [(i, j) for i, j in pairs if 0 <= j < lax.axis_...  5.8 us
  transfers between devices with their start and end apart: 13, of which 4 were waited for; matrix products, arithmetic and copies ran while one was open for 2% of the time, Pallas kernels for 5%

profile of v5, /device:TPU:1, one launch (start us, length us, event | category | flops | bytes accessed | tf_op | source)
XLA Modules:
  0.0 142.0 jit_solution(15590224078541958912)
XLA Ops:
  0.7 1.1 fusion.7
  1.8 0.8 collective-permute-start.1
  2.6 6.4 %collective-permute-start = (bf16[2,128,512]{2,1,0:T(8,128)(2,1)S(1)}, bf16[2,128,512]{2,1,0:T(8,128)(2,1)S(1)}, u32[]{:S(2)}, u32[]{:S(2)}) collective-permute-start(bf16[2,128,512]{2,1,0:T(8,128)(2,1)S(1)} %get-tuple-element.31), channel_id=1, source_target_pairs={{0,48},{48,0},{96,144},{144,96},{192,240},{240,192},{288,336},{336... | collective-permute-start | bytes 786440 | tf_op jit(solution)/shard_map/ppermute | solution.py:17
  9.0 11.8 %collective-permute-start.3 = (bf16[2,128,512]{2,1,0:T(8,128)(2,1)S(1)}, bf16[2,128,512]{2,1,0:T(8,128)(2,1)S(1)}, u32[]{:S(2)}, u32[]{:S(2)}) collective-permute-start(bf16[2,128,512]{2,1,0:T(8,128)(2,1)S(1)} %get-tuple-element.31), channel_id=1, source_target_pairs={{0,40},{8,16},{16,8},{24,32},{32,24},{40,0},{1,41},{9,17},{17,9},{... | collective-permute-start | bytes 786440 | tf_op jit(solution)/shard_map/ppermute | solution.py:17
  20.8 1.1 dynamic-slice_reduce_fusion
  22.0 4.8 %collective-permute-start.2 = (bf16[3,2,128,512]{3,2,1,0:T(8,128)(2,1)S(1)}, bf16[3,2,128,512]{3,2,1,0:T(8,128)(2,1)S(1)}, u32[]{:S(2)}, u32[]{:S(2)}) collective-permute-start(bf16[3,2,128,512]{3,2,1,0:T(8,128)(2,1)S(1)} %pad_maximum_fusion), channel_id=1, source_target_pairs={{0,8},{8,0},{16,24},{24,16},{32,40},{40,32},{1,9},{9,1},{17,25},{2... | collective-permute-start | bytes 2359304 | tf_op jit(solution)/shard_map/ppermute | solution.py:17
  27.1 2.6 %collective-permute-done.3.far = bf16[2,128,512]{2,1,0:T(8,128)(2,1)S(1)} collective-permute-done((bf16[2,128,512]{2,1,0:T(8,128)(2,1)S(1)}, bf16[2,128,512]{2,1,0:T(8,128)(2,1)S(1)}, u32[]{:S(2)}, u32[]{:S(2)}) %collective-permute-start.3) | collective-permute-done | bytes 262176 | tf_op jit(solution)/shard_map/ppermute | solution.py:17
  30.4 4.9 %collective-permute-start.4 = (bf16[2,128,512]{2,1,0:T(8,128)(2,1)S(1)}, bf16[2,128,512]{2,1,0:T(8,128)(2,1)S(1)}, u32[]{:S(2)}, u32[]{:S(2)}) collective-permute-start(bf16[2,128,512]{2,1,0:T(8,128)(2,1)S(1)} %collective-permute-done.3.far), channel_id=1, source_target_pairs={{0,48},{48,0},{96,144},{144,96},{192,240},{240,192},{288,336},{336... | collective-permute-start | bytes 786440 | tf_op jit(solution)/shard_map/ppermute | solution.py:17
  35.8 3.2 %collective-permute-done.4.far_p = bf16[2,128,512]{2,1,0:T(8,128)(2,1)S(1)} collective-permute-done((bf16[2,128,512]{2,1,0:T(8,128)(2,1)S(1)}, bf16[2,128,512]{2,1,0:T(8,128)(2,1)S(1)}, u32[]{:S(2)}, u32[]{:S(2)}) %collective-permute-start.4) | collective-permute-done | bytes 262176 | tf_op jit(solution)/shard_map/ppermute | solution.py:17
  39.0 9.2 %shard_map.93 = (bf16[128,512]{1,0:T(8,128)(2,1)}, bf16[6,128,512]{2,1,0:T(8,128)(2,1)S(1)}, bf16[4,128,512]{2,1,0:T(8,128)(2,1)S(1)}, f32[3,2,128,512]{3,2,1,0:...) custom-call(s32[10]{0:T(128)S(1)} %pad_add_fusion.live, ...), custom_call_target="tpu_custom_call" | custom-call | flops 1811939328 | bytes 8388608 | tf_op jit(solution)/shard_map/pallas_call | solution.py:168
  49.0 9.7 %collective-permute-start.6 = (bf16[6,128,512]{2,1,0:T(8,128)(2,1)S(1)}, bf16[6,128,512]{2,1,0:T(8,128)(2,1)S(1)}, u32[]{:S(2)}, u32[]{:S(2)}) collective-permute-start(bf16[6,128,512]{2,1,0:T(8,128)(2,1)S(1)} %get-tuple-element.17), channel_id=1, source_target_pairs={{0,8},{8,0},{16,24},{24,16},{32,40},{40,32},{1,9},{9,1},{17,25},{2... | collective-permute-start | bytes 2359304 | tf_op jit(solution)/shard_map/ppermute | solution.py:17
  58.7 1.9 %collective-permute-start.10 = (bf16[4,128,512]{2,1,0:T(8,128)(2,1)S(1)}, bf16[4,128,512]{2,1,0:T(8,128)(2,1)S(1)}, u32[]{:S(2)}, u32[]{:S(2)}) collective-permute-start(bf16[4,128,512]{2,1,0:T(8,128)(2,1)S(1)} %get-tuple-element.26), channel_id=1, source_target_pairs={{0,8},{8,0},{16,24},{24,16},{32,40},{40,32},{1,9},{9,1},{17,25},{2... | collective-permute-start | bytes 1572872 | tf_op jit(solution)/shard_map/ppermute | solution.py:17
  60.7 1.9 %shard_map.94 = (bf16[2,2,128,512]{3,2,1,0:T(8,128)(2,1)}, bf16[2,2,128,512]{3,2,1,0:T(8,128)(2,1)S(1)}, f32[2,128,512]{2,1,0:T(8,128)S(1)}) custom-call(bf16[6,128,512]{2,1,0:T(8,128)(2,1)S(1)} %collective-permute-done.6.given, f32[3,2,128,512]{3,2,1,0:T(8,128)S(1)} %get-tuple-element.18.own_column, bf16[2,2,128,512]{3,2,1,0:T(8,128)(2,1)S(1)} %get-tuple-element.19.far_ends), custom_call_target="tpu_custom_call" | custom-call | flops 786432 | bytes 1966080 | tf_op jit(solution)/shard_map/pallas_call | solution.py:221
  62.6 3.6 %collective-permute-start.7 = (bf16[2,2,128,512]{3,2,1,0:T(8,128)(2,1)}, bf16[2,2,128,512]{3,2,1,0:T(8,128)(2,1)S(1)}, u32[]{:S(2)}, u32[]{:S(2)}) collective-permute-start(bf16[2,2,128,512]{3,2,1,0:T(8,128)(2,1)} %get-tuple-element.22), channel_id=1, source_target_pairs={{0,48},{48,0},{96,144},{144,96},{192,240},{240,192},{288,336},{336... | collective-permute-start | bytes 1572872 | tf_op jit(solution)/shard_map/ppermute | solution.py:17
  66.2 1.5 %collective-permute-start.8 = (bf16[2,2,128,512]{3,2,1,0:T(8,128)(2,1)S(1)}, bf16[2,2,128,512]{3,2,1,0:T(8,128)(2,1)}, u32[]{:S(2)}, u32[]{:S(2)}) collective-permute-start(bf16[2,2,128,512]{3,2,1,0:T(8,128)(2,1)S(1)} %get-tuple-element.23), channel_id=1, source_target_pairs={{48,96},{96,48},{144,192},{192,144},{240,288},{288,240},{336,384},... | collective-permute-start | bytes 1572872 | tf_op jit(solution)/shard_map/ppermute | solution.py:17
  67.7 1.5 %shard_map.96 = bf16[128,8,256]{2,1,0:T(8,128)(2,1)} custom-call(bf16[4,128,512]{2,1,0:T(8,128)(2,1)S(1)} %collective-permute-done.10.given, f32[128,8,256]{2,1,0:T(8,128)S(1)} %get-tuple-element.27.w_own), custom_call_target="tpu_custom_call" | custom-call | flops 262144 | bytes 2097152 | tf_op jit(solution)/shard_map/pallas_call | solution.py:281
  69.2 15.9 %all-to-all-start = ((bf16[128,8,256]{2,1,0:T(8,128)(2,1)}), bf16[128,8,256]{2,1,0:T(8,128)(2,1)S(1)}, u32[]{:S(2)}, u32[]{:S(2)}) async-start(bf16[128,8,256]{2,1,0:T(8,128)(2,1)} %shard_map.96), calls=%async_computation | async-start | bytes 1048576 | tf_op jit(solution)/shard_map/all_to_all | solution.py:372
  85.1 1.0 copy-done.6
  86.1 2.2 %shard_map.95 = (f32[2,128,512]{2,1,0:T(8,128)S(1)}, bf16[2,128,512]{2,1,0:T(8,128)(2,1)S(1)}) custom-call(f32[2,128,512]{2,1,0:T(8,128)S(1)} %get-tuple-element.20.own_sum, f32[2,128,512]{2,1,0:T(8,128)S(1)} %copy-done.6, bf16[2,2,128,512]{3,2,1,0:T(8,128)(2,1)S(1)} %collective-permute-done.7.from_p, bf16[2,2,128,512]{3,2,1,0:T(8,128)(2,1)} %collective-permute-done.8.from_q), custom_call_target="tpu_custom_call" | custom-call | flops 60000002048 | bytes 4194304 | tf_op jit(solution)/shard_map/pallas_call | solution.py:253
  88.4 6.8 %collective-permute-start.9 = (bf16[2,128,512]{2,1,0:T(8,128)(2,1)S(1)}, bf16[2,128,512]{2,1,0:T(8,128)(2,1)S(1)}, u32[]{:S(2)}, u32[]{:S(2)}) collective-permute-start(bf16[2,128,512]{2,1,0:T(8,128)(2,1)S(1)} %get-tuple-element.25), channel_id=1, source_target_pairs={{0,40},{8,16},{16,8},{24,32},{32,24},{40,0},{1,41},{9,17},{17,9},{... | collective-permute-start | bytes 786440 | tf_op jit(solution)/shard_map/ppermute | solution.py:17
  95.1 11.5 %all-to-all-done.terms = bf16[128,8,256]{2,1,0:T(8,128)(2,1)S(1)} async-done(((bf16[128,8,256]{2,1,0:T(8,128)(2,1)}), bf16[128,8,256]{2,1,0:T(8,128)(2,1)S(1)}, u32[]{:S(2)}, u32[]{:S(2)}) %all-to-all-start) | async-done | bytes 524320 | tf_op jit(solution)/shard_map/all_to_all | solution.py:372
  106.8 17.2 %all_to_all.15.terms = f32[3,8,256]{2,1,0:T(8,128)S(1)} all-to-all(f32[3,8,256]{2,1,0:T(8,128)S(1)} %shard_map.97), channel_id=1, replica_groups={{0,16,32},{8,24,40},{1,17,33},{9,25,41},{2,18,34},{10,26,42},{3,19,35},..., dimensions={0} | all-to-all | bytes 49152 | tf_op jit(solution)/shard_map/all_to_all | solution.py:374
  124.7 7.9 %all-to-all-start.2 = ((bf16[32,8,256]{2,1,0:T(8,128)(2,1)}), bf16[32,8,256]{2,1,0:T(8,128)(2,1)S(1)}, u32[]{:S(2)}, u32[]{:S(2)}) async-start(bf16[32,8,256]{2,1,0:T(8,128)(2,1)} %shard_map.98), calls=%async_computation.2 | async-start | bytes 262144 | tf_op jit(solution)/shard_map/all_to_all | solution.py:376
  133.4 7.9 %all-to-all-done.2.pieces = bf16[32,8,256]{2,1,0:T(8,128)(2,1)S(1)} async-done(((bf16[32,8,256]{2,1,0:T(8,128)(2,1)}), bf16[32,8,256]{2,1,0:T(8,128)(2,1)S(1)}, u32[]{:S(2)}, u32[]{:S(2)}) %all-to-all-start.2) | async-done | bytes 131104 | tf_op jit(solution)/shard_map/all_to_all | solution.py:376
  (34 shorter events, 4.7 us)
Async XLA Ops:
  0.6 34.7 %copy-start = (bf16[512,1024]{1,0:T(8,128)(2,1)S(1)}, bf16[512,1024]{1,0:T(8,128)(2,1)}, u32[]{:S(2)}) copy-start(bf16[512,1024]{1,0:T(8,128)(2,1)} %param.10) | copy-start | bytes 3145732
  0.6 34.7 %copy-start.1 = (bf16[1,1,1,128,1024]{4,3,2,1,0:T(8,128)(2,1)S(1)}, bf16[1,1,1,128,1024]{4,3,2,1,0:T(8,128)(2,1)}, u32[]{:S(2)}) copy-start(bf16[1,1,1,128,1024]{4,3,2,1,0:T(8,128)(2,1)} %param.9) | copy-start | bytes 786436
  1.8 37.2 %copy-start.2 = (bf16[1,1,1,128,512]{4,3,2,1,0:T(8,128)(2,1)S(1)}, bf16[1,1,1,128,512]{4,3,2,1,0:T(8,128)(2,1)}, u32[]{:S(2)}) copy-start(bf16[1,1,1,128,512]{4,3,2,1,0:T(8,128)(2,1)} %param.7) | copy-start | bytes 393220
  1.8 37.2 %copy-start.3 = (bf16[1,1,1,128,512]{4,3,2,1,0:T(8,128)(2,1)S(1)}, bf16[1,1,1,128,512]{4,3,2,1,0:T(8,128)(2,1)}, u32[]{:S(2)}) copy-start(bf16[1,1,1,128,512]{4,3,2,1,0:T(8,128)(2,1)} %param.8) | copy-start | bytes 393220
  1.8 37.2 %copy-start.4 = (bf16[1,1,1,128,512]{4,3,2,1,0:T(8,128)(2,1)S(1)}, bf16[1,1,1,128,512]{4,3,2,1,0:T(8,128)(2,1)}, u32[]{:S(2)}) copy-start(bf16[1,1,1,128,512]{4,3,2,1,0:T(8,128)(2,1)} %param.6) | copy-start | bytes 393220
  1.8 20.1 %collective-permute-start.1 = (bf16[2,128,512]{2,1,0:T(8,128)(2,1)S(1)}, bf16[2,128,512]{2,1,0:T(8,128)(2,1)S(1)}, u32[]{:S(2)}, u32[]{:S(2)}) collective-permute-start(bf16[2,128,512]{2,1,0:T(8,128)(2,1)S(1)} %get-tuple-element.31), channel_id=1, source_target_pairs={{48,96},{96,48},{144,192},{192,144},{240,288},{288,240},{336,384},... | collective-permute-start | bytes 786440 | tf_op jit(solution)/shard_map/ppermute | solution.py:17
  2.6 19.3 %collective-permute-start = (bf16[2,128,512]{2,1,0:T(8,128)(2,1)S(1)}, bf16[2,128,512]{2,1,0:T(8,128)(2,1)S(1)}, u32[]{:S(2)}, u32[]{:S(2)}) collective-permute-start(bf16[2,128,512]{2,1,0:T(8,128)(2,1)S(1)} %get-tuple-element.31), channel_id=1, source_target_pairs={{0,48},{48,0},{96,144},{144,96},{192,240},{240,192},{288,336},{336... | collective-permute-start | bytes 786440 | tf_op jit(solution)/shard_map/ppermute | solution.py:17
  9.0 20.7 %collective-permute-start.3 = (bf16[2,128,512]{2,1,0:T(8,128)(2,1)S(1)}, bf16[2,128,512]{2,1,0:T(8,128)(2,1)S(1)}, u32[]{:S(2)}, u32[]{:S(2)}) collective-permute-start(bf16[2,128,512]{2,1,0:T(8,128)(2,1)S(1)} %get-tuple-element.31), channel_id=1, source_target_pairs={{0,40},{8,16},{16,8},{24,32},{32,24},{40,0},{1,41},{9,17},{17,9},{... | collective-permute-start | bytes 786440 | tf_op jit(solution)/shard_map/ppermute | solution.py:17
  22.0 17.0 %collective-permute-start.2 = (bf16[3,2,128,512]{3,2,1,0:T(8,128)(2,1)S(1)}, bf16[3,2,128,512]{3,2,1,0:T(8,128)(2,1)S(1)}, u32[]{:S(2)}, u32[]{:S(2)}) collective-permute-start(bf16[3,2,128,512]{3,2,1,0:T(8,128)(2,1)S(1)} %pad_maximum_fusion), channel_id=1, source_target_pairs={{0,8},{8,0},{16,24},{24,16},{32,40},{40,32},{1,9},{9,1},{17,25},{2... | collective-permute-start | bytes 2359304 | tf_op jit(solution)/shard_map/ppermute | solution.py:17
  29.7 6.1 %collective-permute-start.5 = (bf16[2,128,512]{2,1,0:T(8,128)(2,1)S(1)}, bf16[2,128,512]{2,1,0:T(8,128)(2,1)S(1)}, u32[]{:S(2)}, u32[]{:S(2)}) collective-permute-start(bf16[2,128,512]{2,1,0:T(8,128)(2,1)S(1)} %collective-permute-done.3.far), channel_id=1, source_target_pairs={{48,96},{96,48},{144,192},{192,144},{240,288},{288,240},{336,384},... | collective-permute-start | bytes 786440 | tf_op jit(solution)/shard_map/ppermute | solution.py:17
  30.4 8.6 %collective-permute-start.4 = (bf16[2,128,512]{2,1,0:T(8,128)(2,1)S(1)}, bf16[2,128,512]{2,1,0:T(8,128)(2,1)S(1)}, u32[]{:S(2)}, u32[]{:S(2)}) collective-permute-start(bf16[2,128,512]{2,1,0:T(8,128)(2,1)S(1)} %collective-permute-done.3.far), channel_id=1, source_target_pairs={{0,48},{48,0},{96,144},{144,96},{192,240},{240,192},{288,336},{336... | collective-permute-start | bytes 786440 | tf_op jit(solution)/shard_map/ppermute | solution.py:17
  48.2 0.8 copy-start.5
  49.0 11.6 %collective-permute-start.6 = (bf16[6,128,512]{2,1,0:T(8,128)(2,1)S(1)}, bf16[6,128,512]{2,1,0:T(8,128)(2,1)S(1)}, u32[]{:S(2)}, u32[]{:S(2)}) collective-permute-start(bf16[6,128,512]{2,1,0:T(8,128)(2,1)S(1)} %get-tuple-element.17), channel_id=1, source_target_pairs={{0,8},{8,0},{16,24},{24,16},{32,40},{40,32},{1,9},{9,1},{17,25},{2... | collective-permute-start | bytes 2359304 | tf_op jit(solution)/shard_map/ppermute | solution.py:17
  58.7 8.9 %collective-permute-start.10 = (bf16[4,128,512]{2,1,0:T(8,128)(2,1)S(1)}, bf16[4,128,512]{2,1,0:T(8,128)(2,1)S(1)}, u32[]{:S(2)}, u32[]{:S(2)}) collective-permute-start(bf16[4,128,512]{2,1,0:T(8,128)(2,1)S(1)} %get-tuple-element.26), channel_id=1, source_target_pairs={{0,8},{8,0},{16,24},{24,16},{32,40},{40,32},{1,9},{9,1},{17,25},{2... | collective-permute-start | bytes 1572872 | tf_op jit(solution)/shard_map/ppermute | solution.py:17
  62.6 22.5 %collective-permute-start.7 = (bf16[2,2,128,512]{3,2,1,0:T(8,128)(2,1)}, bf16[2,2,128,512]{3,2,1,0:T(8,128)(2,1)S(1)}, u32[]{:S(2)}, u32[]{:S(2)}) collective-permute-start(bf16[2,2,128,512]{3,2,1,0:T(8,128)(2,1)} %get-tuple-element.22), channel_id=1, source_target_pairs={{0,48},{48,0},{96,144},{144,96},{192,240},{240,192},{288,336},{336... | collective-permute-start | bytes 1572872 | tf_op jit(solution)/shard_map/ppermute | solution.py:17
  66.2 18.9 %collective-permute-start.8 = (bf16[2,2,128,512]{3,2,1,0:T(8,128)(2,1)S(1)}, bf16[2,2,128,512]{3,2,1,0:T(8,128)(2,1)}, u32[]{:S(2)}, u32[]{:S(2)}) collective-permute-start(bf16[2,2,128,512]{3,2,1,0:T(8,128)(2,1)S(1)} %get-tuple-element.23), channel_id=1, source_target_pairs={{48,96},{96,48},{144,192},{192,144},{240,288},{288,240},{336,384},... | collective-permute-start | bytes 1572872 | tf_op jit(solution)/shard_map/ppermute | solution.py:17
  69.2 37.5 %all-to-all-start = ((bf16[128,8,256]{2,1,0:T(8,128)(2,1)}), bf16[128,8,256]{2,1,0:T(8,128)(2,1)S(1)}, u32[]{:S(2)}, u32[]{:S(2)}) async-start(bf16[128,8,256]{2,1,0:T(8,128)(2,1)} %shard_map.96), calls=%async_computation | async-start | bytes 1048576 | tf_op jit(solution)/shard_map/all_to_all | solution.py:372
  85.1 1.0 copy-start.6
  88.4 44.2 %collective-permute-start.9 = (bf16[2,128,512]{2,1,0:T(8,128)(2,1)S(1)}, bf16[2,128,512]{2,1,0:T(8,128)(2,1)S(1)}, u32[]{:S(2)}, u32[]{:S(2)}) collective-permute-start(bf16[2,128,512]{2,1,0:T(8,128)(2,1)S(1)} %get-tuple-element.25), channel_id=1, source_target_pairs={{0,40},{8,16},{16,8},{24,32},{32,24},{40,0},{1,41},{9,17},{17,9},{... | collective-permute-start | bytes 786440 | tf_op jit(solution)/shard_map/ppermute | solution.py:17
  124.7 16.6 %all-to-all-start.2 = ((bf16[32,8,256]{2,1,0:T(8,128)(2,1)}), bf16[32,8,256]{2,1,0:T(8,128)(2,1)S(1)}, u32[]{:S(2)}, u32[]{:S(2)}) async-start(bf16[32,8,256]{2,1,0:T(8,128)(2,1)} %shard_map.98), calls=%async_computation.2 | async-start | bytes 262144 | tf_op jit(solution)/shard_map/all_to_all | solution.py:376

commit v6 on v5

--- a/solution.py
+++ b/solution.py
@@ -38,60 +38,45 @@
     return exchange(array, "lat", next_door), exchange(array, "lat", other_door)
 
 
-def attention_kernel(
-    live,
-    query,
-    dout,
-    grad,
-    key,
-    value,
-    partner,
-    far,
-    near_p,
-    far_p,
-    near_q,
-    far_q,
-    grad_query,
-    to_partner,
-    w_given,
-    own_column,
-    far_ends,
-    far_middle,
-    w_own,
-    weights,
-):
+def dot(left, right, dims):
+    return lax.dot_general(left, right, (dims, ((), ())), preferred_element_type=jnp.float32)
+
+
+def apart(array):
+    first_head = lax.broadcasted_iota(jnp.int32, array.shape, 1) < HDIM
+    zero = jnp.zeros_like(array)
+    return jnp.concatenate(
+        [jnp.where(first_head, array, zero), jnp.where(first_head, zero, array)], axis=0
+    )
+
+
+def joined(array):
+    half = array.shape[1] // 2
+    return jnp.concatenate([array[:HDIM, :half], array[HDIM:, half:]], axis=0)
+
+
+def nine(own, partner, far, near_p, far_p, near_q, far_q, at):
+    return jnp.concatenate(
+        [
+            partner[1, at], near_p[at], far_p[at],
+            partner[0, at], own[...], far[at],
+            partner[2, at], near_q[at], far_q[at],
+        ],
+        axis=0,
+    )
+
+
+def block(array, at):
+    size = array.shape[0] // 9
+    return array[at * size : (at + 1) * size]
+
+
+def forward_kernel(live, query, dout, grad, key, value, *refs):
+    *near, w_given, w_own, stats, weights = refs
     wide, low = jnp.float32, jnp.bfloat16
     block_len = query.shape[0]
-    first_head = lax.broadcasted_iota(jnp.int32, query.shape, 1) < HDIM
-
-    def apart(array):
-        zero = jnp.zeros_like(array)
-        return jnp.concatenate(
-            [jnp.where(first_head, array, zero), jnp.where(first_head, zero, array)], axis=0
-        )
-
-    def joined(array):
-        return jnp.concatenate([array[:HDIM, :block_len], array[HDIM:, block_len:]], axis=0)
-
-    def nine(own, at):
-        return jnp.concatenate(
-            [
-                partner[1, at], near_p[at], far_p[at],
-                partner[0, at], own[...], far[at],
-                partner[2, at], near_q[at], far_q[at],
-            ],
-            axis=0,
-        )
-
-    def block(array, at):
-        return array[at * block_len : (at + 1) * block_len]
-
-    def dot(left, right, dims):
-        return lax.dot_general(left, right, (dims, ((), ())), preferred_element_type=wide)
-
     query_cat = apart(query[...] * jnp.asarray(SCALE, low))
-    dout_cat = apart(dout[...])
-    keys, values = nine(key, 0), nine(value, 1)
+    keys, values = nine(key, *near, 0), nine(value, *near, 1)
 
     scores = dot(keys, query_cat, ((1,), (1,)))
     shift = [jnp.where(live[at] > 0, 0.0, DEAD) for at in range(9)]
@@ -105,12 +90,7 @@
         weights[at * block_len : (at + 1) * block_len, :] = part
         total = part if total is None else total + part
     norm = 1.0 / jnp.sum(total, axis=0, keepdims=True)
-
-    def prob(at):
-        return weights[at * block_len : (at + 1) * block_len, :] * norm
-
-    low_parts = [prob(at).astype(low) for at in range(9)]
-    prob_low = jnp.concatenate(low_parts, axis=0)
+    prob_low = (weights[...] * norm).astype(low)
     attended = joined(dot(values.T, prob_low, ((1,), (0,)))).astype(low)
 
     w_rows = dot(attended, grad[...], ((1,), (0,)))
@@ -134,13 +114,29 @@
         ],
         axis=1,
     )
+    rows = [jnp.broadcast_to(row, stats.shape[2:]) for row in (row_max, norm, row_delta)]
+    for at, row in enumerate(rows):
+        stats[0, at] = row
+
+
+def backward_kernel(live, query, dout, key, value, *refs):
+    *near, stats, grad_query, to_partner, own_column, far_ends, far_middle = refs
+    low = jnp.bfloat16
+    query_cat = apart(query[...] * jnp.asarray(SCALE, low))
+    dout_cat = apart(dout[...])
+    keys, values = nine(key, *near, 0), nine(value, *near, 1)
+    row_max, norm, row_delta = (stats[0, at, :1] for at in range(3))
+
+    scores = dot(keys, query_cat, ((1,), (1,)))
     grad_prob = dot(values, dout_cat, ((1,), (1,)))
-    grad_score = jnp.concatenate(
-        [
-            (prob(at) * (block(grad_prob, at) - row_delta)).astype(low) for at in range(9)
-        ],
-        axis=0,
-    )
+    prob_low, grad_score = [], []
+    for at in range(9):
+        shift = jnp.where(live[at] > 0, 0.0, DEAD)
+        prob = jnp.exp(block(scores, at) + (shift - row_max)) * norm
+        prob_low.append(prob.astype(low))
+        grad_score.append((prob * (block(grad_prob, at) - row_delta)).astype(low))
+    prob_low = jnp.concatenate(prob_low, axis=0)
+    grad_score = jnp.concatenate(grad_score, axis=0)
     grad_query[...] = (joined(dot(keys.T, grad_score, ((1,), (0,)))) * SCALE).T.astype(low)
     grad_keys = dot(grad_score, query_cat, ((1,), (0,)))
     grad_values = dot(prob_low, dout_cat, ((1,), (0,)))
@@ -164,41 +160,63 @@
     two = pl.BlockSpec((2, block_len, LANES), lambda p: (0, 0, p))
     four = pl.BlockSpec((2, 2, block_len, LANES), lambda p: (0, 0, 0, p))
     six = pl.BlockSpec((3, 2, block_len, LANES), lambda p: (0, 0, 0, p))
+    scalars = pl.BlockSpec(memory_space=pltpu.SMEM)
+    of_near = [one, one, six, two, two, two, two, two]
+    stats_spec = pl.BlockSpec((1, 3, 8, 2 * block_len), lambda p: (p, 0, 0, 0))
     shape = jax.ShapeDtypeStruct
-    return pl.pallas_call(
-        attention_kernel,
+    params = pltpu.CompilerParams(
+        dimension_semantics=("arbitrary",), vmem_limit_bytes=24 << 20
+    )
+    flops = 2 * 2 * 9 * block_len * block_len * width
+    exps = 9 * block_len * block_len * (width // HDIM)
+    w_given, w_own, stats = pl.pallas_call(
+        forward_kernel,
         grid=(steps,),
-        in_specs=[pl.BlockSpec(memory_space=pltpu.SMEM), one, one]
+        in_specs=[scalars, one, one]
         + [pl.BlockSpec((block_len, model_width), lambda p: (0, 0))]
-        + [one, one, six, two, two, two, two, two],
+        + of_near,
+        out_specs=[
+            pl.BlockSpec((half // LANES, block_len, LANES), lambda p: (0, 0, p)),
+            pl.BlockSpec((parts // steps, PART_ROWS, part_width), lambda p: (p, 0, 0)),
+            stats_spec,
+        ],
+        out_shape=[
+            shape((half // LANES, block_len, width), low),
+            shape((parts, PART_ROWS, part_width), wide),
+            shape((steps, 3, 8, 2 * block_len), wide),
+        ],
+        scratch_shapes=[pltpu.VMEM((9 * block_len, 2 * block_len), wide)],
+        compiler_params=params,
+        cost_estimate=pl.CostEstimate(
+            flops=5 * flops, bytes_accessed=5 << 20, transcendentals=exps
+        ),
+    )(live, query, dout, grad, *near)
+    backward = pl.pallas_call(
+        backward_kernel,
+        grid=(steps,),
+        in_specs=[scalars, one, one] + of_near + [stats_spec],
         out_specs=[
             one,
             pl.BlockSpec((6, block_len, LANES), lambda p: (0, 0, p)),
-            pl.BlockSpec((half // LANES, block_len, LANES), lambda p: (0, 0, p)),
             six,
             four,
             two,
-            pl.BlockSpec((parts // steps, PART_ROWS, part_width), lambda p: (p, 0, 0)),
         ],
         out_shape=[
             shape((block_len, width), low),
             shape((6, block_len, width), low),
-            shape((half // LANES, block_len, width), low),
             shape((3, 2, block_len, width), wide),
             shape((2, 2, block_len, width), low),
             shape((2, block_len, width), wide),
-            shape((parts, PART_ROWS, part_width), wide),
-        ],
-        scratch_shapes=[pltpu.VMEM((9 * block_len, 2 * block_len), wide)],
+        ],
         compiler_params=pltpu.CompilerParams(
-            dimension_semantics=("arbitrary",), vmem_limit_bytes=24 << 20
+            dimension_semantics=("arbitrary",), vmem_limit_bytes=60 << 20
         ),
         cost_estimate=pl.CostEstimate(
-            flops=12 * 9 * block_len * block_len * width * 2,
-            bytes_accessed=8 << 20,
-            transcendentals=9 * block_len * block_len * (width // HDIM),
-        ),
-    )(live, query, dout, grad, *near)
+            flops=10 * flops, bytes_accessed=6 << 20, transcendentals=exps
+        ),
+    )(live, query, dout, *near, stats)
+    return w_given, w_own, backward
 
 
 def chip_sum_kernel(given, own_column, far_ends, send_p, send_q, own_sum):
@@ -259,7 +277,7 @@
         compiler_params=pltpu.CompilerParams(
             dimension_semantics=("arbitrary",), vmem_limit_bytes=8 << 20
         ),
-        cost_estimate=pl.CostEstimate(flops=60_000_000_000, bytes_accessed=4 << 20, transcendentals=0),
+        cost_estimate=pl.CostEstimate(flops=100_000_000, bytes_accessed=4 << 20, transcendentals=0),
     )(own_sum, far_middle, from_p, from_q)
 
 
@@ -354,10 +372,11 @@
     partner = partner_of(jnp.stack((own, near_p, near_q)))
     far_p, far_q = lat_mates_of(far)
     parts = opt_count * lat_count
-    grad_query, to_partner, w_given, own_column, far_ends, far_middle, w_own = attention(
+    w_given, w_own, backward = attention(
         live, query, dout, grad, (key, value, partner, far, near_p, far_p, near_q, far_q), parts
     )
 
+    grad_query, to_partner, own_column, far_ends, far_middle = backward
     to_p, to_q, own_sum = chip_sum(partner_of(to_partner), own_column, far_ends)
     w_parts = weight_sum(partner_of(w_given), w_own)
     from_p, from_q = exchange(to_p, "lat", next_door), exchange(to_q, "lat", other_door)

time: 143 us -> 147 us (1.028)
  waiting for transfers between devices: 25.1 us -> 28.9 us
    ppermute x11, waiting for transfers between devices: 5.8 us -> 21.1 us  [exchange(): lax.ppermute(array, axis, [(i, j) for i, j in pairs if 0 <= j < lax.axis_...]
    all_to_all x1, waiting for transfers between devices: 11.5 us -> 0.01 us  [shards(): w_part = lax.all_to_all(w_parts, ('opt', 'lat'), 0, 0)]
    pallas_call x1 -> x2, Pallas kernels: 9.23 us -> 12.5 us  [the longest x1 6.58 us: attention(): pl.pallas_call(backward_kernel, grid=(steps,), in_specs=[scalars, one, on...]
    pallas_call x1, Pallas kernels: 2.24 us -> 0.66 us  [lat_sum(): pl.pallas_call(lat_sum_kernel, grid=(width // LANES,), in_specs=[two, two...]
    all_to_all x1, starting transfers between devices: 15.9 us -> 14.4 us  [shards(): w_part = lax.all_to_all(w_parts, ('opt', 'lat'), 0, 0)]
  transfers between devices with their start and end apart: 13 -> 13, of which waited for: 4 -> 6; matrix products, arithmetic and copies ran while one was open for 2% -> 2% of each run, Pallas kernels for 5% -> 6%
where the time goes in v6:
time: 147 us; the launch traced here: 146 us
  starting transfers between devices  75.1 us (51%)
  waiting for transfers between devices  28.9 us (20%)
  Pallas kernels  17.1 us (12%)
  blocking collectives  16.9 us (11%)
  local copies, waits for them, and re-layouts  4.34 us (3%)
  other arithmetic  2.26 us (2%)
    ppermute x11, starting transfers between devices, exchange(): lax.ppermute(array, axis, [(i, j) for i, j in pairs if 0 <= j < lax.axis_...  52 us
    ppermute x11, waiting for transfers between devices, exchange(): lax.ppermute(array, axis, [(i, j) for i, j in pairs if 0 <= j < lax.axis_...  21.1 us
    all_to_all x1, blocking collectives, shards(): w_part = lax.all_to_all(w_part, 'lon', 0, 0, axis_index_groups=cores)  16.9 us
    all_to_all x1, starting transfers between devices, shards(): w_part = lax.all_to_all(w_parts, ('opt', 'lat'), 0, 0)  14.4 us
    all_to_all x1, starting transfers between devices, shards(): lax.all_to_all(w_part, ('lat', 'lon'), 0, 0, axis_index_groups=chips)  8.71 us
    all_to_all x1, waiting for transfers between devices, shards(): lax.all_to_all(w_part, ('lat', 'lon'), 0, 0, axis_index_groups=chips)  7.74 us
    pallas_call x1, Pallas kernels, attention(): pl.pallas_call(backward_kernel, grid=(steps,), in_specs=[scalars, one, on...  6.58 us
    pallas_call x1, Pallas kernels, attention(): pl.pallas_call(forward_kernel, grid=(steps,), in_specs=[scalars, one, one...  5.89 us
  transfers between devices with their start and end apart: 13, of which 6 were waited for; matrix products, arithmetic and copies ran while one was open for 2% of the time, Pallas kernels for 6%

profile of v6, /device:TPU:1, one launch (start us, length us, event | category | flops | bytes accessed | tf_op | source)
XLA Modules:
  0.0 146.1 jit_solution(44271931227663316)
XLA Ops:
  0.7 1.8 %fusion.7 = (bf16[1,2,128,512]{3,2,1,0:T(8,128)(2,1)S(1)}, bf16[2,128,512]{2,1,0:T(8,128)(2,1)}) fusion(bf16[1,128,512]{2,1,0:T(8,128)(2,1)} %bitcast.25, bf16[1,128,512]{2,1,0:T(8,128)(2,1)} %bitcast.22), kind=kLoop, calls=%fused_computation.23 | loop fusion | flops 131072 | bytes 786432 | tf_op jit(solution)/shard_map/stack | solution.py:372
  3.3 6.4 %collective-permute-start = (bf16[2,128,512]{2,1,0:T(8,128)(2,1)}, bf16[2,128,512]{2,1,0:T(8,128)(2,1)S(1)}, u32[]{:S(2)}, u32[]{:S(2)}) collective-permute-start(bf16[2,128,512]{2,1,0:T(8,128)(2,1)} %get-tuple-element.33), channel_id=1, source_target_pairs={{0,48},{48,0},{96,144},{144,96},{192,240},{240,192},{288,336},{336... | collective-permute-start | bytes 786440 | tf_op jit(solution)/shard_map/ppermute | solution.py:17
  9.7 11.8 %collective-permute-start.3 = (bf16[2,128,512]{2,1,0:T(8,128)(2,1)}, bf16[2,128,512]{2,1,0:T(8,128)(2,1)S(1)}, u32[]{:S(2)}, u32[]{:S(2)}) collective-permute-start(bf16[2,128,512]{2,1,0:T(8,128)(2,1)} %get-tuple-element.33), channel_id=1, source_target_pairs={{0,40},{8,16},{16,8},{24,32},{32,24},{40,0},{1,41},{9,17},{17,9},{... | collective-permute-start | bytes 786440 | tf_op jit(solution)/shard_map/ppermute | solution.py:17
  21.5 1.1 dynamic-slice_reduce_fusion
  22.7 4.8 %collective-permute-start.2 = (bf16[3,2,128,512]{3,2,1,0:T(8,128)(2,1)S(1)}, bf16[3,2,128,512]{3,2,1,0:T(8,128)(2,1)S(1)}, u32[]{:S(2)}, u32[]{:S(2)}) collective-permute-start(bf16[3,2,128,512]{3,2,1,0:T(8,128)(2,1)S(1)} %pad_maximum_fusion), channel_id=1, source_target_pairs={{0,8},{8,0},{16,24},{24,16},{32,40},{40,32},{1,9},{9,1},{17,25},{2... | collective-permute-start | bytes 2359304 | tf_op jit(solution)/shard_map/ppermute | solution.py:17
  27.8 2.8 %collective-permute-done.3.refs_1_ = bf16[2,128,512]{2,1,0:T(8,128)(2,1)S(1)} collective-permute-done((bf16[2,128,512]{2,1,0:T(8,128)(2,1)}, bf16[2,128,512]{2,1,0:T(8,128)(2,1)S(1)}, u32[]{:S(2)}, u32[]{:S(2)}) %collective-permute-start.3) | collective-permute-done | bytes 262176 | tf_op jit(solution)/shard_map/ppermute | solution.py:17
  31.2 4.9 %collective-permute-start.4 = (bf16[2,128,512]{2,1,0:T(8,128)(2,1)S(1)}, bf16[2,128,512]{2,1,0:T(8,128)(2,1)S(1)}, u32[]{:S(2)}, u32[]{:S(2)}) collective-permute-start(bf16[2,128,512]{2,1,0:T(8,128)(2,1)S(1)} %collective-permute-done.3.refs_1_), channel_id=1, source_target_pairs={{0,48},{48,0},{96,144},{144,96},{192,240},{240,192},{288,336},{336... | collective-permute-start | bytes 786440 | tf_op jit(solution)/shard_map/ppermute | solution.py:17
  36.7 3.1 %collective-permute-done.4.refs_3_ = bf16[2,128,512]{2,1,0:T(8,128)(2,1)S(1)} collective-permute-done((bf16[2,128,512]{2,1,0:T(8,128)(2,1)S(1)}, bf16[2,128,512]{2,1,0:T(8,128)(2,1)S(1)}, u32[]{:S(2)}, u32[]{:S(2)}) %collective-permute-start.4) | collective-permute-done | bytes 262176 | tf_op jit(solution)/shard_map/ppermute | solution.py:17
  39.9 5.9 %shard_map.93 = (bf16[4,128,512]{2,1,0:T(8,128)(2,1)S(1)}, f32[128,8,256]{2,1,0:T(8,128)S(1)}, f32[4,3,8,256]{3,2,1,0:T(8,128)S(1)}) custom-call(s32[10]{0:T(128)S(1)} %pad_add_fusion.live, bf16[128,512]{1,0:T(8,128)(2,1)S(1)} %bitcast.29, bf16[128,512]{1,0:T(8,128)(2,1)S(1)} %convolution_convert_fusion.dout, bf16[128,1024]{1,0:T(8,128)(2,1)S(1)} %bitcast.19, ...), custom_call_target="tpu_custom_call" | custom-call | flops 1509949440 | bytes 5242880 | tf_op jit(solution)/shard_map/pallas_call | solution.py:172
  45.9 9.8 %collective-permute-start.10 = (bf16[4,128,512]{2,1,0:T(8,128)(2,1)S(1)}, bf16[4,128,512]{2,1,0:T(8,128)(2,1)S(1)}, u32[]{:S(2)}, u32[]{:S(2)}) collective-permute-start(bf16[4,128,512]{2,1,0:T(8,128)(2,1)S(1)} %get-tuple-element.28), channel_id=1, source_target_pairs={{0,8},{8,0},{16,24},{24,16},{32,40},{40,32},{1,9},{9,1},{17,25},{2... | collective-permute-start | bytes 1572872 | tf_op jit(solution)/shard_map/ppermute | solution.py:17
  55.7 1.5 %collective-permute-done.10.given = bf16[4,128,512]{2,1,0:T(8,128)(2,1)S(1)} collective-permute-done((bf16[4,128,512]{2,1,0:T(8,128)(2,1)S(1)}, bf16[4,128,512]{2,1,0:T(8,128)(2,1)S(1)}, u32[]{:S(2)}, u32[]{:S(2)}) %collective-permute-start.10) | collective-permute-done | bytes 524320 | tf_op jit(solution)/shard_map/ppermute | solution.py:17
  57.2 1.5 %shard_map.97 = bf16[128,8,256]{2,1,0:T(8,128)(2,1)} custom-call(bf16[4,128,512]{2,1,0:T(8,128)(2,1)S(1)} %collective-permute-done.10.given, f32[128,8,256]{2,1,0:T(8,128)S(1)} %get-tuple-element.29.w_own), custom_call_target="tpu_custom_call" | custom-call | flops 262144 | bytes 2097152 | tf_op jit(solution)/shard_map/pallas_call | solution.py:299
  58.7 14.4 %all-to-all-start = ((bf16[128,8,256]{2,1,0:T(8,128)(2,1)}), bf16[128,8,256]{2,1,0:T(8,128)(2,1)S(1)}, u32[]{:S(2)}, u32[]{:S(2)}) async-start(bf16[128,8,256]{2,1,0:T(8,128)(2,1)} %shard_map.97), calls=%async_computation | async-start | bytes 1048576 | tf_op jit(solution)/shard_map/all_to_all | solution.py:391
  73.1 6.6 %shard_map.94 = (bf16[128,512]{1,0:T(8,128)(2,1)}, bf16[6,128,512]{2,1,0:T(8,128)(2,1)}, f32[3,2,128,512]{3,2,1,0:T(8,128)}, bf16[2,2,128,512]{3,2,1,0:T(8,128)(2,1)}, f32[2,128,512]{2,1,0:T(8,128)}) custom-call(s32[10]{0:T(128)} %copy-done.15, bf16[128,512]{1,0:T(8,128)(2,1)} %bitcast.28, bf16[128,512]{1,0:T(8,128)(2,1)} %copy-done.9, ...), custom_call_target="tpu_custom_call" | custom-call | flops 3019898880 | bytes 6291456 | tf_op jit(solution)/shard_map/pallas_call | solution.py:194
  79.7 2.6 %collective-permute-start.6 = (bf16[6,128,512]{2,1,0:T(8,128)(2,1)}, bf16[6,128,512]{2,1,0:T(8,128)(2,1)S(1)}, u32[]{:S(2)}, u32[]{:S(2)}) collective-permute-start(bf16[6,128,512]{2,1,0:T(8,128)(2,1)} %get-tuple-element.19), channel_id=1, source_target_pairs={{0,8},{8,0},{16,24},{24,16},{32,40},{40,32},{1,9},{9,1},{17,25},{2... | collective-permute-start | bytes 2359304 | tf_op jit(solution)/shard_map/ppermute | solution.py:17
  82.2 2.1 %collective-permute-done.6.given = bf16[6,128,512]{2,1,0:T(8,128)(2,1)S(1)} collective-permute-done((bf16[6,128,512]{2,1,0:T(8,128)(2,1)}, bf16[6,128,512]{2,1,0:T(8,128)(2,1)S(1)}, u32[]{:S(2)}, u32[]{:S(2)}) %collective-permute-start.6) | collective-permute-done | bytes 786464 | tf_op jit(solution)/shard_map/ppermute | solution.py:17
  84.3 1.4 copy-done.1
  85.8 1.0 copy-done.3
  87.7 2.8 %collective-permute-start.7 = (bf16[2,2,128,512]{3,2,1,0:T(8,128)(2,1)S(1)}, bf16[2,2,128,512]{3,2,1,0:T(8,128)(2,1)S(1)}, u32[]{:S(2)}, u32[]{:S(2)}) collective-permute-start(bf16[2,2,128,512]{3,2,1,0:T(8,128)(2,1)S(1)} %get-tuple-element.24), channel_id=1, source_target_pairs={{0,48},{48,0},{96,144},{144,96},{192,240},{240,192},{288,336},{336... | collective-permute-start | bytes 1572872 | tf_op jit(solution)/shard_map/ppermute | solution.py:17
  91.2 11.6 %collective-permute-done.7.from_p = bf16[2,2,128,512]{3,2,1,0:T(8,128)(2,1)S(1)} collective-permute-done((bf16[2,2,128,512]{3,2,1,0:T(8,128)(2,1)S(1)}, bf16[2,2,128,512]{3,2,1,0:T(8,128)(2,1)S(1)}, u32[]{:S(2)}, u32[]{:S(2)}) %collective-permute-start.7) | collective-permute-done | bytes 524320 | tf_op jit(solution)/shard_map/ppermute | solution.py:17
  103.4 6.9 %collective-permute-start.9 = (bf16[2,128,512]{2,1,0:T(8,128)(2,1)S(1)}, bf16[2,128,512]{2,1,0:T(8,128)(2,1)S(1)}, u32[]{:S(2)}, u32[]{:S(2)}) collective-permute-start(bf16[2,128,512]{2,1,0:T(8,128)(2,1)S(1)} %get-tuple-element.27), channel_id=1, source_target_pairs={{0,40},{8,16},{16,8},{24,32},{32,24},{40,0},{1,41},{9,17},{17,9},{... | collective-permute-start | bytes 786440 | tf_op jit(solution)/shard_map/ppermute | solution.py:17
  110.5 16.9 %all_to_all.15.terms = f32[3,8,256]{2,1,0:T(8,128)S(1)} all-to-all(f32[3,8,256]{2,1,0:T(8,128)S(1)} %shard_map.98), channel_id=1, replica_groups={{0,16,32},{8,24,40},{1,17,33},{9,25,41},{2,18,34},{10,26,42},{3,19,35},..., dimensions={0} | all-to-all | bytes 49152 | tf_op jit(solution)/shard_map/all_to_all | solution.py:393
  128.1 8.7 %all-to-all-start.2 = ((bf16[32,8,256]{2,1,0:T(8,128)(2,1)}), bf16[32,8,256]{2,1,0:T(8,128)(2,1)S(1)}, u32[]{:S(2)}, u32[]{:S(2)}) async-start(bf16[32,8,256]{2,1,0:T(8,128)(2,1)} %shard_map.99), calls=%async_computation.2 | async-start | bytes 262144 | tf_op jit(solution)/shard_map/all_to_all | solution.py:395
  137.6 7.7 %all-to-all-done.2.pieces = bf16[32,8,256]{2,1,0:T(8,128)(2,1)S(1)} async-done(((bf16[32,8,256]{2,1,0:T(8,128)(2,1)}), bf16[32,8,256]{2,1,0:T(8,128)(2,1)S(1)}, u32[]{:S(2)}, u32[]{:S(2)}) %all-to-all-start.2) | async-done | bytes 131104 | tf_op jit(solution)/shard_map/all_to_all | solution.py:395
  (55 shorter events, 7.0 us)
Async XLA Ops:
  0.6 35.6 %copy-start = (bf16[512,1024]{1,0:T(8,128)(2,1)S(1)}, bf16[512,1024]{1,0:T(8,128)(2,1)}, u32[]{:S(2)}) copy-start(bf16[512,1024]{1,0:T(8,128)(2,1)} %param.10) | copy-start | bytes 3145732
  0.6 35.5 %copy-start.4 = (bf16[1,1,1,128,1024]{4,3,2,1,0:T(8,128)(2,1)S(1)}, bf16[1,1,1,128,1024]{4,3,2,1,0:T(8,128)(2,1)}, u32[]{:S(2)}) copy-start(bf16[1,1,1,128,1024]{4,3,2,1,0:T(8,128)(2,1)} %param.9) | copy-start | bytes 786436
  2.5 37.4 %copy-start.7 = (bf16[1,1,1,128,512]{4,3,2,1,0:T(8,128)(2,1)S(1)}, bf16[1,1,1,128,512]{4,3,2,1,0:T(8,128)(2,1)}, u32[]{:S(2)}) copy-start(bf16[1,1,1,128,512]{4,3,2,1,0:T(8,128)(2,1)} %param.7) | copy-start | bytes 393220
  2.5 37.4 %copy-start.8 = (bf16[1,1,1,128,512]{4,3,2,1,0:T(8,128)(2,1)S(1)}, bf16[1,1,1,128,512]{4,3,2,1,0:T(8,128)(2,1)}, u32[]{:S(2)}) copy-start(bf16[1,1,1,128,512]{4,3,2,1,0:T(8,128)(2,1)} %param.8) | copy-start | bytes 393220
  2.5 37.4 %copy-start.14 = (bf16[1,1,1,128,512]{4,3,2,1,0:T(8,128)(2,1)S(1)}, bf16[1,1,1,128,512]{4,3,2,1,0:T(8,128)(2,1)}, u32[]{:S(2)}) copy-start(bf16[1,1,1,128,512]{4,3,2,1,0:T(8,128)(2,1)} %param.6) | copy-start | bytes 393220
  2.5 20.1 %collective-permute-start.1 = (bf16[2,128,512]{2,1,0:T(8,128)(2,1)}, bf16[2,128,512]{2,1,0:T(8,128)(2,1)S(1)}, u32[]{:S(2)}, u32[]{:S(2)}) collective-permute-start(bf16[2,128,512]{2,1,0:T(8,128)(2,1)} %get-tuple-element.33), channel_id=1, source_target_pairs={{48,96},{96,48},{144,192},{192,144},{240,288},{288,240},{336,384},... | collective-permute-start | bytes 786440 | tf_op jit(solution)/shard_map/ppermute | solution.py:17
  3.3 19.3 %collective-permute-start = (bf16[2,128,512]{2,1,0:T(8,128)(2,1)}, bf16[2,128,512]{2,1,0:T(8,128)(2,1)S(1)}, u32[]{:S(2)}, u32[]{:S(2)}) collective-permute-start(bf16[2,128,512]{2,1,0:T(8,128)(2,1)} %get-tuple-element.33), channel_id=1, source_target_pairs={{0,48},{48,0},{96,144},{144,96},{192,240},{240,192},{288,336},{336... | collective-permute-start | bytes 786440 | tf_op jit(solution)/shard_map/ppermute | solution.py:17
  9.7 20.9 %collective-permute-start.3 = (bf16[2,128,512]{2,1,0:T(8,128)(2,1)}, bf16[2,128,512]{2,1,0:T(8,128)(2,1)S(1)}, u32[]{:S(2)}, u32[]{:S(2)}) collective-permute-start(bf16[2,128,512]{2,1,0:T(8,128)(2,1)} %get-tuple-element.33), channel_id=1, source_target_pairs={{0,40},{8,16},{16,8},{24,32},{32,24},{40,0},{1,41},{9,17},{17,9},{... | collective-permute-start | bytes 786440 | tf_op jit(solution)/shard_map/ppermute | solution.py:17
  22.6 23.2 %copy-start.5 = (bf16[2,128,512]{2,1,0:T(8,128)(2,1)}, bf16[2,128,512]{2,1,0:T(8,128)(2,1)S(1)}, u32[]{:S(2)}) copy-start(bf16[2,128,512]{2,1,0:T(8,128)(2,1)S(1)} %collective-permute-done.1.refs_4_) | copy-start | bytes 786436
  22.6 23.2 %copy-start.6 = (bf16[2,128,512]{2,1,0:T(8,128)(2,1)}, bf16[2,128,512]{2,1,0:T(8,128)(2,1)S(1)}, u32[]{:S(2)}) copy-start(bf16[2,128,512]{2,1,0:T(8,128)(2,1)S(1)} %collective-permute-done.refs_2_) | copy-start | bytes 786436
  22.7 17.1 %collective-permute-start.2 = (bf16[3,2,128,512]{3,2,1,0:T(8,128)(2,1)S(1)}, bf16[3,2,128,512]{3,2,1,0:T(8,128)(2,1)S(1)}, u32[]{:S(2)}, u32[]{:S(2)}) collective-permute-start(bf16[3,2,128,512]{3,2,1,0:T(8,128)(2,1)S(1)} %pad_maximum_fusion), channel_id=1, source_target_pairs={{0,8},{8,0},{16,24},{24,16},{32,40},{40,32},{1,9},{9,1},{17,25},{2... | collective-permute-start | bytes 2359304 | tf_op jit(solution)/shard_map/ppermute | solution.py:17
  30.6 15.2 %copy-start.11 = (bf16[2,128,512]{2,1,0:T(8,128)(2,1)}, bf16[2,128,512]{2,1,0:T(8,128)(2,1)S(1)}, u32[]{:S(2)}) copy-start(bf16[2,128,512]{2,1,0:T(8,128)(2,1)S(1)} %collective-permute-done.3.refs_1_) | copy-start | bytes 786436
  30.6 6.1 %collective-permute-start.5 = (bf16[2,128,512]{2,1,0:T(8,128)(2,1)S(1)}, bf16[2,128,512]{2,1,0:T(8,128)(2,1)S(1)}, u32[]{:S(2)}, u32[]{:S(2)}) collective-permute-start(bf16[2,128,512]{2,1,0:T(8,128)(2,1)S(1)} %collective-permute-done.3.refs_1_), channel_id=1, source_target_pairs={{48,96},{96,48},{144,192},{192,144},{240,288},{288,240},{336,384},... | collective-permute-start | bytes 786440 | tf_op jit(solution)/shard_map/ppermute | solution.py:17
  31.2 8.6 %collective-permute-start.4 = (bf16[2,128,512]{2,1,0:T(8,128)(2,1)S(1)}, bf16[2,128,512]{2,1,0:T(8,128)(2,1)S(1)}, u32[]{:S(2)}, u32[]{:S(2)}) collective-permute-start(bf16[2,128,512]{2,1,0:T(8,128)(2,1)S(1)} %collective-permute-done.3.refs_1_), channel_id=1, source_target_pairs={{0,48},{48,0},{96,144},{144,96},{192,240},{240,192},{288,336},{336... | collective-permute-start | bytes 786440 | tf_op jit(solution)/shard_map/ppermute | solution.py:17
  36.2 9.6 %copy-start.15 = (s32[10]{0:T(128)}, s32[10]{0:T(128)S(1)}, u32[]{:S(2)}) copy-start(s32[10]{0:T(128)S(1)} %pad_add_fusion.live) | copy-start | bytes 124
  45.9 12.8 %copy-start.16 = (f32[4,3,8,256]{3,2,1,0:T(8,128)}, f32[4,3,8,256]{3,2,1,0:T(8,128)S(1)}, u32[]{:S(2)}) copy-start(f32[4,3,8,256]{3,2,1,0:T(8,128)S(1)} %get-tuple-element.17.refs_6_) | copy-start | bytes 294916
  45.9 11.3 %collective-permute-start.10 = (bf16[4,128,512]{2,1,0:T(8,128)(2,1)S(1)}, bf16[4,128,512]{2,1,0:T(8,128)(2,1)S(1)}, u32[]{:S(2)}, u32[]{:S(2)}) collective-permute-start(bf16[4,128,512]{2,1,0:T(8,128)(2,1)S(1)} %get-tuple-element.28), channel_id=1, source_target_pairs={{0,8},{8,0},{16,24},{24,16},{32,40},{40,32},{1,9},{9,1},{17,25},{2... | collective-permute-start | bytes 1572872 | tf_op jit(solution)/shard_map/ppermute | solution.py:17
  58.7 51.6 %all-to-all-start = ((bf16[128,8,256]{2,1,0:T(8,128)(2,1)}), bf16[128,8,256]{2,1,0:T(8,128)(2,1)S(1)}, u32[]{:S(2)}, u32[]{:S(2)}) async-start(bf16[128,8,256]{2,1,0:T(8,128)(2,1)} %shard_map.97), calls=%async_computation | async-start | bytes 1048576 | tf_op jit(solution)/shard_map/all_to_all | solution.py:391
  79.7 4.7 %collective-permute-start.6 = (bf16[6,128,512]{2,1,0:T(8,128)(2,1)}, bf16[6,128,512]{2,1,0:T(8,128)(2,1)S(1)}, u32[]{:S(2)}, u32[]{:S(2)}) collective-permute-start(bf16[6,128,512]{2,1,0:T(8,128)(2,1)} %get-tuple-element.19), channel_id=1, source_target_pairs={{0,8},{8,0},{16,24},{24,16},{32,40},{40,32},{1,9},{9,1},{17,25},{2... | collective-permute-start | bytes 2359304 | tf_op jit(solution)/shard_map/ppermute | solution.py:17
  86.8 15.9 %copy-start.2 = (f32[2,128,512]{2,1,0:T(8,128)S(1)}, f32[2,128,512]{2,1,0:T(8,128)}, u32[]{:S(2)}) copy-start(f32[2,128,512]{2,1,0:T(8,128)} %get-tuple-element.23.far_middle) | copy-start | bytes 1572868
  87.7 15.0 %collective-permute-start.7 = (bf16[2,2,128,512]{3,2,1,0:T(8,128)(2,1)S(1)}, bf16[2,2,128,512]{3,2,1,0:T(8,128)(2,1)S(1)}, u32[]{:S(2)}, u32[]{:S(2)}) collective-permute-start(bf16[2,2,128,512]{3,2,1,0:T(8,128)(2,1)S(1)} %get-tuple-element.24), channel_id=1, source_target_pairs={{0,48},{48,0},{96,144},{144,96},{192,240},{240,192},{288,336},{336... | collective-permute-start | bytes 1572872 | tf_op jit(solution)/shard_map/ppermute | solution.py:17
  90.5 12.3 %collective-permute-start.8 = (bf16[2,2,128,512]{3,2,1,0:T(8,128)(2,1)S(1)}, bf16[2,2,128,512]{3,2,1,0:T(8,128)(2,1)S(1)}, u32[]{:S(2)}, u32[]{:S(2)}) collective-permute-start(bf16[2,2,128,512]{3,2,1,0:T(8,128)(2,1)S(1)} %get-tuple-element.25), channel_id=1, source_target_pairs={{48,96},{96,48},{144,192},{192,144},{240,288},{288,240},{336,384},... | collective-permute-start | bytes 1572872 | tf_op jit(solution)/shard_map/ppermute | solution.py:17
  103.4 33.4 %collective-permute-start.9 = (bf16[2,128,512]{2,1,0:T(8,128)(2,1)S(1)}, bf16[2,128,512]{2,1,0:T(8,128)(2,1)S(1)}, u32[]{:S(2)}, u32[]{:S(2)}) collective-permute-start(bf16[2,128,512]{2,1,0:T(8,128)(2,1)S(1)} %get-tuple-element.27), channel_id=1, source_target_pairs={{0,40},{8,16},{16,8},{24,32},{32,24},{40,0},{1,41},{9,17},{17,9},{... | collective-permute-start | bytes 786440 | tf_op jit(solution)/shard_map/ppermute | solution.py:17
  128.1 17.3 %all-to-all-start.2 = ((bf16[32,8,256]{2,1,0:T(8,128)(2,1)}), bf16[32,8,256]{2,1,0:T(8,128)(2,1)S(1)}, u32[]{:S(2)}, u32[]{:S(2)}) async-start(bf16[32,8,256]{2,1,0:T(8,128)(2,1)} %shard_map.99), calls=%async_computation.2 | async-start | bytes 262144 | tf_op jit(solution)/shard_map/all_to_all | solution.py:395
  (6 other events, 32.7 us)

commit v7 on v6

--- a/solution.py
+++ b/solution.py
@@ -380,9 +380,6 @@
     to_p, to_q, own_sum = chip_sum(partner_of(to_partner), own_column, far_ends)
     w_parts = weight_sum(partner_of(w_given), w_own)
     from_p, from_q = exchange(to_p, "lat", next_door), exchange(to_q, "lat", other_door)
-    owned, far_sum = lat_sum(own_sum, far_middle, from_p, from_q)
-    owned = (owned + far_of(far_sum).astype(wide)).astype(low)
-
     cores = [list(range(core, lon_count, 2)) for core in range(2)]
     chips = [
         [lat * lon_count + chip + core for lat in range(lat_count) for core in range(2)]
@@ -391,9 +388,12 @@
     w_part = lax.all_to_all(w_parts, ("opt", "lat"), 0, 0)
     w_part = sum_and_copy(w_part, len(cores[0]), wide)
     w_part = lax.all_to_all(w_part, "lon", 0, 0, axis_index_groups=cores)
+    from_p, from_q, w_part = lax.optimization_barrier((from_p, from_q, w_part))
+    owned, far_sum = lat_sum(own_sum, far_middle, from_p, from_q)
     w_part = sum_and_copy(w_part, len(chips[0]), low)
     w_part = lax.all_to_all(w_part, ("lat", "lon"), 0, 0, axis_index_groups=chips)
     grad_weight = assemble(w_part, att_width // opt_count, model_width)
+    owned = (owned + far_of(far_sum).astype(wide)).astype(low)
 
     return (
         grad_query[None, None, None],

time: 147 us -> 137 us (0.932)
  blocking collectives: 16.9 us -> 0 us
  starting transfers between devices: 75.1 us -> 82.8 us
  waiting for transfers between devices: 28.9 us -> 24.9 us
  Pallas kernels: 17.1 us -> 20.3 us
    all_to_all x1 -> x0, blocking collectives: 16.9 us -> none  [shards(): w_part = lax.all_to_all(w_part, 'lon', 0, 0, axis_index_groups=cores)]
    ppermute x11, waiting for transfers between devices: 21.1 us -> 13.8 us  [exchange(): lax.ppermute(array, axis, [(i, j) for i, j in pairs if 0 <= j < lax.axis_...]
    all_to_all x0 -> x1, starting transfers between devices: none -> 6.05 us  [shards(): w_part = lax.all_to_all(w_part, 'lon', 0, 0, axis_index_groups=cores)]
    all_to_all x0 -> x1, waiting for transfers between devices: none -> 2.53 us  [shards(): w_part = lax.all_to_all(w_part, 'lon', 0, 0, axis_index_groups=cores)]
    pallas_call x1, Pallas kernels: 0.66 us -> 2.24 us  [lat_sum(): pl.pallas_call(lat_sum_kernel, grid=(width // LANES,), in_specs=[two, two...]
  transfers between devices with their start and end apart: 13 -> 14, of which waited for: 6 -> 7; matrix products, arithmetic and copies ran while one was open for 2% -> 2% of each run, Pallas kernels for 6% -> 7%
where the time goes in v7:
time: 137 us; the launch traced here: 136 us
  starting transfers between devices  82.8 us (60%)
  waiting for transfers between devices  24.9 us (18%)
  Pallas kernels  20.3 us (15%)
  local copies, waits for them, and re-layouts  4.34 us (3%)
  other arithmetic  2.26 us (2%)
    ppermute x11, starting transfers between devices, exchange(): lax.ppermute(array, axis, [(i, j) for i, j in pairs if 0 <= j < lax.axis_...  53 us
    all_to_all x1, starting transfers between devices, shards(): w_part = lax.all_to_all(w_parts, ('opt', 'lat'), 0, 0)  14.4 us
    ppermute x11, waiting for transfers between devices, exchange(): lax.ppermute(array, axis, [(i, j) for i, j in pairs if 0 <= j < lax.axis_...  13.8 us
    all_to_all x1, starting transfers between devices, shards(): lax.all_to_all(w_part, ('lat', 'lon'), 0, 0, axis_index_groups=chips)  9.39 us
    all_to_all x1, waiting for transfers between devices, shards(): lax.all_to_all(w_part, ('lat', 'lon'), 0, 0, axis_index_groups=chips)  8.6 us
    pallas_call x1, Pallas kernels, attention(): pl.pallas_call(backward_kernel, grid=(steps,), in_specs=[scalars, one, on...  6.56 us
    all_to_all x1, starting transfers between devices, shards(): w_part = lax.all_to_all(w_part, 'lon', 0, 0, axis_index_groups=cores)  6.05 us
    pallas_call x1, Pallas kernels, attention(): pl.pallas_call(forward_kernel, grid=(steps,), in_specs=[scalars, one, one...  5.89 us
  transfers between devices with their start and end apart: 14, of which 7 were waited for; matrix products, arithmetic and copies ran while one was open for 2% of the time, Pallas kernels for 7%

profile of v7, /device:TPU:1, one launch (start us, length us, event | category | flops | bytes accessed | tf_op | source)
XLA Modules:
  0.0 136.1 jit_solution(15424090993680413683)
XLA Ops:
  0.7 1.8 %fusion.7 = (bf16[1,2,128,512]{3,2,1,0:T(8,128)(2,1)S(1)}, bf16[2,128,512]{2,1,0:T(8,128)(2,1)}) fusion(bf16[1,128,512]{2,1,0:T(8,128)(2,1)} %bitcast.25, bf16[1,128,512]{2,1,0:T(8,128)(2,1)} %bitcast.22), kind=kLoop, calls=%fused_computation.23 | loop fusion | flops 131072 | bytes 786432 | tf_op jit(solution)/shard_map/stack | solution.py:372
  3.3 6.4 %collective-permute-start = (bf16[2,128,512]{2,1,0:T(8,128)(2,1)}, bf16[2,128,512]{2,1,0:T(8,128)(2,1)S(1)}, u32[]{:S(2)}, u32[]{:S(2)}) collective-permute-start(bf16[2,128,512]{2,1,0:T(8,128)(2,1)} %get-tuple-element.39), channel_id=1, source_target_pairs={{0,48},{48,0},{96,144},{144,96},{192,240},{240,192},{288,336},{336... | collective-permute-start | bytes 786440 | tf_op jit(solution)/shard_map/ppermute | solution.py:17
  9.7 11.8 %collective-permute-start.3 = (bf16[2,128,512]{2,1,0:T(8,128)(2,1)}, bf16[2,128,512]{2,1,0:T(8,128)(2,1)S(1)}, u32[]{:S(2)}, u32[]{:S(2)}) collective-permute-start(bf16[2,128,512]{2,1,0:T(8,128)(2,1)} %get-tuple-element.39), channel_id=1, source_target_pairs={{0,40},{8,16},{16,8},{24,32},{32,24},{40,0},{1,41},{9,17},{17,9},{... | collective-permute-start | bytes 786440 | tf_op jit(solution)/shard_map/ppermute | solution.py:17
  22.7 4.8 %collective-permute-start.2 = (bf16[3,2,128,512]{3,2,1,0:T(8,128)(2,1)S(1)}, bf16[3,2,128,512]{3,2,1,0:T(8,128)(2,1)S(1)}, u32[]{:S(2)}, u32[]{:S(2)}) collective-permute-start(bf16[3,2,128,512]{3,2,1,0:T(8,128)(2,1)S(1)} %pad_maximum_fusion), channel_id=1, source_target_pairs={{0,8},{8,0},{16,24},{24,16},{32,40},{40,32},{1,9},{9,1},{17,25},{2... | collective-permute-start | bytes 2359304 | tf_op jit(solution)/shard_map/ppermute | solution.py:17
  27.8 2.8 %collective-permute-done.3.refs_1_ = bf16[2,128,512]{2,1,0:T(8,128)(2,1)S(1)} collective-permute-done((bf16[2,128,512]{2,1,0:T(8,128)(2,1)}, bf16[2,128,512]{2,1,0:T(8,128)(2,1)S(1)}, u32[]{:S(2)}, u32[]{:S(2)}) %collective-permute-start.3) | collective-permute-done | bytes 262176 | tf_op jit(solution)/shard_map/ppermute | solution.py:17
  31.2 4.9 %collective-permute-start.4 = (bf16[2,128,512]{2,1,0:T(8,128)(2,1)S(1)}, bf16[2,128,512]{2,1,0:T(8,128)(2,1)S(1)}, u32[]{:S(2)}, u32[]{:S(2)}) collective-permute-start(bf16[2,128,512]{2,1,0:T(8,128)(2,1)S(1)} %collective-permute-done.3.refs_1_), channel_id=1, source_target_pairs={{0,48},{48,0},{96,144},{144,96},{192,240},{240,192},{288,336},{336... | collective-permute-start | bytes 786440 | tf_op jit(solution)/shard_map/ppermute | solution.py:17
  36.7 3.1 %collective-permute-done.4.refs_3_ = bf16[2,128,512]{2,1,0:T(8,128)(2,1)S(1)} collective-permute-done((bf16[2,128,512]{2,1,0:T(8,128)(2,1)S(1)}, bf16[2,128,512]{2,1,0:T(8,128)(2,1)S(1)}, u32[]{:S(2)}, u32[]{:S(2)}) %collective-permute-start.4) | collective-permute-done | bytes 262176 | tf_op jit(solution)/shard_map/ppermute | solution.py:17
  39.9 5.9 %shard_map.93 = (bf16[4,128,512]{2,1,0:T(8,128)(2,1)S(1)}, f32[128,8,256]{2,1,0:T(8,128)S(1)}, f32[4,3,8,256]{3,2,1,0:T(8,128)S(1)}) custom-call(s32[10]{0:T(128)S(1)} %pad_add_fusion.live, bf16[128,512]{1,0:T(8,128)(2,1)S(1)} %bitcast.29, bf16[128,512]{1,0:T(8,128)(2,1)S(1)} %convolution_convert_fusion.dout, bf16[128,1024]{1,0:T(8,128)(2,1)S(1)} %bitcast.19, ...), custom_call_target="tpu_custom_call" | custom-call | flops 1509949440 | bytes 5242880 | tf_op jit(solution)/shard_map/pallas_call | solution.py:172
  45.9 9.8 %collective-permute-start.9 = (bf16[4,128,512]{2,1,0:T(8,128)(2,1)S(1)}, bf16[4,128,512]{2,1,0:T(8,128)(2,1)S(1)}, u32[]{:S(2)}, u32[]{:S(2)}) collective-permute-start(bf16[4,128,512]{2,1,0:T(8,128)(2,1)S(1)} %get-tuple-element.29), channel_id=1, source_target_pairs={{0,8},{8,0},{16,24},{24,16},{32,40},{40,32},{1,9},{9,1},{17,25},{2... | collective-permute-start | bytes 1572872 | tf_op jit(solution)/shard_map/ppermute | solution.py:17
  55.7 1.5 %collective-permute-done.9.given = bf16[4,128,512]{2,1,0:T(8,128)(2,1)S(1)} collective-permute-done((bf16[4,128,512]{2,1,0:T(8,128)(2,1)S(1)}, bf16[4,128,512]{2,1,0:T(8,128)(2,1)S(1)}, u32[]{:S(2)}, u32[]{:S(2)}) %collective-permute-start.9) | collective-permute-done | bytes 524320 | tf_op jit(solution)/shard_map/ppermute | solution.py:17
  57.2 1.5 %shard_map.96 = bf16[128,8,256]{2,1,0:T(8,128)(2,1)} custom-call(bf16[4,128,512]{2,1,0:T(8,128)(2,1)S(1)} %collective-permute-done.9.given, f32[128,8,256]{2,1,0:T(8,128)S(1)} %get-tuple-element.30.w_own), custom_call_target="tpu_custom_call" | custom-call | flops 262144 | bytes 2097152 | tf_op jit(solution)/shard_map/pallas_call | solution.py:299
  58.7 14.4 %all-to-all-start = ((bf16[128,8,256]{2,1,0:T(8,128)(2,1)}), bf16[128,8,256]{2,1,0:T(8,128)(2,1)S(1)}, u32[]{:S(2)}, u32[]{:S(2)}) async-start(bf16[128,8,256]{2,1,0:T(8,128)(2,1)} %shard_map.96), calls=%async_computation | async-start | bytes 1048576 | tf_op jit(solution)/shard_map/all_to_all | solution.py:388
  73.1 6.6 %shard_map.94 = (bf16[128,512]{1,0:T(8,128)(2,1)}, bf16[6,128,512]{2,1,0:T(8,128)(2,1)}, f32[3,2,128,512]{3,2,1,0:T(8,128)}, bf16[2,2,128,512]{3,2,1,0:T(8,128)(2,1)}, f32[2,128,512]{2,1,0:T(8,128)}) custom-call(s32[10]{0:T(128)} %copy-done.15, bf16[128,512]{1,0:T(8,128)(2,1)} %bitcast.28, bf16[128,512]{1,0:T(8,128)(2,1)} %copy-done.9, ...), custom_call_target="tpu_custom_call" | custom-call | flops 3019898880 | bytes 6291456 | tf_op jit(solution)/shard_map/pallas_call | solution.py:194
  79.7 2.6 %collective-permute-start.6 = (bf16[6,128,512]{2,1,0:T(8,128)(2,1)}, bf16[6,128,512]{2,1,0:T(8,128)(2,1)S(1)}, u32[]{:S(2)}, u32[]{:S(2)}) collective-permute-start(bf16[6,128,512]{2,1,0:T(8,128)(2,1)} %get-tuple-element.22), channel_id=1, source_target_pairs={{0,8},{8,0},{16,24},{24,16},{32,40},{40,32},{1,9},{9,1},{17,25},{2... | collective-permute-start | bytes 2359304 | tf_op jit(solution)/shard_map/ppermute | solution.py:17
  82.2 2.1 %collective-permute-done.6.given = bf16[6,128,512]{2,1,0:T(8,128)(2,1)S(1)} collective-permute-done((bf16[6,128,512]{2,1,0:T(8,128)(2,1)}, bf16[6,128,512]{2,1,0:T(8,128)(2,1)S(1)}, u32[]{:S(2)}, u32[]{:S(2)}) %collective-permute-start.6) | collective-permute-done | bytes 786464 | tf_op jit(solution)/shard_map/ppermute | solution.py:17
  86.8 2.0 %shard_map.95 = (bf16[2,2,128,512]{3,2,1,0:T(8,128)(2,1)}, bf16[2,2,128,512]{3,2,1,0:T(8,128)(2,1)}, f32[2,128,512]{2,1,0:T(8,128)S(1)}) custom-call(bf16[6,128,512]{2,1,0:T(8,128)(2,1)S(1)} %collective-permute-done.6.given, f32[3,2,128,512]{3,2,1,0:T(8,128)S(1)} %copy-done.1, bf16[2,2,128,512]{3,2,1,0:T(8,128)(2,1)S(1)} %copy-done.3), custom_call_target="tpu_custom_call" | custom-call | flops 786432 | bytes 1966080 | tf_op jit(solution)/shard_map/pallas_call | solution.py:239
  88.8 2.7 %collective-permute-start.7 = (bf16[2,2,128,512]{3,2,1,0:T(8,128)(2,1)}, bf16[2,2,128,512]{3,2,1,0:T(8,128)(2,1)S(1)}, u32[]{:S(2)}, u32[]{:S(2)}) collective-permute-start(bf16[2,2,128,512]{3,2,1,0:T(8,128)(2,1)} %get-tuple-element.27), channel_id=1, source_target_pairs={{0,48},{48,0},{96,144},{144,96},{192,240},{240,192},{288,336},{336... | collective-permute-start | bytes 1572872 | tf_op jit(solution)/shard_map/ppermute | solution.py:17
  93.8 6.1 %all-to-all-start.1 = ((f32[3,8,256]{2,1,0:T(8,128)}), f32[3,8,256]{2,1,0:T(8,128)S(1)}, u32[]{:S(2)}, u32[]{:S(2)}) async-start(f32[3,8,256]{2,1,0:T(8,128)} %shard_map.97), calls=%async_computation.1 | async-start | bytes 49152 | tf_op jit(solution)/shard_map/all_to_all | solution.py:390
  99.8 4.2 %collective-permute-done.7.from_p = bf16[2,2,128,512]{3,2,1,0:T(8,128)(2,1)S(1)} collective-permute-done((bf16[2,2,128,512]{3,2,1,0:T(8,128)(2,1)}, bf16[2,2,128,512]{3,2,1,0:T(8,128)(2,1)S(1)}, u32[]{:S(2)}, u32[]{:S(2)}) %collective-permute-start.7) | collective-permute-done | bytes 524320 | tf_op jit(solution)/shard_map/ppermute | solution.py:17
  104.0 2.5 %all-to-all-done.1.terms = f32[3,8,256]{2,1,0:T(8,128)S(1)} async-done(((f32[3,8,256]{2,1,0:T(8,128)}), f32[3,8,256]{2,1,0:T(8,128)S(1)}, u32[]{:S(2)}, u32[]{:S(2)}) %all-to-all-start.1) | async-done | bytes 24608 | tf_op jit(solution)/shard_map/all_to_all | solution.py:390
  106.5 2.2 %shard_map.98 = (f32[2,128,512]{2,1,0:T(8,128)S(1)}, bf16[2,128,512]{2,1,0:T(8,128)(2,1)S(1)}) custom-call(f32[2,128,512]{2,1,0:T(8,128)S(1)} %get-tuple-element.25.own_sum, f32[2,128,512]{2,1,0:T(8,128)S(1)} %copy-done.2, bf16[2,2,128,512]{3,2,1,0:T(8,128)(2,1)S(1)} %collective-permute-done.7.from_p, bf16[2,2,128,512]{3,2,1,0:T(8,128)(2,1)} %collective-permute-done.8.from_q), custom_call_target="tpu_custom_call" | custom-call | flops 100000000 | bytes 4194304 | tf_op jit(solution)/shard_map/pallas_call | solution.py:271
  108.8 7.1 %collective-permute-start.10 = (bf16[2,128,512]{2,1,0:T(8,128)(2,1)S(1)}, bf16[2,128,512]{2,1,0:T(8,128)(2,1)S(1)}, u32[]{:S(2)}, u32[]{:S(2)}) collective-permute-start(bf16[2,128,512]{2,1,0:T(8,128)(2,1)S(1)} %get-tuple-element.34), channel_id=1, source_target_pairs={{0,40},{8,16},{16,8},{24,32},{32,24},{40,0},{1,41},{9,17},{17,9},{... | collective-permute-start | bytes 786440 | tf_op jit(solution)/shard_map/ppermute | solution.py:17
  116.6 9.4 %all-to-all-start.2 = ((bf16[32,8,256]{2,1,0:T(8,128)(2,1)}), bf16[32,8,256]{2,1,0:T(8,128)(2,1)S(1)}, u32[]{:S(2)}, u32[]{:S(2)}) async-start(bf16[32,8,256]{2,1,0:T(8,128)(2,1)} %shard_map.99), calls=%async_computation.2 | async-start | bytes 262144 | tf_op jit(solution)/shard_map/all_to_all | solution.py:394
  126.8 8.6 %all-to-all-done.2.pieces = bf16[32,8,256]{2,1,0:T(8,128)(2,1)S(1)} async-done(((bf16[32,8,256]{2,1,0:T(8,128)(2,1)}), bf16[32,8,256]{2,1,0:T(8,128)(2,1)S(1)}, u32[]{:S(2)}, u32[]{:S(2)}) %all-to-all-start.2) | async-done | bytes 131104 | tf_op jit(solution)/shard_map/all_to_all | solution.py:394
  (56 shorter events, 10.4 us)
Async XLA Ops:
  0.6 35.6 %copy-start = (bf16[512,1024]{1,0:T(8,128)(2,1)S(1)}, bf16[512,1024]{1,0:T(8,128)(2,1)}, u32[]{:S(2)}) copy-start(bf16[512,1024]{1,0:T(8,128)(2,1)} %param.10) | copy-start | bytes 3145732
  0.6 35.5 %copy-start.4 = (bf16[1,1,1,128,1024]{4,3,2,1,0:T(8,128)(2,1)S(1)}, bf16[1,1,1,128,1024]{4,3,2,1,0:T(8,128)(2,1)}, u32[]{:S(2)}) copy-start(bf16[1,1,1,128,1024]{4,3,2,1,0:T(8,128)(2,1)} %param.9) | copy-start | bytes 786436
  2.5 37.4 %copy-start.7 = (bf16[1,1,1,128,512]{4,3,2,1,0:T(8,128)(2,1)S(1)}, bf16[1,1,1,128,512]{4,3,2,1,0:T(8,128)(2,1)}, u32[]{:S(2)}) copy-start(bf16[1,1,1,128,512]{4,3,2,1,0:T(8,128)(2,1)} %param.7) | copy-start | bytes 393220
  2.5 37.4 %copy-start.8 = (bf16[1,1,1,128,512]{4,3,2,1,0:T(8,128)(2,1)S(1)}, bf16[1,1,1,128,512]{4,3,2,1,0:T(8,128)(2,1)}, u32[]{:S(2)}) copy-start(bf16[1,1,1,128,512]{4,3,2,1,0:T(8,128)(2,1)} %param.8) | copy-start | bytes 393220
  2.5 37.4 %copy-start.14 = (bf16[1,1,1,128,512]{4,3,2,1,0:T(8,128)(2,1)S(1)}, bf16[1,1,1,128,512]{4,3,2,1,0:T(8,128)(2,1)}, u32[]{:S(2)}) copy-start(bf16[1,1,1,128,512]{4,3,2,1,0:T(8,128)(2,1)} %param.6) | copy-start | bytes 393220
  2.5 20.1 %collective-permute-start.1 = (bf16[2,128,512]{2,1,0:T(8,128)(2,1)}, bf16[2,128,512]{2,1,0:T(8,128)(2,1)S(1)}, u32[]{:S(2)}, u32[]{:S(2)}) collective-permute-start(bf16[2,128,512]{2,1,0:T(8,128)(2,1)} %get-tuple-element.39), channel_id=1, source_target_pairs={{48,96},{96,48},{144,192},{192,144},{240,288},{288,240},{336,384},... | collective-permute-start | bytes 786440 | tf_op jit(solution)/shard_map/ppermute | solution.py:17
  3.3 19.3 %collective-permute-start = (bf16[2,128,512]{2,1,0:T(8,128)(2,1)}, bf16[2,128,512]{2,1,0:T(8,128)(2,1)S(1)}, u32[]{:S(2)}, u32[]{:S(2)}) collective-permute-start(bf16[2,128,512]{2,1,0:T(8,128)(2,1)} %get-tuple-element.39), channel_id=1, source_target_pairs={{0,48},{48,0},{96,144},{144,96},{192,240},{240,192},{288,336},{336... | collective-permute-start | bytes 786440 | tf_op jit(solution)/shard_map/ppermute | solution.py:17
  9.7 20.9 %collective-permute-start.3 = (bf16[2,128,512]{2,1,0:T(8,128)(2,1)}, bf16[2,128,512]{2,1,0:T(8,128)(2,1)S(1)}, u32[]{:S(2)}, u32[]{:S(2)}) collective-permute-start(bf16[2,128,512]{2,1,0:T(8,128)(2,1)} %get-tuple-element.39), channel_id=1, source_target_pairs={{0,40},{8,16},{16,8},{24,32},{32,24},{40,0},{1,41},{9,17},{17,9},{... | collective-permute-start | bytes 786440 | tf_op jit(solution)/shard_map/ppermute | solution.py:17
  22.6 23.2 %copy-start.5 = (bf16[2,128,512]{2,1,0:T(8,128)(2,1)}, bf16[2,128,512]{2,1,0:T(8,128)(2,1)S(1)}, u32[]{:S(2)}) copy-start(bf16[2,128,512]{2,1,0:T(8,128)(2,1)S(1)} %collective-permute-done.1.refs_4_) | copy-start | bytes 786436
  22.6 23.2 %copy-start.6 = (bf16[2,128,512]{2,1,0:T(8,128)(2,1)}, bf16[2,128,512]{2,1,0:T(8,128)(2,1)S(1)}, u32[]{:S(2)}) copy-start(bf16[2,128,512]{2,1,0:T(8,128)(2,1)S(1)} %collective-permute-done.refs_2_) | copy-start | bytes 786436
  22.7 17.1 %collective-permute-start.2 = (bf16[3,2,128,512]{3,2,1,0:T(8,128)(2,1)S(1)}, bf16[3,2,128,512]{3,2,1,0:T(8,128)(2,1)S(1)}, u32[]{:S(2)}, u32[]{:S(2)}) collective-permute-start(bf16[3,2,128,512]{3,2,1,0:T(8,128)(2,1)S(1)} %pad_maximum_fusion), channel_id=1, source_target_pairs={{0,8},{8,0},{16,24},{24,16},{32,40},{40,32},{1,9},{9,1},{17,25},{2... | collective-permute-start | bytes 2359304 | tf_op jit(solution)/shard_map/ppermute | solution.py:17
  30.6 15.2 %copy-start.11 = (bf16[2,128,512]{2,1,0:T(8,128)(2,1)}, bf16[2,128,512]{2,1,0:T(8,128)(2,1)S(1)}, u32[]{:S(2)}) copy-start(bf16[2,128,512]{2,1,0:T(8,128)(2,1)S(1)} %collective-permute-done.3.refs_1_) | copy-start | bytes 786436
  30.6 6.1 %collective-permute-start.5 = (bf16[2,128,512]{2,1,0:T(8,128)(2,1)S(1)}, bf16[2,128,512]{2,1,0:T(8,128)(2,1)S(1)}, u32[]{:S(2)}, u32[]{:S(2)}) collective-permute-start(bf16[2,128,512]{2,1,0:T(8,128)(2,1)S(1)} %collective-permute-done.3.refs_1_), channel_id=1, source_target_pairs={{48,96},{96,48},{144,192},{192,144},{240,288},{288,240},{336,384},... | collective-permute-start | bytes 786440 | tf_op jit(solution)/shard_map/ppermute | solution.py:17
  31.2 8.6 %collective-permute-start.4 = (bf16[2,128,512]{2,1,0:T(8,128)(2,1)S(1)}, bf16[2,128,512]{2,1,0:T(8,128)(2,1)S(1)}, u32[]{:S(2)}, u32[]{:S(2)}) collective-permute-start(bf16[2,128,512]{2,1,0:T(8,128)(2,1)S(1)} %collective-permute-done.3.refs_1_), channel_id=1, source_target_pairs={{0,48},{48,0},{96,144},{144,96},{192,240},{240,192},{288,336},{336... | collective-permute-start | bytes 786440 | tf_op jit(solution)/shard_map/ppermute | solution.py:17
  45.9 12.8 %copy-start.16 = (f32[4,3,8,256]{3,2,1,0:T(8,128)}, f32[4,3,8,256]{3,2,1,0:T(8,128)S(1)}, u32[]{:S(2)}) copy-start(f32[4,3,8,256]{3,2,1,0:T(8,128)S(1)} %get-tuple-element.20.refs_6_) | copy-start | bytes 294916
  45.9 11.3 %collective-permute-start.9 = (bf16[4,128,512]{2,1,0:T(8,128)(2,1)S(1)}, bf16[4,128,512]{2,1,0:T(8,128)(2,1)S(1)}, u32[]{:S(2)}, u32[]{:S(2)}) collective-permute-start(bf16[4,128,512]{2,1,0:T(8,128)(2,1)S(1)} %get-tuple-element.29), channel_id=1, source_target_pairs={{0,8},{8,0},{16,24},{24,16},{32,40},{40,32},{1,9},{9,1},{17,25},{2... | collective-permute-start | bytes 1572872 | tf_op jit(solution)/shard_map/ppermute | solution.py:17
  58.7 34.3 %all-to-all-start = ((bf16[128,8,256]{2,1,0:T(8,128)(2,1)}), bf16[128,8,256]{2,1,0:T(8,128)(2,1)S(1)}, u32[]{:S(2)}, u32[]{:S(2)}) async-start(bf16[128,8,256]{2,1,0:T(8,128)(2,1)} %shard_map.96), calls=%async_computation | async-start | bytes 1048576 | tf_op jit(solution)/shard_map/all_to_all | solution.py:388
  79.7 4.7 %collective-permute-start.6 = (bf16[6,128,512]{2,1,0:T(8,128)(2,1)}, bf16[6,128,512]{2,1,0:T(8,128)(2,1)S(1)}, u32[]{:S(2)}, u32[]{:S(2)}) collective-permute-start(bf16[6,128,512]{2,1,0:T(8,128)(2,1)} %get-tuple-element.22), channel_id=1, source_target_pairs={{0,8},{8,0},{16,24},{24,16},{32,40},{40,32},{1,9},{9,1},{17,25},{2... | collective-permute-start | bytes 2359304 | tf_op jit(solution)/shard_map/ppermute | solution.py:17
  86.8 19.7 %copy-start.2 = (f32[2,128,512]{2,1,0:T(8,128)S(1)}, f32[2,128,512]{2,1,0:T(8,128)}, u32[]{:S(2)}) copy-start(f32[2,128,512]{2,1,0:T(8,128)} %get-tuple-element.26.far_middle) | copy-start | bytes 1572868
  88.8 15.2 %collective-permute-start.7 = (bf16[2,2,128,512]{3,2,1,0:T(8,128)(2,1)}, bf16[2,2,128,512]{3,2,1,0:T(8,128)(2,1)S(1)}, u32[]{:S(2)}, u32[]{:S(2)}) collective-permute-start(bf16[2,2,128,512]{3,2,1,0:T(8,128)(2,1)} %get-tuple-element.27), channel_id=1, source_target_pairs={{0,48},{48,0},{96,144},{144,96},{192,240},{240,192},{288,336},{336... | collective-permute-start | bytes 1572872 | tf_op jit(solution)/shard_map/ppermute | solution.py:17
  91.5 12.5 %collective-permute-start.8 = (bf16[2,2,128,512]{3,2,1,0:T(8,128)(2,1)}, bf16[2,2,128,512]{3,2,1,0:T(8,128)(2,1)}, u32[]{:S(2)}, u32[]{:S(2)}) collective-permute-start(bf16[2,2,128,512]{3,2,1,0:T(8,128)(2,1)} %get-tuple-element.28), channel_id=1, source_target_pairs={{48,96},{96,48},{144,192},{192,144},{240,288},{288,240},{336,384},... | collective-permute-start | bytes 1572872 | tf_op jit(solution)/shard_map/ppermute | solution.py:17
  93.8 12.8 %all-to-all-start.1 = ((f32[3,8,256]{2,1,0:T(8,128)}), f32[3,8,256]{2,1,0:T(8,128)S(1)}, u32[]{:S(2)}, u32[]{:S(2)}) async-start(f32[3,8,256]{2,1,0:T(8,128)} %shard_map.97), calls=%async_computation.1 | async-start | bytes 49152 | tf_op jit(solution)/shard_map/all_to_all | solution.py:390
  108.8 17.2 %collective-permute-start.10 = (bf16[2,128,512]{2,1,0:T(8,128)(2,1)S(1)}, bf16[2,128,512]{2,1,0:T(8,128)(2,1)S(1)}, u32[]{:S(2)}, u32[]{:S(2)}) collective-permute-start(bf16[2,128,512]{2,1,0:T(8,128)(2,1)S(1)} %get-tuple-element.34), channel_id=1, source_target_pairs={{0,40},{8,16},{16,8},{24,32},{32,24},{40,0},{1,41},{9,17},{17,9},{... | collective-permute-start | bytes 786440 | tf_op jit(solution)/shard_map/ppermute | solution.py:17
  116.6 18.8 %all-to-all-start.2 = ((bf16[32,8,256]{2,1,0:T(8,128)(2,1)}), bf16[32,8,256]{2,1,0:T(8,128)(2,1)S(1)}, u32[]{:S(2)}, u32[]{:S(2)}) async-start(bf16[32,8,256]{2,1,0:T(8,128)(2,1)} %shard_map.99), calls=%async_computation.2 | async-start | bytes 262144 | tf_op jit(solution)/shard_map/all_to_all | solution.py:394
  (7 other events, 42.3 us)

commit v8 on v7

--- a/solution.py
+++ b/solution.py
@@ -9,7 +9,8 @@
 SCALE = HDIM ** (-0.5)
 DEAD = -1e30
 LANES = 2 * HDIM
-PART_ROWS = 8
+PART_ROWS = 16
+SPREAD = 4
 
 
 def exchange(array, axis, mate):
@@ -277,7 +278,7 @@
         compiler_params=pltpu.CompilerParams(
             dimension_semantics=("arbitrary",), vmem_limit_bytes=8 << 20
         ),
-        cost_estimate=pl.CostEstimate(flops=100_000_000, bytes_accessed=4 << 20, transcendentals=0),
+        cost_estimate=pl.CostEstimate(flops=1_000_000_000, bytes_accessed=4 << 20, transcendentals=0),
     )(own_sum, far_middle, from_p, from_q)
 
 
@@ -332,8 +333,8 @@
 
     def kernel(pieces, out):
         for at in range(pieces.shape[0]):
-            lat, core = at // 2, at % 2
-            row, column = lat // across * height, (core * across + lat % across) * width
+            x, core = at // 2, at % 2
+            row, column = x // across * height, (core * across + x % across) * width
             out[row : row + height, column : column + width] = pieces[at].astype(jnp.float32)
 
     return pl.pallas_call(
@@ -371,7 +372,7 @@
     near_p, near_q = lat_mates_of(own)
     partner = partner_of(jnp.stack((own, near_p, near_q)))
     far_p, far_q = lat_mates_of(far)
-    parts = opt_count * lat_count
+    parts = opt_count * SPREAD
     w_given, w_own, backward = attention(
         live, query, dout, grad, (key, value, partner, far, near_p, far_p, near_q, far_q), parts
     )
@@ -380,21 +381,35 @@
     to_p, to_q, own_sum = chip_sum(partner_of(to_partner), own_column, far_ends)
     w_parts = weight_sum(partner_of(w_given), w_own)
     from_p, from_q = exchange(to_p, "lat", next_door), exchange(to_q, "lat", other_door)
-    cores = [list(range(core, lon_count, 2)) for core in range(2)]
-    chips = [
-        [lat * lon_count + chip + core for lat in range(lat_count) for core in range(2)]
+    lines = lat_count // SPREAD
+    planes = [
+        [opt * lat_count + line * SPREAD + x for opt in range(opt_count) for x in range(SPREAD)]
+        for line in range(lines)
+    ]
+    columns = [
+        [
+            (line * SPREAD + x) * lon_count + lon
+            for line in range(lines)
+            for lon in range(core, lon_count, 2)
+        ]
+        for x in range(SPREAD)
+        for core in range(2)
+    ]
+    rows = [
+        [(line * SPREAD + x) * lon_count + chip + core for x in range(SPREAD) for core in range(2)]
+        for line in range(lines)
         for chip in range(0, lon_count, 2)
     ]
-    w_part = lax.all_to_all(w_parts, ("opt", "lat"), 0, 0)
-    w_part = sum_and_copy(w_part, len(cores[0]), wide)
-    w_part = lax.all_to_all(w_part, "lon", 0, 0, axis_index_groups=cores)
-    from_p, from_q, w_part = lax.optimization_barrier((from_p, from_q, w_part))
+    w_part = lax.all_to_all(w_parts, ("opt", "lat"), 0, 0, axis_index_groups=planes)
+    w_part, own_sum = lax.optimization_barrier((w_part, own_sum))
+    w_part = sum_and_copy(w_part, len(columns[0]), low)
+    w_part = lax.all_to_all(w_part, ("lat", "lon"), 0, 0, axis_index_groups=columns)
     owned, far_sum = lat_sum(own_sum, far_middle, from_p, from_q)
-    w_part = sum_and_copy(w_part, len(chips[0]), low)
-    w_part = lax.all_to_all(w_part, ("lat", "lon"), 0, 0, axis_index_groups=chips)
+    w_part = sum_and_copy(w_part, len(rows[0]), low)
+    w_part = lax.all_to_all(w_part, ("lat", "lon"), 0, 0, axis_index_groups=rows)
+    owned = (owned + far_of(far_sum).astype(wide)).astype(low)
+    w_part, owned = lax.optimization_barrier((w_part, owned))
     grad_weight = assemble(w_part, att_width // opt_count, model_width)
-    owned = (owned + far_of(far_sum).astype(wide)).astype(low)
-
     return (
         grad_query[None, None, None],
         owned[0][None, None, None],

time: 137 us -> 133 us (0.971)
  waiting for transfers between devices: 24.9 us -> 19.3 us
  local copies, waits for them, and re-layouts: 4.34 us -> 8.64 us
  starting transfers between devices: 82.8 us -> 79.4 us
    ppermute x11, waiting for transfers between devices: 13.8 us -> 7.32 us  [exchange(): lax.ppermute(array, axis, [(i, j) for i, j in pairs if 0 <= j < lax.axis_...]
    all_to_all x3, starting transfers between devices: 29.8 us -> 25 us  [the longest x1 9.62 us: shards(): lax.all_to_all(w_part, ('lat', 'lon'), 0, 0, axis_index_groups=columns)]
    unnamed x34 -> x42, local copies, waits for them, and re-layouts: 2.52 us -> 6.82 us
    pallas_call x1, Pallas kernels: 2.24 us -> 0.66 us  [lat_sum(): pl.pallas_call(lat_sum_kernel, grid=(width // LANES,), in_specs=[two, two...]
    pallas_call x1, Pallas kernels: 1.97 us -> 3.44 us  [chip_sum(): pl.pallas_call(chip_sum_kernel, grid=(width // LANES,), in_specs=[pl.Bloc...]
  transfers between devices with their start and end apart: 14 -> 14, of which waited for: 7 -> 6; matrix products, arithmetic and copies ran while one was open for 2% -> 2% of each run, Pallas kernels for 7% -> 10%
where the time goes in v8:
time: 133 us; the launch traced here: 132 us
  starting transfers between devices  79.4 us (60%)
  Pallas kernels  20.9 us (16%)
  waiting for transfers between devices  19.3 us (15%)
  local copies, waits for them, and re-layouts  8.64 us (6%)
  other arithmetic  2.26 us (2%)
    ppermute x11, starting transfers between devices, exchange(): lax.ppermute(array, axis, [(i, j) for i, j in pairs if 0 <= j < lax.axis_...  54.3 us
    all_to_all x1, starting transfers between devices, shards(): lax.all_to_all(w_part, ('lat', 'lon'), 0, 0, axis_index_groups=columns)  9.62 us
    all_to_all x1, starting transfers between devices, shards(): lax.all_to_all(w_parts, ('opt', 'lat'), 0, 0, axis_index_groups=planes)  9.22 us
    ppermute x11, waiting for transfers between devices, exchange(): lax.ppermute(array, axis, [(i, j) for i, j in pairs if 0 <= j < lax.axis_...  7.32 us
    all_to_all x1, waiting for transfers between devices, shards(): lax.all_to_all(w_parts, ('opt', 'lat'), 0, 0, axis_index_groups=planes)  7.3 us
    unnamed x42, local copies, waits for them, and re-layouts  6.82 us
    pallas_call x1, Pallas kernels, attention(): pl.pallas_call(backward_kernel, grid=(steps,), in_specs=[scalars, one, on...  6.56 us
    pallas_call x1, Pallas kernels, attention(): pl.pallas_call(forward_kernel, grid=(steps,), in_specs=[scalars, one, one...  6.55 us
  transfers between devices with their start and end apart: 14, of which 6 were waited for; matrix products, arithmetic and copies ran while one was open for 2% of the time, Pallas kernels for 10%

profile of v8, /device:TPU:1, one launch (start us, length us, event | category | flops | bytes accessed | tf_op | source)
XLA Modules:
  0.0 132.0 jit_solution(3094153109949258498)
XLA Ops:
  0.7 1.8 %fusion.7 = (bf16[1,2,128,512]{3,2,1,0:T(8,128)(2,1)S(1)}, bf16[2,128,512]{2,1,0:T(8,128)(2,1)}) fusion(bf16[1,128,512]{2,1,0:T(8,128)(2,1)} %bitcast.25, bf16[1,128,512]{2,1,0:T(8,128)(2,1)} %bitcast.22), kind=kLoop, calls=%fused_computation.23 | loop fusion | flops 131072 | bytes 786432 | tf_op jit(solution)/shard_map/stack | solution.py:373
  3.3 6.4 %collective-permute-start = (bf16[2,128,512]{2,1,0:T(8,128)(2,1)}, bf16[2,128,512]{2,1,0:T(8,128)(2,1)S(1)}, u32[]{:S(2)}, u32[]{:S(2)}) collective-permute-start(bf16[2,128,512]{2,1,0:T(8,128)(2,1)} %get-tuple-element.41), channel_id=1, source_target_pairs={{0,48},{48,0},{96,144},{144,96},{192,240},{240,192},{288,336},{336... | collective-permute-start | bytes 786440 | tf_op jit(solution)/shard_map/ppermute | solution.py:18
  9.7 11.8 %collective-permute-start.3 = (bf16[2,128,512]{2,1,0:T(8,128)(2,1)}, bf16[2,128,512]{2,1,0:T(8,128)(2,1)S(1)}, u32[]{:S(2)}, u32[]{:S(2)}) collective-permute-start(bf16[2,128,512]{2,1,0:T(8,128)(2,1)} %get-tuple-element.41), channel_id=1, source_target_pairs={{0,40},{8,16},{16,8},{24,32},{32,24},{40,0},{1,41},{9,17},{17,9},{... | collective-permute-start | bytes 786440 | tf_op jit(solution)/shard_map/ppermute | solution.py:18
  21.5 1.1 dynamic-slice_reduce_fusion
  22.7 4.8 %collective-permute-start.2 = (bf16[3,2,128,512]{3,2,1,0:T(8,128)(2,1)S(1)}, bf16[3,2,128,512]{3,2,1,0:T(8,128)(2,1)S(1)}, u32[]{:S(2)}, u32[]{:S(2)}) collective-permute-start(bf16[3,2,128,512]{3,2,1,0:T(8,128)(2,1)S(1)} %pad_maximum_fusion), channel_id=1, source_target_pairs={{0,8},{8,0},{16,24},{24,16},{32,40},{40,32},{1,9},{9,1},{17,25},{2... | collective-permute-start | bytes 2359304 | tf_op jit(solution)/shard_map/ppermute | solution.py:18
  27.8 2.8 %collective-permute-done.3.refs_1_ = bf16[2,128,512]{2,1,0:T(8,128)(2,1)S(1)} collective-permute-done((bf16[2,128,512]{2,1,0:T(8,128)(2,1)}, bf16[2,128,512]{2,1,0:T(8,128)(2,1)S(1)}, u32[]{:S(2)}, u32[]{:S(2)}) %collective-permute-start.3) | collective-permute-done | bytes 262176 | tf_op jit(solution)/shard_map/ppermute | solution.py:18
  31.2 4.9 %collective-permute-start.4 = (bf16[2,128,512]{2,1,0:T(8,128)(2,1)S(1)}, bf16[2,128,512]{2,1,0:T(8,128)(2,1)S(1)}, u32[]{:S(2)}, u32[]{:S(2)}) collective-permute-start(bf16[2,128,512]{2,1,0:T(8,128)(2,1)S(1)} %collective-permute-done.3.refs_1_), channel_id=1, source_target_pairs={{0,48},{48,0},{96,144},{144,96},{192,240},{240,192},{288,336},{336... | collective-permute-start | bytes 786440 | tf_op jit(solution)/shard_map/ppermute | solution.py:18
  36.7 3.1 %collective-permute-done.4.refs_3_ = bf16[2,128,512]{2,1,0:T(8,128)(2,1)S(1)} collective-permute-done((bf16[2,128,512]{2,1,0:T(8,128)(2,1)S(1)}, bf16[2,128,512]{2,1,0:T(8,128)(2,1)S(1)}, u32[]{:S(2)}, u32[]{:S(2)}) %collective-permute-start.4) | collective-permute-done | bytes 262176 | tf_op jit(solution)/shard_map/ppermute | solution.py:18
  39.9 6.6 %shard_map.93 = (bf16[4,128,512]{2,1,0:T(8,128)(2,1)}, f32[32,16,512]{2,1,0:T(8,128)S(1)}, f32[4,3,8,256]{3,2,1,0:T(8,128)S(1)}) custom-call(s32[10]{0:T(128)S(1)} %pad_add_fusion.live, bf16[128,512]{1,0:T(8,128)(2,1)S(1)} %bitcast.29, bf16[128,512]{1,0:T(8,128)(2,1)S(1)} %convolution_convert_fusion.dout, bf16[128,1024]{1,0:T(8,128)(2,1)S(1)} %bitcast.19, ...), custom_call_target="tpu_custom_call" | custom-call | flops 1509949440 | bytes 5242880 | tf_op jit(solution)/shard_map/pallas_call | solution.py:173
  48.1 9.8 %collective-permute-start.6 = (bf16[4,128,512]{2,1,0:T(8,128)(2,1)}, bf16[4,128,512]{2,1,0:T(8,128)(2,1)S(1)}, u32[]{:S(2)}, u32[]{:S(2)}) collective-permute-start(bf16[4,128,512]{2,1,0:T(8,128)(2,1)} %get-tuple-element.23), channel_id=1, source_target_pairs={{0,8},{8,0},{16,24},{24,16},{32,40},{40,32},{1,9},{9,1},{17,25},{2... | collective-permute-start | bytes 1572872 | tf_op jit(solution)/shard_map/ppermute | solution.py:18
  57.9 6.6 %shard_map.94 = (bf16[128,512]{1,0:T(8,128)(2,1)}, bf16[6,128,512]{2,1,0:T(8,128)(2,1)}, f32[3,2,128,512]{3,2,1,0:T(8,128)}, bf16[2,2,128,512]{3,2,1,0:T(8,128)(2,1)}, f32[2,128,512]{2,1,0:T(8,128)}) custom-call(s32[10]{0:T(128)} %copy-done.18, bf16[128,512]{1,0:T(8,128)(2,1)} %bitcast.28, bf16[128,512]{1,0:T(8,128)(2,1)} %copy-done.10, ...), custom_call_target="tpu_custom_call" | custom-call | flops 3019898880 | bytes 6291456 | tf_op jit(solution)/shard_map/pallas_call | solution.py:195
  64.5 1.9 %collective-permute-start.7 = (bf16[6,128,512]{2,1,0:T(8,128)(2,1)}, bf16[6,128,512]{2,1,0:T(8,128)(2,1)}, u32[]{:S(2)}, u32[]{:S(2)}) collective-permute-start(bf16[6,128,512]{2,1,0:T(8,128)(2,1)} %get-tuple-element.25), channel_id=1, source_target_pairs={{0,8},{8,0},{16,24},{24,16},{32,40},{40,32},{1,9},{9,1},{17,25},{2... | collective-permute-start | bytes 2359304 | tf_op jit(solution)/shard_map/ppermute | solution.py:18
  66.5 1.2 copy-done.3
  67.7 1.5 %shard_map.95 = bf16[32,16,512]{2,1,0:T(8,128)(2,1)} custom-call(bf16[4,128,512]{2,1,0:T(8,128)(2,1)S(1)} %collective-permute-done.6.given, f32[32,16,512]{2,1,0:T(8,128)S(1)} %copy-done.3), custom_call_target="tpu_custom_call" | custom-call | flops 262144 | bytes 2097152 | tf_op jit(solution)/shard_map/pallas_call | solution.py:300
  69.2 9.2 %all-to-all-start = ((bf16[32,16,512]{2,1,0:T(8,128)(2,1)}), bf16[32,16,512]{2,1,0:T(8,128)(2,1)S(1)}, u32[]{:S(2)}, u32[]{:S(2)}) async-start(bf16[32,16,512]{2,1,0:T(8,128)(2,1)} %shard_map.95), calls=%async_computation | async-start | bytes 1048576 | tf_op jit(solution)/shard_map/all_to_all | solution.py:403
  79.5 3.4 %shard_map.96 = (bf16[2,2,128,512]{3,2,1,0:T(8,128)(2,1)}, bf16[2,2,128,512]{3,2,1,0:T(8,128)(2,1)}, f32[2,128,512]{2,1,0:T(8,128)S(1)}) custom-call(bf16[6,128,512]{2,1,0:T(8,128)(2,1)} %collective-permute-done.7.given, f32[3,2,128,512]{3,2,1,0:T(8,128)S(1)} %copy-done.1, bf16[2,2,128,512]{3,2,1,0:T(8,128)(2,1)S(1)} %copy-done.4), custom_call_target="tpu_custom_call" | custom-call | flops 786432 | bytes 1966080 | tf_op jit(solution)/shard_map/pallas_call | solution.py:240
  83.7 3.1 %collective-permute-start.8 = (bf16[2,2,128,512]{3,2,1,0:T(8,128)(2,1)}, bf16[2,2,128,512]{3,2,1,0:T(8,128)(2,1)S(1)}, u32[]{:S(2)}, u32[]{:S(2)}) collective-permute-start(bf16[2,2,128,512]{3,2,1,0:T(8,128)(2,1)} %get-tuple-element.32), channel_id=1, source_target_pairs={{0,48},{48,0},{96,144},{144,96},{192,240},{240,192},{288,336},{336... | collective-permute-start | bytes 1572872 | tf_op jit(solution)/shard_map/ppermute | solution.py:18
  87.5 7.3 %all-to-all-done.terms = bf16[32,16,512]{2,1,0:T(8,128)(2,1)S(1)} async-done(((bf16[32,16,512]{2,1,0:T(8,128)(2,1)}), bf16[32,16,512]{2,1,0:T(8,128)(2,1)S(1)}, u32[]{:S(2)}, u32[]{:S(2)}) %all-to-all-start) | async-done | bytes 524320 | tf_op jit(solution)/shard_map/all_to_all | solution.py:403
  95.6 9.6 %all-to-all-start.1 = ((bf16[12,16,512]{2,1,0:T(8,128)(2,1)}), bf16[12,16,512]{2,1,0:T(8,128)(2,1)S(1)}, u32[]{:S(2)}, u32[]{:S(2)}) async-start(bf16[12,16,512]{2,1,0:T(8,128)(2,1)} %shard_map.97), calls=%async_computation.1 | async-start | bytes 393216 | tf_op jit(solution)/shard_map/all_to_all | solution.py:406
  106.3 1.0 copy-done.19
  108.0 9.5 %collective-permute-start.10 = (bf16[2,128,512]{2,1,0:T(8,128)(2,1)S(1)}, bf16[2,128,512]{2,1,0:T(8,128)(2,1)S(1)}, u32[]{:S(2)}, u32[]{:S(2)}) collective-permute-start(bf16[2,128,512]{2,1,0:T(8,128)(2,1)S(1)} %get-tuple-element.35), channel_id=1, source_target_pairs={{0,40},{8,16},{16,8},{24,32},{32,24},{40,0},{1,41},{9,17},{17,9},{... | collective-permute-start | bytes 786440 | tf_op jit(solution)/shard_map/ppermute | solution.py:18
  119.1 6.2 %all-to-all-start.2 = ((bf16[8,16,512]{2,1,0:T(8,128)(2,1)}), bf16[8,16,512]{2,1,0:T(8,128)(2,1)S(1)}, u32[]{:S(2)}, u32[]{:S(2)}) async-start(bf16[8,16,512]{2,1,0:T(8,128)(2,1)} %shard_map.98), calls=%async_computation.2 | async-start | bytes 262144 | tf_op jit(solution)/shard_map/all_to_all | solution.py:409
  125.3 1.4 %collective-permute-done.10 = bf16[2,128,512]{2,1,0:T(8,128)(2,1)S(1)} collective-permute-done((bf16[2,128,512]{2,1,0:T(8,128)(2,1)S(1)}, bf16[2,128,512]{2,1,0:T(8,128)(2,1)S(1)}, u32[]{:S(2)}, u32[]{:S(2)}) %collective-permute-start.10) | collective-permute-done | bytes 262176 | tf_op jit(solution)/shard_map/ppermute | solution.py:18
  126.7 3.9 %all-to-all-done.2.pieces = bf16[8,16,512]{2,1,0:T(8,128)(2,1)S(1)} async-done(((bf16[8,16,512]{2,1,0:T(8,128)(2,1)}), bf16[8,16,512]{2,1,0:T(8,128)(2,1)S(1)}, u32[]{:S(2)}, u32[]{:S(2)}) %all-to-all-start.2) | async-done | bytes 131104 | tf_op jit(solution)/shard_map/all_to_all | solution.py:409
  (64 shorter events, 12.1 us)
Async XLA Ops:
  0.6 35.6 %copy-start = (bf16[512,1024]{1,0:T(8,128)(2,1)S(1)}, bf16[512,1024]{1,0:T(8,128)(2,1)}, u32[]{:S(2)}) copy-start(bf16[512,1024]{1,0:T(8,128)(2,1)} %param.10) | copy-start | bytes 3145732
  0.6 35.5 %copy-start.5 = (bf16[1,1,1,128,1024]{4,3,2,1,0:T(8,128)(2,1)S(1)}, bf16[1,1,1,128,1024]{4,3,2,1,0:T(8,128)(2,1)}, u32[]{:S(2)}) copy-start(bf16[1,1,1,128,1024]{4,3,2,1,0:T(8,128)(2,1)} %param.9) | copy-start | bytes 786436
  2.5 37.4 %copy-start.8 = (bf16[1,1,1,128,512]{4,3,2,1,0:T(8,128)(2,1)S(1)}, bf16[1,1,1,128,512]{4,3,2,1,0:T(8,128)(2,1)}, u32[]{:S(2)}) copy-start(bf16[1,1,1,128,512]{4,3,2,1,0:T(8,128)(2,1)} %param.7) | copy-start | bytes 393220
  2.5 37.4 %copy-start.9 = (bf16[1,1,1,128,512]{4,3,2,1,0:T(8,128)(2,1)S(1)}, bf16[1,1,1,128,512]{4,3,2,1,0:T(8,128)(2,1)}, u32[]{:S(2)}) copy-start(bf16[1,1,1,128,512]{4,3,2,1,0:T(8,128)(2,1)} %param.8) | copy-start | bytes 393220
  2.5 37.4 %copy-start.17 = (bf16[1,1,1,128,512]{4,3,2,1,0:T(8,128)(2,1)S(1)}, bf16[1,1,1,128,512]{4,3,2,1,0:T(8,128)(2,1)}, u32[]{:S(2)}) copy-start(bf16[1,1,1,128,512]{4,3,2,1,0:T(8,128)(2,1)} %param.6) | copy-start | bytes 393220
  2.5 20.1 %collective-permute-start.1 = (bf16[2,128,512]{2,1,0:T(8,128)(2,1)}, bf16[2,128,512]{2,1,0:T(8,128)(2,1)S(1)}, u32[]{:S(2)}, u32[]{:S(2)}) collective-permute-start(bf16[2,128,512]{2,1,0:T(8,128)(2,1)} %get-tuple-element.41), channel_id=1, source_target_pairs={{48,96},{96,48},{144,192},{192,144},{240,288},{288,240},{336,384},... | collective-permute-start | bytes 786440 | tf_op jit(solution)/shard_map/ppermute | solution.py:18
  3.3 19.3 %collective-permute-start = (bf16[2,128,512]{2,1,0:T(8,128)(2,1)}, bf16[2,128,512]{2,1,0:T(8,128)(2,1)S(1)}, u32[]{:S(2)}, u32[]{:S(2)}) collective-permute-start(bf16[2,128,512]{2,1,0:T(8,128)(2,1)} %get-tuple-element.41), channel_id=1, source_target_pairs={{0,48},{48,0},{96,144},{144,96},{192,240},{240,192},{288,336},{336... | collective-permute-start | bytes 786440 | tf_op jit(solution)/shard_map/ppermute | solution.py:18
  9.7 20.9 %collective-permute-start.3 = (bf16[2,128,512]{2,1,0:T(8,128)(2,1)}, bf16[2,128,512]{2,1,0:T(8,128)(2,1)S(1)}, u32[]{:S(2)}, u32[]{:S(2)}) collective-permute-start(bf16[2,128,512]{2,1,0:T(8,128)(2,1)} %get-tuple-element.41), channel_id=1, source_target_pairs={{0,40},{8,16},{16,8},{24,32},{32,24},{40,0},{1,41},{9,17},{17,9},{... | collective-permute-start | bytes 786440 | tf_op jit(solution)/shard_map/ppermute | solution.py:18
  22.6 23.9 %copy-start.6 = (bf16[2,128,512]{2,1,0:T(8,128)(2,1)}, bf16[2,128,512]{2,1,0:T(8,128)(2,1)S(1)}, u32[]{:S(2)}) copy-start(bf16[2,128,512]{2,1,0:T(8,128)(2,1)S(1)} %collective-permute-done.1.refs_4_) | copy-start | bytes 786436
  22.6 23.8 %copy-start.7 = (bf16[2,128,512]{2,1,0:T(8,128)(2,1)}, bf16[2,128,512]{2,1,0:T(8,128)(2,1)S(1)}, u32[]{:S(2)}) copy-start(bf16[2,128,512]{2,1,0:T(8,128)(2,1)S(1)} %collective-permute-done.refs_2_) | copy-start | bytes 786436
  22.7 17.1 %collective-permute-start.2 = (bf16[3,2,128,512]{3,2,1,0:T(8,128)(2,1)S(1)}, bf16[3,2,128,512]{3,2,1,0:T(8,128)(2,1)S(1)}, u32[]{:S(2)}, u32[]{:S(2)}) collective-permute-start(bf16[3,2,128,512]{3,2,1,0:T(8,128)(2,1)S(1)} %pad_maximum_fusion), channel_id=1, source_target_pairs={{0,8},{8,0},{16,24},{24,16},{32,40},{40,32},{1,9},{9,1},{17,25},{2... | collective-permute-start | bytes 2359304 | tf_op jit(solution)/shard_map/ppermute | solution.py:18
  30.6 15.9 %copy-start.14 = (bf16[2,128,512]{2,1,0:T(8,128)(2,1)}, bf16[2,128,512]{2,1,0:T(8,128)(2,1)S(1)}, u32[]{:S(2)}) copy-start(bf16[2,128,512]{2,1,0:T(8,128)(2,1)S(1)} %collective-permute-done.3.refs_1_) | copy-start | bytes 786436
  30.6 6.1 %collective-permute-start.5 = (bf16[2,128,512]{2,1,0:T(8,128)(2,1)S(1)}, bf16[2,128,512]{2,1,0:T(8,128)(2,1)S(1)}, u32[]{:S(2)}, u32[]{:S(2)}) collective-permute-start(bf16[2,128,512]{2,1,0:T(8,128)(2,1)S(1)} %collective-permute-done.3.refs_1_), channel_id=1, source_target_pairs={{48,96},{96,48},{144,192},{192,144},{240,288},{288,240},{336,384},... | collective-permute-start | bytes 786440 | tf_op jit(solution)/shard_map/ppermute | solution.py:18
  31.2 8.6 %collective-permute-start.4 = (bf16[2,128,512]{2,1,0:T(8,128)(2,1)S(1)}, bf16[2,128,512]{2,1,0:T(8,128)(2,1)S(1)}, u32[]{:S(2)}, u32[]{:S(2)}) collective-permute-start(bf16[2,128,512]{2,1,0:T(8,128)(2,1)S(1)} %collective-permute-done.3.refs_1_), channel_id=1, source_target_pairs={{0,48},{48,0},{96,144},{144,96},{192,240},{240,192},{288,336},{336... | collective-permute-start | bytes 786440 | tf_op jit(solution)/shard_map/ppermute | solution.py:18
  36.2 10.3 %copy-start.18 = (s32[10]{0:T(128)}, s32[10]{0:T(128)S(1)}, u32[]{:S(2)}) copy-start(s32[10]{0:T(128)S(1)} %pad_add_fusion.live) | copy-start | bytes 124
  48.1 18.3 %collective-permute-start.6 = (bf16[4,128,512]{2,1,0:T(8,128)(2,1)}, bf16[4,128,512]{2,1,0:T(8,128)(2,1)S(1)}, u32[]{:S(2)}, u32[]{:S(2)}) collective-permute-start(bf16[4,128,512]{2,1,0:T(8,128)(2,1)} %get-tuple-element.23), channel_id=1, source_target_pairs={{0,8},{8,0},{16,24},{24,16},{32,40},{40,32},{1,9},{9,1},{17,25},{2... | collective-permute-start | bytes 1572872 | tf_op jit(solution)/shard_map/ppermute | solution.py:18
  64.5 13.9 %collective-permute-start.7 = (bf16[6,128,512]{2,1,0:T(8,128)(2,1)}, bf16[6,128,512]{2,1,0:T(8,128)(2,1)}, u32[]{:S(2)}, u32[]{:S(2)}) collective-permute-start(bf16[6,128,512]{2,1,0:T(8,128)(2,1)} %get-tuple-element.25), channel_id=1, source_target_pairs={{0,8},{8,0},{16,24},{24,16},{32,40},{40,32},{1,9},{9,1},{17,25},{2... | collective-permute-start | bytes 2359304 | tf_op jit(solution)/shard_map/ppermute | solution.py:18
  67.7 10.7 %copy-start.1 = (f32[3,2,128,512]{3,2,1,0:T(8,128)S(1)}, f32[3,2,128,512]{3,2,1,0:T(8,128)}, u32[]{:S(2)}) copy-start(f32[3,2,128,512]{3,2,1,0:T(8,128)} %get-tuple-element.26.own_column) | copy-start | bytes 4718596
  69.2 25.7 %all-to-all-start = ((bf16[32,16,512]{2,1,0:T(8,128)(2,1)}), bf16[32,16,512]{2,1,0:T(8,128)(2,1)S(1)}, u32[]{:S(2)}, u32[]{:S(2)}) async-start(bf16[32,16,512]{2,1,0:T(8,128)(2,1)} %shard_map.95), calls=%async_computation | async-start | bytes 1048576 | tf_op jit(solution)/shard_map/all_to_all | solution.py:403
  83.7 21.5 %collective-permute-start.8 = (bf16[2,2,128,512]{3,2,1,0:T(8,128)(2,1)}, bf16[2,2,128,512]{3,2,1,0:T(8,128)(2,1)S(1)}, u32[]{:S(2)}, u32[]{:S(2)}) collective-permute-start(bf16[2,2,128,512]{3,2,1,0:T(8,128)(2,1)} %get-tuple-element.32), channel_id=1, source_target_pairs={{0,48},{48,0},{96,144},{144,96},{192,240},{240,192},{288,336},{336... | collective-permute-start | bytes 1572872 | tf_op jit(solution)/shard_map/ppermute | solution.py:18
  86.8 18.4 %collective-permute-start.9 = (bf16[2,2,128,512]{3,2,1,0:T(8,128)(2,1)}, bf16[2,2,128,512]{3,2,1,0:T(8,128)(2,1)S(1)}, u32[]{:S(2)}, u32[]{:S(2)}) collective-permute-start(bf16[2,2,128,512]{3,2,1,0:T(8,128)(2,1)} %get-tuple-element.33), channel_id=1, source_target_pairs={{48,96},{96,48},{144,192},{192,144},{240,288},{288,240},{336,384},... | collective-permute-start | bytes 1572872 | tf_op jit(solution)/shard_map/ppermute | solution.py:18
  95.6 22.8 %all-to-all-start.1 = ((bf16[12,16,512]{2,1,0:T(8,128)(2,1)}), bf16[12,16,512]{2,1,0:T(8,128)(2,1)S(1)}, u32[]{:S(2)}, u32[]{:S(2)}) async-start(bf16[12,16,512]{2,1,0:T(8,128)(2,1)} %shard_map.97), calls=%async_computation.1 | async-start | bytes 393216 | tf_op jit(solution)/shard_map/all_to_all | solution.py:406
  108.0 18.6 %collective-permute-start.10 = (bf16[2,128,512]{2,1,0:T(8,128)(2,1)S(1)}, bf16[2,128,512]{2,1,0:T(8,128)(2,1)S(1)}, u32[]{:S(2)}, u32[]{:S(2)}) collective-permute-start(bf16[2,128,512]{2,1,0:T(8,128)(2,1)S(1)} %get-tuple-element.35), channel_id=1, source_target_pairs={{0,40},{8,16},{16,8},{24,32},{32,24},{40,0},{1,41},{9,17},{17,9},{... | collective-permute-start | bytes 786440 | tf_op jit(solution)/shard_map/ppermute | solution.py:18
  119.1 11.5 %all-to-all-start.2 = ((bf16[8,16,512]{2,1,0:T(8,128)(2,1)}), bf16[8,16,512]{2,1,0:T(8,128)(2,1)S(1)}, u32[]{:S(2)}, u32[]{:S(2)}) async-start(bf16[8,16,512]{2,1,0:T(8,128)(2,1)} %shard_map.98), calls=%async_computation.2 | async-start | bytes 262144 | tf_op jit(solution)/shard_map/all_to_all | solution.py:409
  (11 other events, 39.6 us)

commit v9 on v8

--- a/solution.py
+++ b/solution.py
@@ -37,6 +37,10 @@
 
 def lat_mates_of(array):
     return exchange(array, "lat", next_door), exchange(array, "lat", other_door)
+
+
+def in_hbm(array):
+    return pltpu.with_memory_space_constraint(array, pltpu.HBM)
 
 
 def dot(left, right, dims):
@@ -183,8 +187,8 @@
         ],
         out_shape=[
             shape((half // LANES, block_len, width), low),
-            shape((parts, PART_ROWS, part_width), wide),
-            shape((steps, 3, 8, 2 * block_len), wide),
+            pltpu.HBM((parts, PART_ROWS, part_width), wide),
+            pltpu.HBM((steps, 3, 8, 2 * block_len), wide),
         ],
         scratch_shapes=[pltpu.VMEM((9 * block_len, 2 * block_len), wide)],
         compiler_params=params,
@@ -206,17 +210,17 @@
         out_shape=[
             shape((block_len, width), low),
             shape((6, block_len, width), low),
-            shape((3, 2, block_len, width), wide),
-            shape((2, 2, block_len, width), low),
-            shape((2, block_len, width), wide),
+            pltpu.HBM((3, 2, block_len, width), wide),
+            pltpu.HBM((2, 2, block_len, width), low),
+            pltpu.HBM((2, block_len, width), wide),
         ],
         compiler_params=pltpu.CompilerParams(
-            dimension_semantics=("arbitrary",), vmem_limit_bytes=60 << 20
+            dimension_semantics=("arbitrary",), vmem_limit_bytes=24 << 20
         ),
         cost_estimate=pl.CostEstimate(
             flops=10 * flops, bytes_accessed=6 << 20, transcendentals=exps
         ),
-    )(live, query, dout, *near, stats)
+    )(live, query, dout, *near, in_hbm(stats))
     return w_given, w_own, backward
 
 
@@ -245,7 +249,7 @@
         out_shape=[
             shape((2, 2, block_len, width), low),
             shape((2, 2, block_len, width), low),
-            shape((2, block_len, width), wide),
+            pltpu.HBM((2, block_len, width), wide),
         ],
         compiler_params=pltpu.CompilerParams(
             dimension_semantics=("arbitrary",), vmem_limit_bytes=8 << 20
@@ -253,7 +257,7 @@
         cost_estimate=pl.CostEstimate(
             flops=2 * given.size, bytes_accessed=5 * given.size, transcendentals=0
         ),
-    )(given, own_column, far_ends)
+    )(given, in_hbm(own_column), in_hbm(far_ends))
 
 
 def lat_sum_kernel(own_sum, far_middle, from_p, from_q, owned, far_sum):
@@ -279,7 +283,7 @@
             dimension_semantics=("arbitrary",), vmem_limit_bytes=8 << 20
         ),
         cost_estimate=pl.CostEstimate(flops=1_000_000_000, bytes_accessed=4 << 20, transcendentals=0),
-    )(own_sum, far_middle, from_p, from_q)
+    )(in_hbm(own_sum), in_hbm(far_middle), from_p, from_q)
 
 
 def weight_sum_kernel(given, w_own, w_parts):
@@ -309,7 +313,7 @@
         cost_estimate=pl.CostEstimate(
             flops=w_own.size, bytes_accessed=8 * w_own.size, transcendentals=0
         ),
-    )(given, w_own)
+    )(given, in_hbm(w_own))
 
 
 def sum_and_copy(array, copies, dtype):

time: 133 us -> 131 us (0.985)
  local copies, waits for them, and re-layouts: 8.64 us -> 1.86 us
  Pallas kernels: 20.9 us -> 24.6 us
  waiting for transfers between devices: 19.3 us -> 21.1 us
    unnamed x42 -> x10, local copies, waits for them, and re-layouts: 6.82 us -> 0.03 us
    all_to_all x1, waiting for transfers between devices: 3.86 us -> 1.57 us  [shards(): lax.all_to_all(w_part, ('lat', 'lon'), 0, 0, axis_index_groups=rows)]
    ppermute x11, waiting for transfers between devices: 7.32 us -> 9.45 us  [exchange(): lax.ppermute(array, axis, [(i, j) for i, j in pairs if 0 <= j < lax.axis_...]
    pallas_call x1, Pallas kernels: 1.5 us -> 3.35 us  [weight_sum(): pl.pallas_call(weight_sum_kernel, grid=(steps,), in_specs=[pl.BlockSpec((...]
    pallas_call x1, Pallas kernels: 0.66 us -> 2.28 us  [lat_sum(): pl.pallas_call(lat_sum_kernel, grid=(width // LANES,), in_specs=[two, two...]
    all_to_all x1, waiting for transfers between devices: 7.3 us -> 8.83 us  [shards(): lax.all_to_all(w_parts, ('opt', 'lat'), 0, 0, axis_index_groups=planes)]
  transfers between devices with their start and end apart: 14 -> 14, of which waited for: 6 -> 6; matrix products, arithmetic and copies ran while one was open for 2% -> 2% of each run, Pallas kernels for 10% -> 13%
where the time goes in v9:
time: 131 us; the launch traced here: 130 us
  starting transfers between devices  79.4 us (61%)
  Pallas kernels  24.6 us (19%)
  waiting for transfers between devices  21.1 us (16%)
  local copies, waits for them, and re-layouts  1.86 us (1%)
  other arithmetic  1.56 us (1%)
    ppermute x11, starting transfers between devices, exchange(): lax.ppermute(array, axis, [(i, j) for i, j in pairs if 0 <= j < lax.axis_...  54.2 us
    all_to_all x1, starting transfers between devices, shards(): lax.all_to_all(w_part, ('lat', 'lon'), 0, 0, axis_index_groups=columns)  9.8 us
    ppermute x11, waiting for transfers between devices, exchange(): lax.ppermute(array, axis, [(i, j) for i, j in pairs if 0 <= j < lax.axis_...  9.45 us
    all_to_all x1, starting transfers between devices, shards(): lax.all_to_all(w_parts, ('opt', 'lat'), 0, 0, axis_index_groups=planes)  9.22 us
    all_to_all x1, waiting for transfers between devices, shards(): lax.all_to_all(w_parts, ('opt', 'lat'), 0, 0, axis_index_groups=planes)  8.83 us
    pallas_call x1, Pallas kernels, attention(): pl.pallas_call(forward_kernel, grid=(steps,), in_specs=[scalars, one, one...  6.67 us
    pallas_call x1, Pallas kernels, attention(): pl.pallas_call(backward_kernel, grid=(steps,), in_specs=[scalars, one, on...  6.37 us
    all_to_all x1, starting transfers between devices, shards(): lax.all_to_all(w_part, ('lat', 'lon'), 0, 0, axis_index_groups=rows)  6.19 us
  transfers between devices with their start and end apart: 14, of which 6 were waited for; matrix products, arithmetic and copies ran while one was open for 2% of the time, Pallas kernels for 13%

profile of v9, /device:TPU:1, one launch (start us, length us, event | category | flops | bytes accessed | tf_op | source)
XLA Modules:
  0.0 129.9 jit_solution(13253865236604421765)
XLA Ops:
  0.7 1.1 fusion.7
  2.6 6.4 %collective-permute-start = (bf16[2,128,512]{2,1,0:T(8,128)(2,1)S(1)}, bf16[2,128,512]{2,1,0:T(8,128)(2,1)S(1)}, u32[]{:S(2)}, u32[]{:S(2)}) collective-permute-start(bf16[2,128,512]{2,1,0:T(8,128)(2,1)S(1)} %get-tuple-element.41), channel_id=1, source_target_pairs={{0,48},{48,0},{96,144},{144,96},{192,240},{240,192},{288,336},{336... | collective-permute-start | bytes 786440 | tf_op jit(solution)/shard_map/ppermute | solution.py:18
  9.0 11.8 %collective-permute-start.3 = (bf16[2,128,512]{2,1,0:T(8,128)(2,1)S(1)}, bf16[2,128,512]{2,1,0:T(8,128)(2,1)S(1)}, u32[]{:S(2)}, u32[]{:S(2)}) collective-permute-start(bf16[2,128,512]{2,1,0:T(8,128)(2,1)S(1)} %get-tuple-element.41), channel_id=1, source_target_pairs={{0,40},{8,16},{16,8},{24,32},{32,24},{40,0},{1,41},{9,17},{17,9},{... | collective-permute-start | bytes 786440 | tf_op jit(solution)/shard_map/ppermute | solution.py:18
  20.8 1.1 dynamic-slice_reduce_fusion
  22.0 4.8 %collective-permute-start.2 = (bf16[3,2,128,512]{3,2,1,0:T(8,128)(2,1)S(1)}, bf16[3,2,128,512]{3,2,1,0:T(8,128)(2,1)S(1)}, u32[]{:S(2)}, u32[]{:S(2)}) collective-permute-start(bf16[3,2,128,512]{3,2,1,0:T(8,128)(2,1)S(1)} %pad_maximum_fusion), channel_id=1, source_target_pairs={{0,8},{8,0},{16,24},{24,16},{32,40},{40,32},{1,9},{9,1},{17,25},{2... | collective-permute-start | bytes 2359304 | tf_op jit(solution)/shard_map/ppermute | solution.py:18
  27.1 2.6 %collective-permute-done.3.refs_1_ = bf16[2,128,512]{2,1,0:T(8,128)(2,1)S(1)} collective-permute-done((bf16[2,128,512]{2,1,0:T(8,128)(2,1)S(1)}, bf16[2,128,512]{2,1,0:T(8,128)(2,1)S(1)}, u32[]{:S(2)}, u32[]{:S(2)}) %collective-permute-start.3) | collective-permute-done | bytes 262176 | tf_op jit(solution)/shard_map/ppermute | solution.py:18
  30.4 4.9 %collective-permute-start.4 = (bf16[2,128,512]{2,1,0:T(8,128)(2,1)S(1)}, bf16[2,128,512]{2,1,0:T(8,128)(2,1)S(1)}, u32[]{:S(2)}, u32[]{:S(2)}) collective-permute-start(bf16[2,128,512]{2,1,0:T(8,128)(2,1)S(1)} %collective-permute-done.3.refs_1_), channel_id=1, source_target_pairs={{0,48},{48,0},{96,144},{144,96},{192,240},{240,192},{288,336},{336... | collective-permute-start | bytes 786440 | tf_op jit(solution)/shard_map/ppermute | solution.py:18
  35.8 3.2 %collective-permute-done.4.refs_3_ = bf16[2,128,512]{2,1,0:T(8,128)(2,1)S(1)} collective-permute-done((bf16[2,128,512]{2,1,0:T(8,128)(2,1)S(1)}, bf16[2,128,512]{2,1,0:T(8,128)(2,1)S(1)}, u32[]{:S(2)}, u32[]{:S(2)}) %collective-permute-start.4) | collective-permute-done | bytes 262176 | tf_op jit(solution)/shard_map/ppermute | solution.py:18
  39.0 6.7 %shard_map.93 = (bf16[4,128,512]{2,1,0:T(8,128)(2,1)S(1)}, f32[32,16,512]{2,1,0:T(8,128)}, f32[4,3,8,256]{3,2,1,0:T(8,128)}) custom-call(s32[10]{0:T(128)S(1)} %pad_add_fusion.live, bf16[128,512]{1,0:T(8,128)(2,1)S(1)} %bitcast.28, bf16[128,512]{1,0:T(8,128)(2,1)S(1)} %convolution_convert_fusion.dout, bf16[128,1024]{1,0:T(8,128)(2,1)S(1)} %bitcast.19, ...), custom_call_target="tpu_custom_call" | custom-call | flops 1509949440 | bytes 5242880 | tf_op jit(solution)/shard_map/pallas_call | solution.py:177
  45.7 9.7 %collective-permute-start.6 = (bf16[4,128,512]{2,1,0:T(8,128)(2,1)S(1)}, bf16[4,128,512]{2,1,0:T(8,128)(2,1)S(1)}, u32[]{:S(2)}, u32[]{:S(2)}) collective-permute-start(bf16[4,128,512]{2,1,0:T(8,128)(2,1)S(1)} %get-tuple-element.23), channel_id=1, source_target_pairs={{0,8},{8,0},{16,24},{24,16},{32,40},{40,32},{1,9},{9,1},{17,25},{2... | collective-permute-start | bytes 1572872 | tf_op jit(solution)/shard_map/ppermute | solution.py:18
  55.4 6.4 %shard_map.94 = (bf16[128,512]{1,0:T(8,128)(2,1)}, bf16[6,128,512]{2,1,0:T(8,128)(2,1)S(1)}, f32[3,2,128,512]{3,2,1,0:T(8,128)}, bf16[2,2,128,512]{3,2,1,0:T(8,128)(2,1)}, f32[2,128,512]{2,1,0:T(8,128)}) custom-call(s32[10]{0:T(128)S(1)} %pad_add_fusion.live, bf16[128,512]{1,0:T(8,128)(2,1)S(1)} %bitcast.29, ...), custom_call_target="tpu_custom_call" | custom-call | flops 3019898880 | bytes 6291456 | tf_op jit(solution)/shard_map/pallas_call | solution.py:199
  61.7 1.9 %collective-permute-start.7 = (bf16[6,128,512]{2,1,0:T(8,128)(2,1)S(1)}, bf16[6,128,512]{2,1,0:T(8,128)(2,1)S(1)}, u32[]{:S(2)}, u32[]{:S(2)}) collective-permute-start(bf16[6,128,512]{2,1,0:T(8,128)(2,1)S(1)} %get-tuple-element.25), channel_id=1, source_target_pairs={{0,8},{8,0},{16,24},{24,16},{32,40},{40,32},{1,9},{9,1},{17,25},{2... | collective-permute-start | bytes 2359304 | tf_op jit(solution)/shard_map/ppermute | solution.py:18
  63.7 3.4 %shard_map.95 = bf16[32,16,512]{2,1,0:T(8,128)(2,1)} custom-call(bf16[4,128,512]{2,1,0:T(8,128)(2,1)S(1)} %collective-permute-done.6.given, f32[32,16,512]{2,1,0:T(8,128)} %get-tuple-element.24.w_own), custom_call_target="tpu_custom_call" | custom-call | flops 262144 | bytes 2097152 | tf_op jit(solution)/shard_map/pallas_call | solution.py:304
  67.0 9.2 %all-to-all-start = ((bf16[32,16,512]{2,1,0:T(8,128)(2,1)}), bf16[32,16,512]{2,1,0:T(8,128)(2,1)S(1)}, u32[]{:S(2)}, u32[]{:S(2)}) async-start(bf16[32,16,512]{2,1,0:T(8,128)(2,1)} %shard_map.95), calls=%async_computation | async-start | bytes 1048576 | tf_op jit(solution)/shard_map/all_to_all | solution.py:407
  76.2 3.8 %shard_map.96 = (bf16[2,2,128,512]{3,2,1,0:T(8,128)(2,1)}, bf16[2,2,128,512]{3,2,1,0:T(8,128)(2,1)S(1)}, f32[2,128,512]{2,1,0:T(8,128)}) custom-call(bf16[6,128,512]{2,1,0:T(8,128)(2,1)S(1)} %collective-permute-done.7.given, f32[3,2,128,512]{3,2,1,0:T(8,128)} %get-tuple-element.26.own_column, bf16[2,2,128,512]{3,2,1,0:T(8,128)(2,1)} %get-tuple-element.27.far_ends), custom_call_target="tpu_custom_call" | custom-call | flops 786432 | bytes 1966080 | tf_op jit(solution)/shard_map/pallas_call | solution.py:244
  80.0 3.1 %collective-permute-start.8 = (bf16[2,2,128,512]{3,2,1,0:T(8,128)(2,1)}, bf16[2,2,128,512]{3,2,1,0:T(8,128)(2,1)S(1)}, u32[]{:S(2)}, u32[]{:S(2)}) collective-permute-start(bf16[2,2,128,512]{3,2,1,0:T(8,128)(2,1)} %get-tuple-element.32), channel_id=1, source_target_pairs={{0,48},{48,0},{96,144},{144,96},{192,240},{240,192},{288,336},{336... | collective-permute-start | bytes 1572872 | tf_op jit(solution)/shard_map/ppermute | solution.py:18
  83.8 8.8 %all-to-all-done.terms = bf16[32,16,512]{2,1,0:T(8,128)(2,1)S(1)} async-done(((bf16[32,16,512]{2,1,0:T(8,128)(2,1)}), bf16[32,16,512]{2,1,0:T(8,128)(2,1)S(1)}, u32[]{:S(2)}, u32[]{:S(2)}) %all-to-all-start) | async-done | bytes 524320 | tf_op jit(solution)/shard_map/all_to_all | solution.py:407
  93.4 9.8 %all-to-all-start.1 = ((bf16[12,16,512]{2,1,0:T(8,128)(2,1)}), bf16[12,16,512]{2,1,0:T(8,128)(2,1)S(1)}, u32[]{:S(2)}, u32[]{:S(2)}) async-start(bf16[12,16,512]{2,1,0:T(8,128)(2,1)} %shard_map.97), calls=%async_computation.1 | async-start | bytes 393216 | tf_op jit(solution)/shard_map/all_to_all | solution.py:410
  103.3 2.3 %shard_map.99 = (f32[2,128,512]{2,1,0:T(8,128)S(1)}, bf16[2,128,512]{2,1,0:T(8,128)(2,1)S(1)}) custom-call(f32[2,128,512]{2,1,0:T(8,128)} %get-tuple-element.30.own_sum, f32[2,128,512]{2,1,0:T(8,128)} %get-tuple-element.31.far_middle, bf16[2,2,128,512]{3,2,1,0:T(8,128)(2,1)S(1)} %collective-permute-done.8.from_p, ...), custom_call_target="tpu_custom_call" | custom-call | flops 1000000000 | bytes 4194304 | tf_op jit(solution)/shard_map/pallas_call | solution.py:276
  105.5 9.5 %collective-permute-start.10 = (bf16[2,128,512]{2,1,0:T(8,128)(2,1)S(1)}, bf16[2,128,512]{2,1,0:T(8,128)(2,1)S(1)}, u32[]{:S(2)}, u32[]{:S(2)}) collective-permute-start(bf16[2,128,512]{2,1,0:T(8,128)(2,1)S(1)} %get-tuple-element.35), channel_id=1, source_target_pairs={{0,40},{8,16},{16,8},{24,32},{32,24},{40,0},{1,41},{9,17},{17,9},{... | collective-permute-start | bytes 786440 | tf_op jit(solution)/shard_map/ppermute | solution.py:18
  115.0 1.3 all-to-all-done.1.terms
  117.0 6.2 %all-to-all-start.2 = ((bf16[8,16,512]{2,1,0:T(8,128)(2,1)}), bf16[8,16,512]{2,1,0:T(8,128)(2,1)S(1)}, u32[]{:S(2)}, u32[]{:S(2)}) async-start(bf16[8,16,512]{2,1,0:T(8,128)(2,1)} %shard_map.98), calls=%async_computation.2 | async-start | bytes 262144 | tf_op jit(solution)/shard_map/all_to_all | solution.py:413
  123.2 3.7 %collective-permute-done.10 = bf16[2,128,512]{2,1,0:T(8,128)(2,1)S(1)} collective-permute-done((bf16[2,128,512]{2,1,0:T(8,128)(2,1)S(1)}, bf16[2,128,512]{2,1,0:T(8,128)(2,1)S(1)}, u32[]{:S(2)}, u32[]{:S(2)}) %collective-permute-start.10) | collective-permute-done | bytes 262176 | tf_op jit(solution)/shard_map/ppermute | solution.py:18
  126.9 1.6 %all-to-all-done.2.pieces = bf16[8,16,512]{2,1,0:T(8,128)(2,1)S(1)} async-done(((bf16[8,16,512]{2,1,0:T(8,128)(2,1)}), bf16[8,16,512]{2,1,0:T(8,128)(2,1)S(1)}, u32[]{:S(2)}, u32[]{:S(2)}) %all-to-all-start.2) | async-done | bytes 131104 | tf_op jit(solution)/shard_map/all_to_all | solution.py:413
  (32 shorter events, 6.0 us)
Async XLA Ops:
  0.6 34.7 %copy-start = (bf16[512,1024]{1,0:T(8,128)(2,1)S(1)}, bf16[512,1024]{1,0:T(8,128)(2,1)}, u32[]{:S(2)}) copy-start(bf16[512,1024]{1,0:T(8,128)(2,1)} %param.10) | copy-start | bytes 3145732
  0.6 34.7 %copy-start.1 = (bf16[1,1,1,128,1024]{4,3,2,1,0:T(8,128)(2,1)S(1)}, bf16[1,1,1,128,1024]{4,3,2,1,0:T(8,128)(2,1)}, u32[]{:S(2)}) copy-start(bf16[1,1,1,128,1024]{4,3,2,1,0:T(8,128)(2,1)} %param.9) | copy-start | bytes 786436
  1.8 37.2 %copy-start.2 = (bf16[1,1,1,128,512]{4,3,2,1,0:T(8,128)(2,1)S(1)}, bf16[1,1,1,128,512]{4,3,2,1,0:T(8,128)(2,1)}, u32[]{:S(2)}) copy-start(bf16[1,1,1,128,512]{4,3,2,1,0:T(8,128)(2,1)} %param.7) | copy-start | bytes 393220
  1.8 37.2 %copy-start.3 = (bf16[1,1,1,128,512]{4,3,2,1,0:T(8,128)(2,1)S(1)}, bf16[1,1,1,128,512]{4,3,2,1,0:T(8,128)(2,1)}, u32[]{:S(2)}) copy-start(bf16[1,1,1,128,512]{4,3,2,1,0:T(8,128)(2,1)} %param.8) | copy-start | bytes 393220
  1.8 37.2 %copy-start.4 = (bf16[1,1,1,128,512]{4,3,2,1,0:T(8,128)(2,1)S(1)}, bf16[1,1,1,128,512]{4,3,2,1,0:T(8,128)(2,1)}, u32[]{:S(2)}) copy-start(bf16[1,1,1,128,512]{4,3,2,1,0:T(8,128)(2,1)} %param.6) | copy-start | bytes 393220
  1.8 20.1 %collective-permute-start.1 = (bf16[2,128,512]{2,1,0:T(8,128)(2,1)S(1)}, bf16[2,128,512]{2,1,0:T(8,128)(2,1)S(1)}, u32[]{:S(2)}, u32[]{:S(2)}) collective-permute-start(bf16[2,128,512]{2,1,0:T(8,128)(2,1)S(1)} %get-tuple-element.41), channel_id=1, source_target_pairs={{48,96},{96,48},{144,192},{192,144},{240,288},{288,240},{336,384},... | collective-permute-start | bytes 786440 | tf_op jit(solution)/shard_map/ppermute | solution.py:18
  2.6 19.3 %collective-permute-start = (bf16[2,128,512]{2,1,0:T(8,128)(2,1)S(1)}, bf16[2,128,512]{2,1,0:T(8,128)(2,1)S(1)}, u32[]{:S(2)}, u32[]{:S(2)}) collective-permute-start(bf16[2,128,512]{2,1,0:T(8,128)(2,1)S(1)} %get-tuple-element.41), channel_id=1, source_target_pairs={{0,48},{48,0},{96,144},{144,96},{192,240},{240,192},{288,336},{336... | collective-permute-start | bytes 786440 | tf_op jit(solution)/shard_map/ppermute | solution.py:18
  9.0 20.7 %collective-permute-start.3 = (bf16[2,128,512]{2,1,0:T(8,128)(2,1)S(1)}, bf16[2,128,512]{2,1,0:T(8,128)(2,1)S(1)}, u32[]{:S(2)}, u32[]{:S(2)}) collective-permute-start(bf16[2,128,512]{2,1,0:T(8,128)(2,1)S(1)} %get-tuple-element.41), channel_id=1, source_target_pairs={{0,40},{8,16},{16,8},{24,32},{32,24},{40,0},{1,41},{9,17},{17,9},{... | collective-permute-start | bytes 786440 | tf_op jit(solution)/shard_map/ppermute | solution.py:18
  22.0 17.0 %collective-permute-start.2 = (bf16[3,2,128,512]{3,2,1,0:T(8,128)(2,1)S(1)}, bf16[3,2,128,512]{3,2,1,0:T(8,128)(2,1)S(1)}, u32[]{:S(2)}, u32[]{:S(2)}) collective-permute-start(bf16[3,2,128,512]{3,2,1,0:T(8,128)(2,1)S(1)} %pad_maximum_fusion), channel_id=1, source_target_pairs={{0,8},{8,0},{16,24},{24,16},{32,40},{40,32},{1,9},{9,1},{17,25},{2... | collective-permute-start | bytes 2359304 | tf_op jit(solution)/shard_map/ppermute | solution.py:18
  29.7 6.1 %collective-permute-start.5 = (bf16[2,128,512]{2,1,0:T(8,128)(2,1)S(1)}, bf16[2,128,512]{2,1,0:T(8,128)(2,1)S(1)}, u32[]{:S(2)}, u32[]{:S(2)}) collective-permute-start(bf16[2,128,512]{2,1,0:T(8,128)(2,1)S(1)} %collective-permute-done.3.refs_1_), channel_id=1, source_target_pairs={{48,96},{96,48},{144,192},{192,144},{240,288},{288,240},{336,384},... | collective-permute-start | bytes 786440 | tf_op jit(solution)/shard_map/ppermute | solution.py:18
  30.4 8.6 %collective-permute-start.4 = (bf16[2,128,512]{2,1,0:T(8,128)(2,1)S(1)}, bf16[2,128,512]{2,1,0:T(8,128)(2,1)S(1)}, u32[]{:S(2)}, u32[]{:S(2)}) collective-permute-start(bf16[2,128,512]{2,1,0:T(8,128)(2,1)S(1)} %collective-permute-done.3.refs_1_), channel_id=1, source_target_pairs={{0,48},{48,0},{96,144},{144,96},{192,240},{240,192},{288,336},{336... | collective-permute-start | bytes 786440 | tf_op jit(solution)/shard_map/ppermute | solution.py:18
  45.7 18.0 %collective-permute-start.6 = (bf16[4,128,512]{2,1,0:T(8,128)(2,1)S(1)}, bf16[4,128,512]{2,1,0:T(8,128)(2,1)S(1)}, u32[]{:S(2)}, u32[]{:S(2)}) collective-permute-start(bf16[4,128,512]{2,1,0:T(8,128)(2,1)S(1)} %get-tuple-element.23), channel_id=1, source_target_pairs={{0,8},{8,0},{16,24},{24,16},{32,40},{40,32},{1,9},{9,1},{17,25},{2... | collective-permute-start | bytes 1572872 | tf_op jit(solution)/shard_map/ppermute | solution.py:18
  61.7 14.5 %collective-permute-start.7 = (bf16[6,128,512]{2,1,0:T(8,128)(2,1)S(1)}, bf16[6,128,512]{2,1,0:T(8,128)(2,1)S(1)}, u32[]{:S(2)}, u32[]{:S(2)}) collective-permute-start(bf16[6,128,512]{2,1,0:T(8,128)(2,1)S(1)} %get-tuple-element.25), channel_id=1, source_target_pairs={{0,8},{8,0},{16,24},{24,16},{32,40},{40,32},{1,9},{9,1},{17,25},{2... | collective-permute-start | bytes 2359304 | tf_op jit(solution)/shard_map/ppermute | solution.py:18
  67.0 25.7 %all-to-all-start = ((bf16[32,16,512]{2,1,0:T(8,128)(2,1)}), bf16[32,16,512]{2,1,0:T(8,128)(2,1)S(1)}, u32[]{:S(2)}, u32[]{:S(2)}) async-start(bf16[32,16,512]{2,1,0:T(8,128)(2,1)} %shard_map.95), calls=%async_computation | async-start | bytes 1048576 | tf_op jit(solution)/shard_map/all_to_all | solution.py:407
  80.0 23.2 %collective-permute-start.8 = (bf16[2,2,128,512]{3,2,1,0:T(8,128)(2,1)}, bf16[2,2,128,512]{3,2,1,0:T(8,128)(2,1)S(1)}, u32[]{:S(2)}, u32[]{:S(2)}) collective-permute-start(bf16[2,2,128,512]{3,2,1,0:T(8,128)(2,1)} %get-tuple-element.32), channel_id=1, source_target_pairs={{0,48},{48,0},{96,144},{144,96},{192,240},{240,192},{288,336},{336... | collective-permute-start | bytes 1572872 | tf_op jit(solution)/shard_map/ppermute | solution.py:18
  83.1 20.1 %collective-permute-start.9 = (bf16[2,2,128,512]{3,2,1,0:T(8,128)(2,1)S(1)}, bf16[2,2,128,512]{3,2,1,0:T(8,128)(2,1)S(1)}, u32[]{:S(2)}, u32[]{:S(2)}) collective-permute-start(bf16[2,2,128,512]{3,2,1,0:T(8,128)(2,1)S(1)} %get-tuple-element.33), channel_id=1, source_target_pairs={{48,96},{96,48},{144,192},{192,144},{240,288},{288,240},{336,384},... | collective-permute-start | bytes 1572872 | tf_op jit(solution)/shard_map/ppermute | solution.py:18
  93.4 22.9 %all-to-all-start.1 = ((bf16[12,16,512]{2,1,0:T(8,128)(2,1)}), bf16[12,16,512]{2,1,0:T(8,128)(2,1)S(1)}, u32[]{:S(2)}, u32[]{:S(2)}) async-start(bf16[12,16,512]{2,1,0:T(8,128)(2,1)} %shard_map.97), calls=%async_computation.1 | async-start | bytes 393216 | tf_op jit(solution)/shard_map/all_to_all | solution.py:410
  105.5 21.3 %collective-permute-start.10 = (bf16[2,128,512]{2,1,0:T(8,128)(2,1)S(1)}, bf16[2,128,512]{2,1,0:T(8,128)(2,1)S(1)}, u32[]{:S(2)}, u32[]{:S(2)}) collective-permute-start(bf16[2,128,512]{2,1,0:T(8,128)(2,1)S(1)} %get-tuple-element.35), channel_id=1, source_target_pairs={{0,40},{8,16},{16,8},{24,32},{32,24},{40,0},{1,41},{9,17},{17,9},{... | collective-permute-start | bytes 786440 | tf_op jit(solution)/shard_map/ppermute | solution.py:18
  117.0 11.5 %all-to-all-start.2 = ((bf16[8,16,512]{2,1,0:T(8,128)(2,1)}), bf16[8,16,512]{2,1,0:T(8,128)(2,1)S(1)}, u32[]{:S(2)}, u32[]{:S(2)}) async-start(bf16[8,16,512]{2,1,0:T(8,128)(2,1)} %shard_map.98), calls=%async_computation.2 | async-start | bytes 262144 | tf_op jit(solution)/shard_map/all_to_all | solution.py:413

commit v10 on v9

--- a/solution.py
+++ b/solution.py
@@ -237,14 +237,15 @@
 def chip_sum(given, own_column, far_ends):
     block_len, width = given.shape[1:]
     low, wide = given.dtype, jnp.float32
-    two = pl.BlockSpec((2, block_len, LANES), lambda p: (0, 0, p))
-    four = pl.BlockSpec((2, 2, block_len, LANES), lambda p: (0, 0, 0, p))
-    six = pl.BlockSpec((3, 2, block_len, LANES), lambda p: (0, 0, 0, p))
+    rows = block_len // 2
+    two = pl.BlockSpec((2, rows, width), lambda p: (0, p, 0))
+    four = pl.BlockSpec((2, 2, rows, width), lambda p: (0, 0, p, 0))
+    six = pl.BlockSpec((3, 2, rows, width), lambda p: (0, 0, p, 0))
     shape = jax.ShapeDtypeStruct
     return pl.pallas_call(
         chip_sum_kernel,
-        grid=(width // LANES,),
-        in_specs=[pl.BlockSpec((6, block_len, LANES), lambda p: (0, 0, p)), six, four],
+        grid=(2,),
+        in_specs=[pl.BlockSpec((6, rows, width), lambda p: (0, p, 0)), six, four],
         out_specs=[four, four, two],
         out_shape=[
             shape((2, 2, block_len, width), low),
@@ -270,12 +271,13 @@
 
 def lat_sum(own_sum, far_middle, from_p, from_q):
     _, block_len, width = own_sum.shape
-    two = pl.BlockSpec((2, block_len, LANES), lambda p: (0, 0, p))
-    four = pl.BlockSpec((2, 2, block_len, LANES), lambda p: (0, 0, 0, p))
+    rows = block_len // 2
+    two = pl.BlockSpec((2, rows, width), lambda p: (0, p, 0))
+    four = pl.BlockSpec((2, 2, rows, width), lambda p: (0, 0, p, 0))
     shape = jax.ShapeDtypeStruct
     return pl.pallas_call(
         lat_sum_kernel,
-        grid=(width // LANES,),
+        grid=(2,),
         in_specs=[two, two, four, four],
         out_specs=[two, two],
         out_shape=[shape(own_sum.shape, own_sum.dtype), shape(own_sum.shape, from_p.dtype)],
@@ -288,28 +290,25 @@
 
 def weight_sum_kernel(given, w_own, w_parts):
     wide, low = jnp.float32, jnp.bfloat16
-    w_given = [given[at].astype(wide) for at in range(given.shape[0])]
+    count, block_len, width = given.shape
     tiles = w_parts.shape[2] // LANES
-    across = len(w_given) // tiles
+    across = count // tiles
+    per_pair = w_parts.shape[0] // (width // LANES)
     for at in range(w_parts.shape[0]):
-        row, first = at // across * PART_ROWS, at % across * tiles
-        there = [w_given[first + tile][row : row + PART_ROWS] for tile in range(tiles)]
-        w_parts[at] = (w_own[at] + jnp.concatenate(there, axis=1)).astype(low)
+        pair, inside = at // per_pair, at % per_pair
+        row, first = inside // across * PART_ROWS, inside % across * tiles
+        there = [
+            given[first + tile, row : row + PART_ROWS, pair * LANES : (pair + 1) * LANES]
+            for tile in range(tiles)
+        ]
+        w_parts[at] = (w_own[at] + jnp.concatenate(there, axis=1).astype(wide)).astype(low)
 
 
 def weight_sum(given, w_own):
-    count, block_len, width = given.shape
-    steps = width // LANES
-    parts = pl.BlockSpec((w_own.shape[0] // steps,) + w_own.shape[1:], lambda p: (p, 0, 0))
     return pl.pallas_call(
         weight_sum_kernel,
-        grid=(steps,),
-        in_specs=[pl.BlockSpec((count, block_len, LANES), lambda p: (0, 0, p)), parts],
-        out_specs=parts,
         out_shape=jax.ShapeDtypeStruct(w_own.shape, given.dtype),
-        compiler_params=pltpu.CompilerParams(
-            dimension_semantics=("arbitrary",), vmem_limit_bytes=8 << 20
-        ),
+        compiler_params=pltpu.CompilerParams(vmem_limit_bytes=8 << 20),
         cost_estimate=pl.CostEstimate(
             flops=w_own.size, bytes_accessed=8 * w_own.size, transcendentals=0
         ),

time: 131 us -> 131 us (level)
  Pallas kernels: 24.6 us -> 21.1 us
  waiting for transfers between devices: 21.1 us -> 23.4 us
    pallas_call x3, Pallas kernels: 9.4 us -> 5.9 us  [the longest x1 2.45 us: chip_sum(): pl.pallas_call(chip_sum_kernel, grid=(2,), in_specs=[pl.BlockSpec((6, row...]
    all_to_all x1, waiting for transfers between devices: 8.83 us -> 10.1 us  [shards(): lax.all_to_all(w_parts, ('opt', 'lat'), 0, 0, axis_index_groups=planes)]
  transfers between devices with their start and end apart: 14 -> 14, of which waited for: 6 -> 6; matrix products, arithmetic and copies ran while one was open for 2% -> 2% of each run, Pallas kernels for 13% -> 11%
where the time goes in v10:
time: 131 us; the launch traced here: 129 us
  starting transfers between devices  79.4 us (61%)
  waiting for transfers between devices  23.4 us (18%)
  Pallas kernels  21.1 us (16%)
  local copies, waits for them, and re-layouts  1.86 us (1%)
  other arithmetic  1.56 us (1%)
    ppermute x11, starting transfers between devices, exchange(): lax.ppermute(array, axis, [(i, j) for i, j in pairs if 0 <= j < lax.axis_...  54.2 us
    all_to_all x1, waiting for transfers between devices, shards(): lax.all_to_all(w_parts, ('opt', 'lat'), 0, 0, axis_index_groups=planes)  10.1 us
    all_to_all x1, starting transfers between devices, shards(): lax.all_to_all(w_part, ('lat', 'lon'), 0, 0, axis_index_groups=columns)  9.8 us
    all_to_all x1, starting transfers between devices, shards(): lax.all_to_all(w_parts, ('opt', 'lat'), 0, 0, axis_index_groups=planes)  9.22 us
    ppermute x11, waiting for transfers between devices, exchange(): lax.ppermute(array, axis, [(i, j) for i, j in pairs if 0 <= j < lax.axis_...  8.18 us
    pallas_call x1, Pallas kernels, attention(): pl.pallas_call(forward_kernel, grid=(steps,), in_specs=[scalars, one, one...  6.67 us
    pallas_call x1, Pallas kernels, attention(): pl.pallas_call(backward_kernel, grid=(steps,), in_specs=[scalars, one, on...  6.37 us
    all_to_all x1, starting transfers between devices, shards(): lax.all_to_all(w_part, ('lat', 'lon'), 0, 0, axis_index_groups=rows)  6.16 us
  transfers between devices with their start and end apart: 14, of which 6 were waited for; matrix products, arithmetic and copies ran while one was open for 2% of the time, Pallas kernels for 11%

profile of v10, /device:TPU:1, one launch (start us, length us, event | category | flops | bytes accessed | tf_op | source)
XLA Modules:
  0.0 128.7 jit_solution(3651888509605227372)
XLA Ops:
  0.7 1.1 fusion.7
  2.6 6.4 %collective-permute-start = (bf16[2,128,512]{2,1,0:T(8,128)(2,1)S(1)}, bf16[2,128,512]{2,1,0:T(8,128)(2,1)S(1)}, u32[]{:S(2)}, u32[]{:S(2)}) collective-permute-start(bf16[2,128,512]{2,1,0:T(8,128)(2,1)S(1)} %get-tuple-element.41), channel_id=1, source_target_pairs={{0,48},{48,0},{96,144},{144,96},{192,240},{240,192},{288,336},{336... | collective-permute-start | bytes 786440 | tf_op jit(solution)/shard_map/ppermute | solution.py:18
  9.0 11.8 %collective-permute-start.3 = (bf16[2,128,512]{2,1,0:T(8,128)(2,1)S(1)}, bf16[2,128,512]{2,1,0:T(8,128)(2,1)S(1)}, u32[]{:S(2)}, u32[]{:S(2)}) collective-permute-start(bf16[2,128,512]{2,1,0:T(8,128)(2,1)S(1)} %get-tuple-element.41), channel_id=1, source_target_pairs={{0,40},{8,16},{16,8},{24,32},{32,24},{40,0},{1,41},{9,17},{17,9},{... | collective-permute-start | bytes 786440 | tf_op jit(solution)/shard_map/ppermute | solution.py:18
  20.8 1.1 dynamic-slice_reduce_fusion
  22.0 4.8 %collective-permute-start.2 = (bf16[3,2,128,512]{3,2,1,0:T(8,128)(2,1)S(1)}, bf16[3,2,128,512]{3,2,1,0:T(8,128)(2,1)S(1)}, u32[]{:S(2)}, u32[]{:S(2)}) collective-permute-start(bf16[3,2,128,512]{3,2,1,0:T(8,128)(2,1)S(1)} %pad_maximum_fusion), channel_id=1, source_target_pairs={{0,8},{8,0},{16,24},{24,16},{32,40},{40,32},{1,9},{9,1},{17,25},{2... | collective-permute-start | bytes 2359304 | tf_op jit(solution)/shard_map/ppermute | solution.py:18
  27.1 2.6 %collective-permute-done.3.refs_1_ = bf16[2,128,512]{2,1,0:T(8,128)(2,1)S(1)} collective-permute-done((bf16[2,128,512]{2,1,0:T(8,128)(2,1)S(1)}, bf16[2,128,512]{2,1,0:T(8,128)(2,1)S(1)}, u32[]{:S(2)}, u32[]{:S(2)}) %collective-permute-start.3) | collective-permute-done | bytes 262176 | tf_op jit(solution)/shard_map/ppermute | solution.py:18
  30.4 4.9 %collective-permute-start.4 = (bf16[2,128,512]{2,1,0:T(8,128)(2,1)S(1)}, bf16[2,128,512]{2,1,0:T(8,128)(2,1)S(1)}, u32[]{:S(2)}, u32[]{:S(2)}) collective-permute-start(bf16[2,128,512]{2,1,0:T(8,128)(2,1)S(1)} %collective-permute-done.3.refs_1_), channel_id=1, source_target_pairs={{0,48},{48,0},{96,144},{144,96},{192,240},{240,192},{288,336},{336... | collective-permute-start | bytes 786440 | tf_op jit(solution)/shard_map/ppermute | solution.py:18
  35.8 3.2 %collective-permute-done.4.refs_3_ = bf16[2,128,512]{2,1,0:T(8,128)(2,1)S(1)} collective-permute-done((bf16[2,128,512]{2,1,0:T(8,128)(2,1)S(1)}, bf16[2,128,512]{2,1,0:T(8,128)(2,1)S(1)}, u32[]{:S(2)}, u32[]{:S(2)}) %collective-permute-start.4) | collective-permute-done | bytes 262176 | tf_op jit(solution)/shard_map/ppermute | solution.py:18
  39.0 6.7 %shard_map.93 = (bf16[4,128,512]{2,1,0:T(8,128)(2,1)S(1)}, f32[32,16,512]{2,1,0:T(8,128)}, f32[4,3,8,256]{3,2,1,0:T(8,128)}) custom-call(s32[10]{0:T(128)S(1)} %pad_add_fusion.live, bf16[128,512]{1,0:T(8,128)(2,1)S(1)} %bitcast.28, bf16[128,512]{1,0:T(8,128)(2,1)S(1)} %convolution_convert_fusion.dout, bf16[128,1024]{1,0:T(8,128)(2,1)S(1)} %bitcast.19, ...), custom_call_target="tpu_custom_call" | custom-call | flops 1509949440 | bytes 5242880 | tf_op jit(solution)/shard_map/pallas_call | solution.py:177
  45.7 9.7 %collective-permute-start.6 = (bf16[4,128,512]{2,1,0:T(8,128)(2,1)S(1)}, bf16[4,128,512]{2,1,0:T(8,128)(2,1)S(1)}, u32[]{:S(2)}, u32[]{:S(2)}) collective-permute-start(bf16[4,128,512]{2,1,0:T(8,128)(2,1)S(1)} %get-tuple-element.23), channel_id=1, source_target_pairs={{0,8},{8,0},{16,24},{24,16},{32,40},{40,32},{1,9},{9,1},{17,25},{2... | collective-permute-start | bytes 1572872 | tf_op jit(solution)/shard_map/ppermute | solution.py:18
  55.4 6.4 %shard_map.94 = (bf16[128,512]{1,0:T(8,128)(2,1)}, bf16[6,128,512]{2,1,0:T(8,128)(2,1)S(1)}, f32[3,2,128,512]{3,2,1,0:T(8,128)}, bf16[2,2,128,512]{3,2,1,0:T(8,128)(2,1)}, f32[2,128,512]{2,1,0:T(8,128)}) custom-call(s32[10]{0:T(128)S(1)} %pad_add_fusion.live, bf16[128,512]{1,0:T(8,128)(2,1)S(1)} %bitcast.29, ...), custom_call_target="tpu_custom_call" | custom-call | flops 3019898880 | bytes 6291456 | tf_op jit(solution)/shard_map/pallas_call | solution.py:199
  61.7 1.9 %collective-permute-start.7 = (bf16[6,128,512]{2,1,0:T(8,128)(2,1)S(1)}, bf16[6,128,512]{2,1,0:T(8,128)(2,1)S(1)}, u32[]{:S(2)}, u32[]{:S(2)}) collective-permute-start(bf16[6,128,512]{2,1,0:T(8,128)(2,1)S(1)} %get-tuple-element.25), channel_id=1, source_target_pairs={{0,8},{8,0},{16,24},{24,16},{32,40},{40,32},{1,9},{9,1},{17,25},{2... | collective-permute-start | bytes 2359304 | tf_op jit(solution)/shard_map/ppermute | solution.py:18
  63.7 2.1 %shard_map.95 = bf16[32,16,512]{2,1,0:T(8,128)(2,1)} custom-call(bf16[4,128,512]{2,1,0:T(8,128)(2,1)S(1)} %collective-permute-done.6.given, f32[32,16,512]{2,1,0:T(8,128)} %get-tuple-element.24.w_own), custom_call_target="tpu_custom_call" | custom-call | flops 262144 | bytes 2097152 | tf_op jit(solution)/shard_map/pallas_call | solution.py:308
  65.8 9.2 %all-to-all-start = ((bf16[32,16,512]{2,1,0:T(8,128)(2,1)}), bf16[32,16,512]{2,1,0:T(8,128)(2,1)S(1)}, u32[]{:S(2)}, u32[]{:S(2)}) async-start(bf16[32,16,512]{2,1,0:T(8,128)(2,1)} %shard_map.95), calls=%async_computation | async-start | bytes 1048576 | tf_op jit(solution)/shard_map/all_to_all | solution.py:406
  75.0 2.4 %shard_map.96 = (bf16[2,2,128,512]{3,2,1,0:T(8,128)(2,1)}, bf16[2,2,128,512]{3,2,1,0:T(8,128)(2,1)S(1)}, f32[2,128,512]{2,1,0:T(8,128)}) custom-call(bf16[6,128,512]{2,1,0:T(8,128)(2,1)S(1)} %collective-permute-done.7.given, f32[3,2,128,512]{3,2,1,0:T(8,128)} %get-tuple-element.26.own_column, bf16[2,2,128,512]{3,2,1,0:T(8,128)(2,1)} %get-tuple-element.27.far_ends), custom_call_target="tpu_custom_call" | custom-call | flops 786432 | bytes 1966080 | tf_op jit(solution)/shard_map/pallas_call | solution.py:245
  77.5 3.1 %collective-permute-start.8 = (bf16[2,2,128,512]{3,2,1,0:T(8,128)(2,1)}, bf16[2,2,128,512]{3,2,1,0:T(8,128)(2,1)S(1)}, u32[]{:S(2)}, u32[]{:S(2)}) collective-permute-start(bf16[2,2,128,512]{3,2,1,0:T(8,128)(2,1)} %get-tuple-element.32), channel_id=1, source_target_pairs={{0,48},{48,0},{96,144},{144,96},{192,240},{240,192},{288,336},{336... | collective-permute-start | bytes 1572872 | tf_op jit(solution)/shard_map/ppermute | solution.py:18
  81.3 10.1 %all-to-all-done.terms = bf16[32,16,512]{2,1,0:T(8,128)(2,1)S(1)} async-done(((bf16[32,16,512]{2,1,0:T(8,128)(2,1)}), bf16[32,16,512]{2,1,0:T(8,128)(2,1)S(1)}, u32[]{:S(2)}, u32[]{:S(2)}) %all-to-all-start) | async-done | bytes 524320 | tf_op jit(solution)/shard_map/all_to_all | solution.py:406
  92.2 9.8 %all-to-all-start.1 = ((bf16[12,16,512]{2,1,0:T(8,128)(2,1)}), bf16[12,16,512]{2,1,0:T(8,128)(2,1)S(1)}, u32[]{:S(2)}, u32[]{:S(2)}) async-start(bf16[12,16,512]{2,1,0:T(8,128)(2,1)} %shard_map.97), calls=%async_computation.1 | async-start | bytes 393216 | tf_op jit(solution)/shard_map/all_to_all | solution.py:409
  102.0 1.3 %shard_map.99 = (f32[2,128,512]{2,1,0:T(8,128)S(1)}, bf16[2,128,512]{2,1,0:T(8,128)(2,1)S(1)}) custom-call(f32[2,128,512]{2,1,0:T(8,128)} %get-tuple-element.30.own_sum, f32[2,128,512]{2,1,0:T(8,128)} %get-tuple-element.31.far_middle, bf16[2,2,128,512]{3,2,1,0:T(8,128)(2,1)S(1)} %collective-permute-done.8.from_p, ...), custom_call_target="tpu_custom_call" | custom-call | flops 1000000000 | bytes 4194304 | tf_op jit(solution)/shard_map/pallas_call | solution.py:278
  103.4 9.5 %collective-permute-start.10 = (bf16[2,128,512]{2,1,0:T(8,128)(2,1)S(1)}, bf16[2,128,512]{2,1,0:T(8,128)(2,1)S(1)}, u32[]{:S(2)}, u32[]{:S(2)}) collective-permute-start(bf16[2,128,512]{2,1,0:T(8,128)(2,1)S(1)} %get-tuple-element.35), channel_id=1, source_target_pairs={{0,40},{8,16},{16,8},{24,32},{32,24},{40,0},{1,41},{9,17},{17,9},{... | collective-permute-start | bytes 786440 | tf_op jit(solution)/shard_map/ppermute | solution.py:18
  112.9 2.2 %all-to-all-done.1.terms = bf16[12,16,512]{2,1,0:T(8,128)(2,1)S(1)} async-done(((bf16[12,16,512]{2,1,0:T(8,128)(2,1)}), bf16[12,16,512]{2,1,0:T(8,128)(2,1)S(1)}, u32[]{:S(2)}, u32[]{:S(2)}) %all-to-all-start.1) | async-done | bytes 196640 | tf_op jit(solution)/shard_map/all_to_all | solution.py:409
  115.8 6.2 %all-to-all-start.2 = ((bf16[8,16,512]{2,1,0:T(8,128)(2,1)}), bf16[8,16,512]{2,1,0:T(8,128)(2,1)S(1)}, u32[]{:S(2)}, u32[]{:S(2)}) async-start(bf16[8,16,512]{2,1,0:T(8,128)(2,1)} %shard_map.98), calls=%async_computation.2 | async-start | bytes 262144 | tf_op jit(solution)/shard_map/all_to_all | solution.py:412
  121.9 2.4 %collective-permute-done.10 = bf16[2,128,512]{2,1,0:T(8,128)(2,1)S(1)} collective-permute-done((bf16[2,128,512]{2,1,0:T(8,128)(2,1)S(1)}, bf16[2,128,512]{2,1,0:T(8,128)(2,1)S(1)}, u32[]{:S(2)}, u32[]{:S(2)}) %collective-permute-start.10) | collective-permute-done | bytes 262176 | tf_op jit(solution)/shard_map/ppermute | solution.py:18
  124.4 2.8 %all-to-all-done.2.pieces = bf16[8,16,512]{2,1,0:T(8,128)(2,1)S(1)} async-done(((bf16[8,16,512]{2,1,0:T(8,128)(2,1)}), bf16[8,16,512]{2,1,0:T(8,128)(2,1)S(1)}, u32[]{:S(2)}, u32[]{:S(2)}) %all-to-all-start.2) | async-done | bytes 131104 | tf_op jit(solution)/shard_map/all_to_all | solution.py:412
  (32 shorter events, 6.0 us)
Async XLA Ops:
  0.6 34.7 %copy-start = (bf16[512,1024]{1,0:T(8,128)(2,1)S(1)}, bf16[512,1024]{1,0:T(8,128)(2,1)}, u32[]{:S(2)}) copy-start(bf16[512,1024]{1,0:T(8,128)(2,1)} %param.10) | copy-start | bytes 3145732
  0.6 34.7 %copy-start.1 = (bf16[1,1,1,128,1024]{4,3,2,1,0:T(8,128)(2,1)S(1)}, bf16[1,1,1,128,1024]{4,3,2,1,0:T(8,128)(2,1)}, u32[]{:S(2)}) copy-start(bf16[1,1,1,128,1024]{4,3,2,1,0:T(8,128)(2,1)} %param.9) | copy-start | bytes 786436
  1.8 37.2 %copy-start.2 = (bf16[1,1,1,128,512]{4,3,2,1,0:T(8,128)(2,1)S(1)}, bf16[1,1,1,128,512]{4,3,2,1,0:T(8,128)(2,1)}, u32[]{:S(2)}) copy-start(bf16[1,1,1,128,512]{4,3,2,1,0:T(8,128)(2,1)} %param.7) | copy-start | bytes 393220
  1.8 37.2 %copy-start.3 = (bf16[1,1,1,128,512]{4,3,2,1,0:T(8,128)(2,1)S(1)}, bf16[1,1,1,128,512]{4,3,2,1,0:T(8,128)(2,1)}, u32[]{:S(2)}) copy-start(bf16[1,1,1,128,512]{4,3,2,1,0:T(8,128)(2,1)} %param.8) | copy-start | bytes 393220
  1.8 37.2 %copy-start.4 = (bf16[1,1,1,128,512]{4,3,2,1,0:T(8,128)(2,1)S(1)}, bf16[1,1,1,128,512]{4,3,2,1,0:T(8,128)(2,1)}, u32[]{:S(2)}) copy-start(bf16[1,1,1,128,512]{4,3,2,1,0:T(8,128)(2,1)} %param.6) | copy-start | bytes 393220
  1.8 20.1 %collective-permute-start.1 = (bf16[2,128,512]{2,1,0:T(8,128)(2,1)S(1)}, bf16[2,128,512]{2,1,0:T(8,128)(2,1)S(1)}, u32[]{:S(2)}, u32[]{:S(2)}) collective-permute-start(bf16[2,128,512]{2,1,0:T(8,128)(2,1)S(1)} %get-tuple-element.41), channel_id=1, source_target_pairs={{48,96},{96,48},{144,192},{192,144},{240,288},{288,240},{336,384},... | collective-permute-start | bytes 786440 | tf_op jit(solution)/shard_map/ppermute | solution.py:18
  2.6 19.3 %collective-permute-start = (bf16[2,128,512]{2,1,0:T(8,128)(2,1)S(1)}, bf16[2,128,512]{2,1,0:T(8,128)(2,1)S(1)}, u32[]{:S(2)}, u32[]{:S(2)}) collective-permute-start(bf16[2,128,512]{2,1,0:T(8,128)(2,1)S(1)} %get-tuple-element.41), channel_id=1, source_target_pairs={{0,48},{48,0},{96,144},{144,96},{192,240},{240,192},{288,336},{336... | collective-permute-start | bytes 786440 | tf_op jit(solution)/shard_map/ppermute | solution.py:18
  9.0 20.7 %collective-permute-start.3 = (bf16[2,128,512]{2,1,0:T(8,128)(2,1)S(1)}, bf16[2,128,512]{2,1,0:T(8,128)(2,1)S(1)}, u32[]{:S(2)}, u32[]{:S(2)}) collective-permute-start(bf16[2,128,512]{2,1,0:T(8,128)(2,1)S(1)} %get-tuple-element.41), channel_id=1, source_target_pairs={{0,40},{8,16},{16,8},{24,32},{32,24},{40,0},{1,41},{9,17},{17,9},{... | collective-permute-start | bytes 786440 | tf_op jit(solution)/shard_map/ppermute | solution.py:18
  22.0 17.0 %collective-permute-start.2 = (bf16[3,2,128,512]{3,2,1,0:T(8,128)(2,1)S(1)}, bf16[3,2,128,512]{3,2,1,0:T(8,128)(2,1)S(1)}, u32[]{:S(2)}, u32[]{:S(2)}) collective-permute-start(bf16[3,2,128,512]{3,2,1,0:T(8,128)(2,1)S(1)} %pad_maximum_fusion), channel_id=1, source_target_pairs={{0,8},{8,0},{16,24},{24,16},{32,40},{40,32},{1,9},{9,1},{17,25},{2... | collective-permute-start | bytes 2359304 | tf_op jit(solution)/shard_map/ppermute | solution.py:18
  29.7 6.1 %collective-permute-start.5 = (bf16[2,128,512]{2,1,0:T(8,128)(2,1)S(1)}, bf16[2,128,512]{2,1,0:T(8,128)(2,1)S(1)}, u32[]{:S(2)}, u32[]{:S(2)}) collective-permute-start(bf16[2,128,512]{2,1,0:T(8,128)(2,1)S(1)} %collective-permute-done.3.refs_1_), channel_id=1, source_target_pairs={{48,96},{96,48},{144,192},{192,144},{240,288},{288,240},{336,384},... | collective-permute-start | bytes 786440 | tf_op jit(solution)/shard_map/ppermute | solution.py:18
  30.4 8.6 %collective-permute-start.4 = (bf16[2,128,512]{2,1,0:T(8,128)(2,1)S(1)}, bf16[2,128,512]{2,1,0:T(8,128)(2,1)S(1)}, u32[]{:S(2)}, u32[]{:S(2)}) collective-permute-start(bf16[2,128,512]{2,1,0:T(8,128)(2,1)S(1)} %collective-permute-done.3.refs_1_), channel_id=1, source_target_pairs={{0,48},{48,0},{96,144},{144,96},{192,240},{240,192},{288,336},{336... | collective-permute-start | bytes 786440 | tf_op jit(solution)/shard_map/ppermute | solution.py:18
  45.7 18.0 %collective-permute-start.6 = (bf16[4,128,512]{2,1,0:T(8,128)(2,1)S(1)}, bf16[4,128,512]{2,1,0:T(8,128)(2,1)S(1)}, u32[]{:S(2)}, u32[]{:S(2)}) collective-permute-start(bf16[4,128,512]{2,1,0:T(8,128)(2,1)S(1)} %get-tuple-element.23), channel_id=1, source_target_pairs={{0,8},{8,0},{16,24},{24,16},{32,40},{40,32},{1,9},{9,1},{17,25},{2... | collective-permute-start | bytes 1572872 | tf_op jit(solution)/shard_map/ppermute | solution.py:18
  61.7 13.3 %collective-permute-start.7 = (bf16[6,128,512]{2,1,0:T(8,128)(2,1)S(1)}, bf16[6,128,512]{2,1,0:T(8,128)(2,1)S(1)}, u32[]{:S(2)}, u32[]{:S(2)}) collective-permute-start(bf16[6,128,512]{2,1,0:T(8,128)(2,1)S(1)} %get-tuple-element.25), channel_id=1, source_target_pairs={{0,8},{8,0},{16,24},{24,16},{32,40},{40,32},{1,9},{9,1},{17,25},{2... | collective-permute-start | bytes 2359304 | tf_op jit(solution)/shard_map/ppermute | solution.py:18
  65.8 25.7 %all-to-all-start = ((bf16[32,16,512]{2,1,0:T(8,128)(2,1)}), bf16[32,16,512]{2,1,0:T(8,128)(2,1)S(1)}, u32[]{:S(2)}, u32[]{:S(2)}) async-start(bf16[32,16,512]{2,1,0:T(8,128)(2,1)} %shard_map.95), calls=%async_computation | async-start | bytes 1048576 | tf_op jit(solution)/shard_map/all_to_all | solution.py:406
  77.5 24.6 %collective-permute-start.8 = (bf16[2,2,128,512]{3,2,1,0:T(8,128)(2,1)}, bf16[2,2,128,512]{3,2,1,0:T(8,128)(2,1)S(1)}, u32[]{:S(2)}, u32[]{:S(2)}) collective-permute-start(bf16[2,2,128,512]{3,2,1,0:T(8,128)(2,1)} %get-tuple-element.32), channel_id=1, source_target_pairs={{0,48},{48,0},{96,144},{144,96},{192,240},{240,192},{288,336},{336... | collective-permute-start | bytes 1572872 | tf_op jit(solution)/shard_map/ppermute | solution.py:18
  80.6 21.4 %collective-permute-start.9 = (bf16[2,2,128,512]{3,2,1,0:T(8,128)(2,1)S(1)}, bf16[2,2,128,512]{3,2,1,0:T(8,128)(2,1)S(1)}, u32[]{:S(2)}, u32[]{:S(2)}) collective-permute-start(bf16[2,2,128,512]{3,2,1,0:T(8,128)(2,1)S(1)} %get-tuple-element.33), channel_id=1, source_target_pairs={{48,96},{96,48},{144,192},{192,144},{240,288},{288,240},{336,384},... | collective-permute-start | bytes 1572872 | tf_op jit(solution)/shard_map/ppermute | solution.py:18
  92.2 22.9 %all-to-all-start.1 = ((bf16[12,16,512]{2,1,0:T(8,128)(2,1)}), bf16[12,16,512]{2,1,0:T(8,128)(2,1)S(1)}, u32[]{:S(2)}, u32[]{:S(2)}) async-start(bf16[12,16,512]{2,1,0:T(8,128)(2,1)} %shard_map.97), calls=%async_computation.1 | async-start | bytes 393216 | tf_op jit(solution)/shard_map/all_to_all | solution.py:409
  103.4 21.0 %collective-permute-start.10 = (bf16[2,128,512]{2,1,0:T(8,128)(2,1)S(1)}, bf16[2,128,512]{2,1,0:T(8,128)(2,1)S(1)}, u32[]{:S(2)}, u32[]{:S(2)}) collective-permute-start(bf16[2,128,512]{2,1,0:T(8,128)(2,1)S(1)} %get-tuple-element.35), channel_id=1, source_target_pairs={{0,40},{8,16},{16,8},{24,32},{32,24},{40,0},{1,41},{9,17},{17,9},{... | collective-permute-start | bytes 786440 | tf_op jit(solution)/shard_map/ppermute | solution.py:18
  115.8 11.5 %all-to-all-start.2 = ((bf16[8,16,512]{2,1,0:T(8,128)(2,1)}), bf16[8,16,512]{2,1,0:T(8,128)(2,1)S(1)}, u32[]{:S(2)}, u32[]{:S(2)}) async-start(bf16[8,16,512]{2,1,0:T(8,128)(2,1)} %shard_map.98), calls=%async_computation.2 | async-start | bytes 262144 | tf_op jit(solution)/shard_map/all_to_all | solution.py:412
